TPU v7x, 512 devices: a whole 4x4x16 slice. The times are simulated.
512 devices in a mesh: firm: 16 (over z), worker: 8 (over y, core), probe: 4 (over x).
Axes of the slice: x: 4, y: 4, z: 16, core: 2. Of those that a mesh axis runs over, the one named last changes fastest.
Arguments:
- tiles: bfloat16 [16384, 128, 128], P(('firm', 'worker')), may hold values from -0.046875 to 0.046875
- tile_rows: int32 [128, 128], P(('firm', 'worker')), may hold values from 0 to 3
- tile_firms: int32 [128, 128], P(('firm', 'worker')), may hold values from 0 to 127
- worker_ids: int32 [128, 512], P(('firm', 'worker')), may hold values from 0 to 127, never falling along the last dimension, each value on 1 to 8 neighbouring positions
- sign_words: int32 [32, 512, 5], P('probe', ('firm', 'worker')), may hold values from 0 to 1073741823
- regular: float32 [16384], P('firm'), may hold values from 0.5 to 4
Outputs:
- solution: float32 [32, 16384], P('probe', 'firm')
- residual: float32 [32, 16384], P('probe', 'firm')
Inputs may be any that keep to these rules, and one draw needn't show every extreme that they name: `worker_ids`: within each row shard the worker ids never fall, and each of the ids 0 to 127 has 1 to 8 rows. `sign_words`: only the bits that the steps read carry signs.
All inputs are finite; a program needn't handle non-finite values.
Results may differ from a plain program's by a relative error of at most 0.0064.
Values may be sent and summed in bfloat16 or wider, within the bound.
No kernel may reach another device: no remote copies, remote signals or barrier semaphores. Data moves between devices by JAX's collectives and lax.ppermute only.
A program may use at most 64 MiB of HBM per device.

v0:
```python
import jax
import jax.numpy as jnp
import numpy as np
from jax import lax
from jax.sharding import PartitionSpec as P

TILE = 128
ITERS = 2
ROWB_DEV = 4
ROWS_DEV = 512
SHARD_WORKERS = 128


largest_value = lax.Precision.HIGHEST


def unpack_signs(words):
    position = np.arange(TILE)
    word_of = jnp.asarray(position // 30, jnp.int32)
    bit_of = jnp.asarray(position % 30, jnp.int32)
    selected_rows = jnp.take(words, word_of, axis=2)
    bit_values = jnp.bitwise_and(jnp.right_shift(selected_rows, bit_of), 1)
    return (2 * bit_values - 1).astype(jnp.float32).reshape(words.shape[0], words.shape[1] * TILE)


def demean(values, worker_row):
    onehot = (worker_row[:, None] == jnp.arange(SHARD_WORKERS)[None, :]).astype(jnp.float32)
    totals = jnp.dot(values, onehot, precision=largest_value)
    counts = jnp.sum(onehot, axis=0)
    return values - jnp.dot(totals / counts, onehot.T, precision=largest_value)


def gram_of(left_part, right_part):
    return jnp.einsum("bpf,bqf->pq", left_part, right_part, precision=largest_value)


def symmetric(matrix):
    return 0.5 * (matrix + matrix.T)


def combine_rows(weights, field):
    return jnp.einsum("pq,bpf->bqf", weights, field, precision=largest_value)


def solve_spd(matrix, target):
    factor = jnp.linalg.cholesky(matrix)
    inner = lax.linalg.triangular_solve(factor, target, left_side=True, lower=True)
    return lax.linalg.triangular_solve(factor, inner, left_side=True, lower=True, transpose_a=True)


def local(tiles, tile_rows, tile_firms, worker_ids, sign_words, regular):
    probe_dev = sign_words.shape[0]
    firm_count = lax.axis_size("firm")
    blocks_dev = regular.shape[0] // TILE
    blocks_all = blocks_dev * firm_count
    row_ids = tile_rows[0]
    firm_ids = tile_firms[0]
    worker_row = worker_ids[0]
    firm_hot = (firm_ids[None, :] == jnp.arange(blocks_all)[:, None]).astype(jnp.float32)
    row_hot = (row_ids[None, :] == jnp.arange(ROWB_DEV)[:, None]).astype(jnp.float32)
    reg_blocks = regular.reshape(blocks_dev, 1, TILE)

    def owner_total(block_products):
        owned_part = lax.psum_scatter(
            jnp.einsum("gt,tpf->gpf", firm_hot, block_products, precision=largest_value),
            "firm",
            scatter_dimension=0,
            tiled=True,
        )
        return lax.psum(owned_part, "worker")

    def adjoint(demeaned):
        feature_blocks = demeaned.reshape(probe_dev, ROWB_DEV, TILE)[:, row_ids]
        block_products = jnp.einsum(
            "wqx,qxk->qwk", feature_blocks, tiles, preferred_element_type=jnp.float32
        )
        return owner_total(block_products)

    def spread(local_part):
        return lax.all_gather(local_part, "probe", axis=1, tiled=True)

    def one_sum(matrix):
        return lax.psum(matrix, "firm")

    offset = lax.axis_index("probe") * probe_dev

    def own_rows(full_field):
        return lax.dynamic_slice_in_dim(full_field, offset, probe_dev, 1)

    signs_demeaned = demean(unpack_signs(sign_words), worker_row).astype(jnp.bfloat16)
    right_side = spread(adjoint(signs_demeaned))
    solution = jnp.zeros_like(right_side)
    residual = right_side
    direction = right_side
    current = symmetric(one_sum(gram_of(residual, residual)))
    for turn_index in range(ITERS):
        field = own_rows(direction)
        collected_rows = lax.all_gather(field.astype(jnp.bfloat16), "firm", axis=0, tiled=True)
        selected_rows = collected_rows[firm_ids]
        operator_block_products = jnp.einsum(
            "awl,agl->awg", selected_rows, tiles, preferred_element_type=jnp.float32
        )
        summed = jnp.einsum(
            "bt,tpr->pbr", row_hot, operator_block_products, precision=largest_value
        ).reshape(probe_dev, ROWS_DEV)
        operator_demeaned = demean(summed, worker_row).astype(jnp.bfloat16)
        mapped = spread(adjoint(operator_demeaned) + reg_blocks * field)
        last_turn = turn_index + 1 == ITERS
        curvature = symmetric(one_sum(gram_of(direction, mapped)))
        step_size = solve_spd(curvature, current)
        solution = solution + combine_rows(step_size, direction)
        residual = residual - combine_rows(step_size, mapped)
        if not last_turn:
            following = symmetric(one_sum(gram_of(residual, residual)))
            carry_mix = solve_spd(current, following)
            direction = residual + combine_rows(carry_mix, direction)
            current = following
    solution_rows = jnp.transpose(own_rows(solution), (1, 0, 2)).reshape(
        probe_dev, blocks_dev * TILE
    )
    residual_rows = jnp.transpose(own_rows(residual), (1, 0, 2)).reshape(
        probe_dev, blocks_dev * TILE
    )
    return (solution_rows, residual_rows)


def solution(mesh):
    placed = (
        P(("firm", "worker"), None, None),
        P(("firm", "worker"), None),
        P(("firm", "worker"), None),
        P(("firm", "worker"), None),
        P("probe", ("firm", "worker"), None),
        P("firm"),
    )
    return jax.shard_map(
        local,
        mesh=mesh,
        in_specs=placed,
        out_specs=(P("probe", "firm"), P("probe", "firm")),
        check_vma=False,
    )
```

profile of v0, /device:TPU:2, one launch (start us, length us, event | category | flops | bytes accessed | tf_op | source)
XLA Modules:
  0.0 606.7 jit_solution(15595256011000213017)
XLA Ops:
  7.2 0.8 convert_reduce_fusion
  8.1 0.7 fusion.90
  8.7 0.7 broadcast_bitcast_fusion
  9.4 0.7 pad_clamp_fusion.2
  10.1 0.8 gather_fusion
  10.9 1.0 convolution_divide_fusion.2
  11.9 1.0 fusion.5
  12.9 0.7 gather_fusion.1
  13.6 3.4 fusion.18
  17.0 1.3 fusion.12
  18.3 74.7 %reduce-scatter.4.cloned.1.call-done = f32[8,8,128]{2,0,1:T(8,128)} async-done(((f32[128,8,128]{2,0,1:T(8,128)}), f32[8,8,128]{2,0,1:T(8,128)}) %reduce-scatter.4.cloned.1.call-update) | async-done | bytes 32784 | tf_op jit(solution)/shard_map/reduce_scatter | solution.py:64
  93.0 24.1 %psum.49 = f32[8,8,128]{2,0,1:T(8,128)S(1)} all-reduce(f32[8,8,128]{2,0,1:T(8,128)} %reduce-scatter.4.cloned.1.call-done), channel_id=1, replica_groups=mesh['firm'=16,'worker'=8,'probe'=4] {'worker'}, use_global_device_ids=true, to_apply=%region_2.3 | all-reduce | flops 8192 | bytes 65536 | tf_op jit(solution)/shard_map/psum | solution.py:70
  117.2 12.0 %all_gather.15 = f32[8,32,128]{2,0,1:T(8,128)S(1)} all-gather(f32[8,8,128]{2,0,1:T(8,128)S(1)} %psum.49), channel_id=1, replica_groups=mesh['firm'=16,'worker'=8,'probe'=4] {'probe'}, dimensions={1}, use_global_device_ids=true | all-gather | bytes 163840 | tf_op jit(solution)/shard_map/all_gather | solution.py:80
  129.1 28.7 %all_gather.16 = bf16[128,8,128]{2,0,1:T(8,128)(2,1)S(1)} all-gather(bf16[8,8,128]{2,0,1:T(8,128)(2,1)S(1)} %dynamic-slice_convert_fusion.1), channel_id=1, replica_groups=mesh['firm'=16,'worker'=8,'probe'=4] {'firm'}, dimensions={0}, use_global_device_ids=true | all-gather | bytes 278528 | tf_op jit(solution)/shard_map/all_gather | solution.py:98
  158.0 0.7 gather_fusion.2
  158.7 4.4 fusion.97
  164.1 0.7 gather_fusion.3
  164.8 3.4 fusion.16
  168.2 1.3 fusion.9
  169.8 65.9 %reduce-scatter.6.cloned.1.call-done = f32[8,8,128]{2,0,1:T(8,128)} async-done(((f32[128,8,128]{2,0,1:T(8,128)}), f32[8,8,128]{2,0,1:T(8,128)}) %reduce-scatter.6.cloned.1.call-update) | async-done | bytes 32784 | tf_op jit(solution)/shard_map/reduce_scatter | solution.py:64
  235.7 24.1 %psum.50 = f32[8,8,128]{2,0,1:T(8,128)S(1)} all-reduce(f32[8,8,128]{2,0,1:T(8,128)} %reduce-scatter.6.cloned.1.call-done), channel_id=1, replica_groups=mesh['firm'=16,'worker'=8,'probe'=4] {'worker'}, use_global_device_ids=true, to_apply=%region_4.5 | all-reduce | flops 8192 | bytes 65536 | tf_op jit(solution)/shard_map/psum | solution.py:70
  259.8 12.0 %all_gather.17 = f32[8,32,128]{2,0,1:T(8,128)S(1)} all-gather(f32[8,8,128]{2,0,1:T(8,128)S(1)} %multiply_add_fusion.1), channel_id=1, replica_groups=mesh['firm'=16,'worker'=8,'probe'=4] {'probe'}, dimensions={1}, use_global_device_ids=true | all-gather | bytes 163840 | tf_op jit(solution)/shard_map/all_gather | solution.py:80
  272.1 54.0 %all-reduce = (f32[32,32]{1,0:T(8,128)S(1)}, f32[32,32]{1,0:T(8,128)S(1)}) all-reduce(f32[32,32]{1,0:T(8,128)S(1)} %convolution_bitcast_fusion.6, f32[32,32]{1,0:T(8,128)S(1)} %convolution_bitcast_fusion.7), channel_id=1, replica_groups=mesh['firm'=16,'worker'=8,'probe'=4] {'firm'}, use_global_device_ids=true, to_apply=%region_8.10 | all-reduce | flops 2048 | bytes 16384 | tf_op jit(solution)/shard_map/psum | solution.py:83
  326.3 2.9 cholesky.59
  329.2 0.6 compare_reduce_fusion.2
  329.9 0.7 fusion.51
  330.5 2.4 custom-call.13
  334.1 53.2 %psum.53 = f32[32,32]{1,0:T(8,128)S(1)} all-reduce(f32[32,32]{1,0:T(8,128)S(1)} %convolution_bitcast_fusion.4), channel_id=1, replica_groups=mesh['firm'=16,'worker'=8,'probe'=4] {'firm'}, use_global_device_ids=true, to_apply=%region_9.0 | all-reduce | flops 1024 | bytes 8192 | tf_op jit(solution)/shard_map/psum | solution.py:83
  387.4 2.9 cholesky.70
  390.4 0.6 compare_reduce_fusion.1
  391.0 0.7 fusion.52
  391.7 2.4 custom-call.15
  394.9 29.5 %all_gather.18 = bf16[128,8,128]{2,0,1:T(8,128)(2,1)S(1)} all-gather(bf16[8,8,128]{2,0,1:T(8,128)(2,1)S(1)} %dynamic-slice_convert_fusion), channel_id=1, replica_groups=mesh['firm'=16,'worker'=8,'probe'=4] {'firm'}, dimensions={0}, use_global_device_ids=true | all-gather | bytes 278528 | tf_op jit(solution)/shard_map/all_gather | solution.py:98
  424.7 0.7 gather_fusion.4
  425.3 4.4 fusion.98
  430.7 0.7 gather_fusion.5
  431.4 3.4 fusion.14
  434.8 1.3 fusion.6
  436.4 64.3 %reduce-scatter.8.cloned.1.call-done = f32[8,8,128]{2,0,1:T(8,128)} async-done(((f32[128,8,128]{2,0,1:T(8,128)}), f32[8,8,128]{2,0,1:T(8,128)}) %reduce-scatter.8.cloned.1.call-update) | async-done | bytes 32784 | tf_op jit(solution)/shard_map/reduce_scatter | solution.py:64
  500.7 24.1 %psum.54 = f32[8,8,128]{2,0,1:T(8,128)S(1)} all-reduce(f32[8,8,128]{2,0,1:T(8,128)} %reduce-scatter.8.cloned.1.call-done), channel_id=1, replica_groups=mesh['firm'=16,'worker'=8,'probe'=4] {'worker'}, use_global_device_ids=true, to_apply=%region_11.0 | all-reduce | flops 8192 | bytes 65536 | tf_op jit(solution)/shard_map/psum | solution.py:70
  524.8 12.0 %all_gather.19 = f32[8,32,128]{2,0,1:T(8,128)S(1)} all-gather(f32[8,8,128]{2,0,1:T(8,128)S(1)} %multiply_add_fusion), channel_id=1, replica_groups=mesh['firm'=16,'worker'=8,'probe'=4] {'probe'}, dimensions={1}, use_global_device_ids=true | all-gather | bytes 163840 | tf_op jit(solution)/shard_map/all_gather | solution.py:80
  537.1 53.8 %psum.55 = f32[32,32]{1,0:T(8,128)S(1)} all-reduce(f32[32,32]{1,0:T(8,128)S(1)} %convolution_bitcast_fusion.1), channel_id=1, replica_groups=mesh['firm'=16,'worker'=8,'probe'=4] {'firm'}, use_global_device_ids=true, to_apply=%region_12.0 | all-reduce | flops 1024 | bytes 8192 | tf_op jit(solution)/shard_map/psum | solution.py:83
  591.1 2.9 cholesky.81
  594.0 0.6 compare_reduce_fusion
  594.7 0.7 fusion.53
  595.3 2.4 custom-call.17
  598.9 0.6 copy.193
  599.5 0.6 fusion.47
  (66 shorter events, 7.2 us)
Async XLA Ops:
  7.2 2.9 copy-start
  7.2 9.8 %copy-start.2 = (s32[1,128]{1,0:T(1,128)S(1)}, s32[1,128]{1,0:T(1,128)}, u32[]{:S(2)}) copy-start(s32[1,128]{1,0:T(1,128)} %param.15) | copy-start | bytes 1540
  7.2 85.8 %reduce-scatter.4.cloned.1.call-start = ((), (), s32[]{:S(2)}) async-start(), calls=%async_computation.3 | async-start | bytes 557056 | tf_op jit(solution)/shard_map/reduce_scatter | solution.py:64
  17.0 146.2 %copy-start.3 = (s32[1,128]{1,0:T(1,128)S(1)}, s32[1,128]{1,0:T(1,128)}, u32[]{:S(2)}) copy-start(s32[1,128]{1,0:T(1,128)} %param.14) | copy-start | bytes 1540
  17.0 146.5 %copy-start.4 = (s32[1,512]{1,0:T(1,128)S(1)}, s32[1,512]{1,0:T(1,128)}, u32[]{:S(2)}) copy-start(s32[1,512]{1,0:T(1,128)} %param.16) | copy-start | bytes 6148
  18.2 217.4 %reduce-scatter.6.cloned.1.call-start = ((), (), s32[]{:S(2)}) async-start(), calls=%async_computation.4 | async-start | bytes 557056 | tf_op jit(solution)/shard_map/reduce_scatter | solution.py:64
  163.1 96.7 %copy-start.1 = (f32[1024]{0:T(1024)S(1)}, f32[1024]{0:T(1024)}, u32[]{:S(2)}) copy-start(f32[1024]{0:T(1024)} %param.18) | copy-start | bytes 12292
  169.5 331.2 %reduce-scatter.8.cloned.1.call-start = ((), (), s32[]{:S(2)}) async-start(), calls=%async_computation.5 | async-start | bytes 557056 | tf_op jit(solution)/shard_map/reduce_scatter | solution.py:64
Sparse Core Ops, SparseCore 0:
  18.4 74.6 reduce-scatter.3
  169.6 66.0 reduce-scatter.5
  436.2 64.3 reduce-scatter.7
where the time goes:
time: 607 us
  blocking collectives  328 us (54%)
  waiting for transfers between devices  205 us (34%)
  matrix products  30.4 us (5%)
  other arithmetic  23.1 us (4%)
  between operations  14 us (2%)
  local copies, waits for them, and re-layouts  6.56 us (1%)
    reduce_scatter x3, waiting for transfers between devices, owner_total(): lax.psum_scatter(jnp.einsum('gt,tpf->gpf', firm_hot, block_products, prec...  205 us
    psum x3, blocking collectives, one_sum(): return lax.psum(matrix, 'firm')  161 us
    psum x3, blocking collectives, owner_total(): return lax.psum(owned_part, 'worker')  72.4 us
    all_gather x2, blocking collectives, local(): lax.all_gather(field.astype(jnp.bfloat16), 'firm', axis=0, tiled=True)  58.2 us
    all_gather x3, blocking collectives, spread(): return lax.all_gather(local_part, 'probe', axis=1, tiled=True)  36 us
  transfers between devices with their start and end apart: 3, of which 3 were waited for; matrix products, arithmetic and copies ran while one was open for 0% of the time, Pallas kernels for 0%

commit v1 on v0

v1 whole, which is shorter than its diff:
```python
import jax
import jax.numpy as jnp
import numpy as np
from jax import lax
from jax.sharding import PartitionSpec as P

TILE = 128
ROWB_DEV = 4
ROWS_DEV = 512
SHARD_WORKERS = 128


largest_value = lax.Precision.HIGHEST


def unpack_signs(words):
    position = np.arange(TILE)
    word_of = jnp.asarray(position // 30, jnp.int32)
    bit_of = jnp.asarray(position % 30, jnp.int32)
    selected_rows = jnp.take(words, word_of, axis=2)
    bit_values = jnp.bitwise_and(jnp.right_shift(selected_rows, bit_of), 1)
    return (2 * bit_values - 1).astype(jnp.float32).reshape(words.shape[0], words.shape[1] * TILE)


def demean(values, worker_row):
    onehot = (worker_row[:, None] == jnp.arange(SHARD_WORKERS)[None, :]).astype(jnp.float32)
    totals = jnp.dot(values, onehot, precision=largest_value)
    counts = jnp.sum(onehot, axis=0)
    return values - jnp.dot(totals / counts, onehot.T, precision=largest_value)


def symmetric(matrix):
    return 0.5 * (matrix + matrix.T)


def product(left, right):
    return jnp.dot(left, right, precision=largest_value)


def cross(left, right):
    return lax.dot_general(left, right, (((1,), (1,)), ((), ())), precision=largest_value)


def solve_spd(matrix, target):
    factor = jnp.linalg.cholesky(matrix)
    inner = lax.linalg.triangular_solve(factor, target, left_side=True, lower=True)
    return lax.linalg.triangular_solve(factor, inner, left_side=True, lower=True, transpose_a=True)


def everyone(rows, axis, size):
    copies = jnp.broadcast_to(rows[None], (size,) + rows.shape)
    return lax.all_to_all(copies, axis, 0, 0, tiled=True)


def local(tiles, tile_rows, tile_firms, worker_ids, sign_words, regular):
    probe_dev = sign_words.shape[0]
    firms = lax.axis_size("firm")
    workers = lax.axis_size("worker")
    probes = lax.axis_size("probe")
    blocks = firms * workers
    row_ids = tile_rows[0]
    firm_ids = tile_firms[0]
    worker_row = worker_ids[0]
    places = (firm_ids % workers) * firms + firm_ids // workers
    place_hot = (places[None, :] == jnp.arange(blocks)[:, None]).astype(jnp.float32)
    row_hot = (row_ids[None, :] == jnp.arange(ROWB_DEV)[:, None]).astype(jnp.float32)
    reg_own = lax.dynamic_slice_in_dim(regular, lax.axis_index("worker") * TILE, TILE)[None, :]

    def adjoint(demeaned):
        feature_blocks = demeaned.reshape(probe_dev, ROWB_DEV, TILE)[:, row_ids]
        block_products = jnp.einsum(
            "wqx,qxk->qwk", feature_blocks, tiles, preferred_element_type=jnp.float32
        )
        return jnp.einsum("gt,tpf->gpf", place_hot, block_products, precision=largest_value)

    def forward(collected):
        block_products = jnp.einsum(
            "awl,agl->awg", collected[places], tiles, preferred_element_type=jnp.float32
        )
        summed = jnp.einsum(
            "bt,tpr->pbr", row_hot, block_products, precision=largest_value
        ).reshape(probe_dev, ROWS_DEV)
        return demean(summed, worker_row)

    def owner_total(parts, extra):
        kept = firms * probe_dev
        chunk = parts.reshape(workers, kept, TILE)
        if extra is not None:
            added = extra.shape[0]
            chunk = jnp.concatenate(
                [chunk, jnp.broadcast_to(extra[None], (workers, added, TILE))], axis=1
            )
        got = jnp.sum(lax.all_to_all(chunk, "worker", 0, 0, tiled=True), axis=0)
        chunk = got[:kept].reshape(firms, probe_dev, TILE)
        if extra is not None:
            chunk = jnp.concatenate(
                [chunk, jnp.broadcast_to(got[None, kept:], (firms, added, TILE))], axis=1
            )
        return jnp.sum(lax.all_to_all(chunk, "firm", 0, 0, tiled=True), axis=0)

    def collect(own):
        rounded = own.astype(jnp.bfloat16)
        column = everyone(rounded, "firm", firms)
        return everyone(column, "worker", workers).reshape(blocks, probe_dev, TILE)

    signs_demeaned = demean(unpack_signs(sign_words), worker_row).astype(jnp.bfloat16)
    first = owner_total(adjoint(signs_demeaned), None)

    first_rows = forward(collect(first))
    above = jnp.sum(first_rows * first_rows, axis=1) + jnp.sum(first * first * reg_own, axis=1)
    below = jnp.sum(first * first, axis=1)
    lane = jnp.arange(TILE)[None, :]
    extra = jnp.where(lane < TILE // 2, above[:, None], below[:, None])
    got = owner_total(adjoint(first_rows.astype(jnp.bfloat16)), extra)
    quotient = got[probe_dev:, :1] / got[probe_dev:, TILE // 2 : TILE // 2 + 1]
    second = first - (got[:probe_dev] + reg_own * first) / quotient

    second_rows = forward(collect(second))
    mine = jnp.concatenate([first, second], axis=0)
    mine_rows = jnp.concatenate([first_rows, second_rows], axis=0)
    sent = jnp.concatenate(
        [mine, jnp.transpose(mine_rows.reshape(-1, ROWB_DEV, TILE), (1, 0, 2)).reshape(-1, TILE)],
        axis=0,
    )
    given = everyone(sent, "probe", probes)
    given = given.reshape(probes, 1 + ROWB_DEV, 2, probe_dev, TILE)
    total = probes * probe_dev
    basis = jnp.transpose(given[:, 0], (1, 0, 2, 3)).reshape(2 * total, TILE)
    basis_rows = jnp.transpose(given[:, 1:], (2, 0, 3, 1, 4)).reshape(2 * total, ROWS_DEV)
    grams = cross(mine, basis)
    mapped_grams = cross(mine_rows, basis_rows) + cross(mine * reg_own, basis)
    extra = jnp.concatenate([grams, mapped_grams], axis=1)
    got = owner_total(adjoint(second_rows.astype(jnp.bfloat16)), extra)
    third = got[:probe_dev] + reg_own * second

    given = everyone(jnp.concatenate([third, got[probe_dev:]], axis=0), "probe", probes)
    given = given.reshape(probes, 3, probe_dev, TILE)
    third_all = given[:, 0].reshape(total, TILE)
    tables = jnp.transpose(given[:, 1:], (1, 0, 2, 3)).reshape(2 * total, TILE)
    grams = symmetric(tables[:, : 2 * total])
    mapped_grams = symmetric(tables[:, 2 * total :])
    current = grams[:total, :total]
    curvature = mapped_grams[:total, :total]
    scale = (jnp.diagonal(curvature) / jnp.diagonal(current))[None, :]
    step_first = solve_spd(curvature, current)
    onto_second = step_first.T * scale
    onto_first = jnp.eye(total) - onto_second
    residual_mix = jnp.concatenate([onto_first, onto_second], axis=1)
    following = symmetric(cross(product(residual_mix, grams), residual_mix))
    carry_mix = solve_spd(current, following)
    direction_mix = jnp.concatenate([onto_first + carry_mix.T, onto_second], axis=1)
    curvature = symmetric(cross(product(direction_mix, mapped_grams), direction_mix))
    step_second = solve_spd(curvature, following)
    begin = lax.axis_index("probe") * probe_dev
    first_own = lax.dynamic_slice_in_dim(step_first, begin, probe_dev, 1).T
    second_own = lax.dynamic_slice_in_dim(step_second, begin, probe_dev, 1).T
    residual_own = lax.dynamic_slice_in_dim(residual_mix, begin, probe_dev, 0)
    moved = product(second_own, direction_mix)
    image = moved[:, :total] * scale
    solution_own = product(moved, basis) + product(first_own, basis[:total])
    residual_own = product(
        residual_own + jnp.concatenate([-image, image], axis=1), basis
    ) - product(moved[:, total:], third_all)
    outs = everyone(jnp.concatenate([solution_own, residual_own], axis=0), "worker", workers)
    outs = jnp.transpose(outs.reshape(workers, 2, probe_dev, TILE), (1, 2, 0, 3))
    outs = outs.reshape(2, probe_dev, workers * TILE)
    return (outs[0], outs[1])


def solution(mesh):
    placed = (
        P(("firm", "worker"), None, None),
        P(("firm", "worker"), None),
        P(("firm", "worker"), None),
        P(("firm", "worker"), None),
        P("probe", ("firm", "worker"), None),
        P("firm"),
    )
    return jax.shard_map(
        local,
        mesh=mesh,
        in_specs=placed,
        out_specs=(P("probe", "firm"), P("probe", "firm")),
        check_vma=False,
    )
```

time: 607 us -> 250 us (0.41)
  the two profiles are of different devices: /device:TPU:2 before, /device:TPU:1 now
where the time goes in v1:
time: 250 us; the launch traced here: 249 us
  blocking collectives  132 us (53%)
  matrix products  27.9 us (11%)
  starting transfers between devices  25.8 us (10%)
  waiting for transfers between devices  25.7 us (10%)
  other arithmetic  24.8 us (10%)
  local copies, waits for them, and re-layouts  11.6 us (5%)
    all_to_all x4, blocking collectives, everyone(): return lax.all_to_all(copies, axis, 0, 0, tiled=True)  55.3 us
    all_to_all x3, blocking collectives, owner_total(): got = jnp.sum(lax.all_to_all(chunk, 'worker', 0, 0, tiled=True), axis=0)  47.3 us
    all_to_all x2, blocking collectives, owner_total(): return jnp.sum(lax.all_to_all(chunk, 'firm', 0, 0, tiled=True), axis=0)  29.8 us
    all_to_all x3, waiting for transfers between devices, everyone(): return lax.all_to_all(copies, axis, 0, 0, tiled=True)  14.8 us
    all_to_all x3, starting transfers between devices, everyone(): return lax.all_to_all(copies, axis, 0, 0, tiled=True)  14.4 us
    all_to_all x1, starting transfers between devices, owner_total(): return jnp.sum(lax.all_to_all(chunk, 'firm', 0, 0, tiled=True), axis=0)  11.4 us
    all_to_all x1, waiting for transfers between devices, owner_total(): return jnp.sum(lax.all_to_all(chunk, 'firm', 0, 0, tiled=True), axis=0)  10.8 us
    another operation x9, other arithmetic, solve_spd(): factor = jnp.linalg.cholesky(matrix)  10.8 us
  transfers between devices with their start and end apart: 4, of which 4 were waited for; matrix products, arithmetic and copies ran while one was open for 1% of the time, Pallas kernels for 0%

profile of v1, /device:TPU:1, one launch (start us, length us, event | category | flops | bytes accessed | tf_op | source)
XLA Modules:
  0.0 249.2 jit_solution(3427123884251164472)
XLA Ops:
  0.6 0.8 convert_reduce_fusion
  1.5 0.7 pad_clamp_fusion.2
  2.1 0.8 gather_fusion
  3.0 0.7 broadcast_bitcast_fusion
  3.7 1.0 convolution_divide_fusion.2
  4.6 1.0 fusion.2
  5.6 0.7 fusion.104
  6.3 0.7 fusion.106
  7.0 0.7 gather_fusion.1
  7.7 3.4 %fusion.15 = f32[128,8,128]{2,1,0:T(8,128)S(1)} fusion(bf16[128,128,128]{2,1,0:T(8,128)(2,1)} %param.13, bf16[128,8,128]{2,1,0:T(8,128)(2,1)S(1)} %gather_fusion.1), kind=kOutput, calls=%fused_computation.37 | convolution fusion | flops 33554432 | bytes 4980736 | tf_op jit(solution)/shard_map/wqx,qxk->qwk/dot_general | solution.py:71
  11.9 18.6 %all_to_all.65 = f32[8,128,128]{2,1,0:T(8,128)S(1)} all-to-all(f32[8,128,128]{2,1,0:T(8,128)S(1)} %bitcast.212), channel_id=1, replica_groups=mesh['firm'=16,'worker'=8,'probe'=4] {'worker'}, dimensions={0} | all-to-all | bytes 1048576 | tf_op jit(solution)/shard_map/all_to_all | solution.py:93
  31.1 11.4 %all-to-all-start.1 = ((f32[16,8,128]{2,1,0:T(8,128)}), f32[16,8,128]{2,1,0:T(8,128)S(1)}, u32[]{:S(2)}, u32[]{:S(2)}) async-start(f32[16,8,128]{2,1,0:T(8,128)} %bitcast.11), calls=%async_computation.1 | async-start | bytes 131072 | tf_op jit(solution)/shard_map/all_to_all | solution.py:99
  42.5 0.8 dynamic_slice.12
  43.3 10.8 %all-to-all-done.1 = f32[16,8,128]{2,1,0:T(8,128)S(1)} async-done(((f32[16,8,128]{2,1,0:T(8,128)}), f32[16,8,128]{2,1,0:T(8,128)S(1)}, u32[]{:S(2)}, u32[]{:S(2)}) %all-to-all-start.1) | async-done | bytes 65568 | tf_op jit(solution)/shard_map/all_to_all | solution.py:99
  54.3 14.3 %all_to_all.66 = bf16[16,8,128]{2,1,0:T(8,128)(2,1)S(1)} all-to-all(bf16[16,8,128]{2,1,0:T(8,128)(2,1)S(1)} %broadcast_in_dim.71), channel_id=1, replica_groups=mesh['firm'=16,'worker'=8,'probe'=4] {'firm'}, dimensions={0} | all-to-all | bytes 65536 | tf_op jit(solution)/shard_map/all_to_all | solution.py:52
  68.6 0.7 broadcast_in_dim.72
  69.3 6.9 %all-to-all-start.3 = ((bf16[8,16,8,128]{3,2,1,0:T(8,128)(2,1)}), bf16[8,16,8,128]{3,2,1,0:T(8,128)(2,1)S(1)}, u32[]{:S(2)}, u32[]{:S(2)}) async-start(bf16[8,16,8,128]{3,2,1,0:T(8,128)(2,1)} %broadcast_in_dim.72), calls=%async_computation.3 | async-start | bytes 524288 | tf_op jit(solution)/shard_map/all_to_all | solution.py:52
  76.3 6.5 %all-to-all-done.3 = bf16[8,16,8,128]{3,2,1,0:T(8,128)(2,1)S(1)} async-done(((bf16[8,16,8,128]{3,2,1,0:T(8,128)(2,1)}), bf16[8,16,8,128]{3,2,1,0:T(8,128)(2,1)S(1)}, u32[]{:S(2)}, u32[]{:S(2)}) %all-to-all-start.3) | async-done | bytes 262176 | tf_op jit(solution)/shard_map/all_to_all | solution.py:52
  82.7 0.7 gather_fusion.2
  83.4 4.4 %fusion.124 = f32[128,8,128]{2,1,0:T(8,128)S(1)} fusion(bf16[128,8,128]{2,1,0:T(8,128)(2,1)S(1)} %gather_fusion.2, bf16[128,128,128]{2,1,0:T(8,128)(2,1)} %param.13), kind=kOutput, calls=%fused_computation.210 | convolution fusion | flops 33554432 | bytes 4980736 | tf_op jit(solution)/shard_map/awl,agl->awg/dot_general | solution.py:77
  88.9 0.7 gather_fusion.3
  89.6 3.4 %fusion.13 = f32[128,8,128]{2,1,0:T(8,128)S(1)} fusion(bf16[128,128,128]{2,1,0:T(8,128)(2,1)} %param.13, bf16[128,8,128]{2,1,0:T(8,128)(2,1)S(1)} %gather_fusion.3), kind=kOutput, calls=%fused_computation.35 | convolution fusion | flops 33554432 | bytes 4980736 | tf_op jit(solution)/shard_map/wqx,qxk->qwk/dot_general | solution.py:71
  93.9 13.6 %all_to_all.67 = f32[8,136,128]{2,1,0:T(8,128)S(1)} all-to-all(f32[8,136,128]{2,1,0:T(8,128)S(1)} %pad_maximum_fusion.1), channel_id=1, replica_groups=mesh['firm'=16,'worker'=8,'probe'=4] {'worker'}, dimensions={0} | all-to-all | bytes 1114112 | tf_op jit(solution)/shard_map/all_to_all | solution.py:93
  107.6 14.7 %all_to_all.68 = f32[16,16,128]{2,1,0:T(8,128)S(1)} all-to-all(f32[16,16,128]{2,1,0:T(8,128)S(1)} %pad_maximum_fusion.3), channel_id=1, replica_groups=mesh['firm'=16,'worker'=8,'probe'=4] {'firm'}, dimensions={0} | all-to-all | bytes 262144 | tf_op jit(solution)/shard_map/all_to_all | solution.py:99
  122.5 17.6 %all_to_all.69 = bf16[16,8,128]{2,1,0:T(8,128)(2,1)S(1)} all-to-all(bf16[16,8,128]{2,1,0:T(8,128)(2,1)S(1)} %broadcast_in_dim.78), channel_id=1, replica_groups=mesh['firm'=16,'worker'=8,'probe'=4] {'firm'}, dimensions={0} | all-to-all | bytes 65536 | tf_op jit(solution)/shard_map/all_to_all | solution.py:52
  140.2 11.0 %all_to_all.70 = bf16[8,16,8,128]{3,2,1,0:T(8,128)(2,1)S(1)} all-to-all(bf16[8,16,8,128]{3,2,1,0:T(8,128)(2,1)S(1)} %broadcast_in_dim.79), channel_id=1, replica_groups=mesh['firm'=16,'worker'=8,'probe'=4] {'worker'}, dimensions={0} | all-to-all | bytes 524288 | tf_op jit(solution)/shard_map/all_to_all | solution.py:52
  151.2 0.7 gather_fusion.4
  151.9 4.4 %fusion.125 = f32[128,8,128]{2,1,0:T(8,128)S(1)} fusion(bf16[128,8,128]{2,1,0:T(8,128)(2,1)S(1)} %gather_fusion.4, bf16[128,128,128]{2,1,0:T(8,128)(2,1)} %param.13), kind=kOutput, calls=%fused_computation.211 | convolution fusion | flops 33554432 | bytes 4980736 | tf_op jit(solution)/shard_map/awl,agl->awg/dot_general | solution.py:77
  157.3 0.7 gather_fusion.5
  158.0 3.4 %fusion.11 = f32[128,8,128]{2,1,0:T(8,128)S(1)} fusion(bf16[128,128,128]{2,1,0:T(8,128)(2,1)} %param.13, bf16[128,8,128]{2,1,0:T(8,128)(2,1)S(1)} %gather_fusion.5), kind=kOutput, calls=%fused_computation.33 | convolution fusion | flops 33554432 | bytes 4980736 | tf_op jit(solution)/shard_map/wqx,qxk->qwk/dot_general | solution.py:71
  161.3 0.7 broadcast_in_dim.80
  162.0 4.0 %all-to-all-start.8 = ((f32[4,80,128]{2,1,0:T(8,128)}), f32[4,80,128]{2,1,0:T(8,128)S(1)}, u32[]{:S(2)}, u32[]{:S(2)}) async-start(f32[4,80,128]{2,1,0:T(8,128)} %broadcast_in_dim.80), calls=%async_computation.8 | async-start | bytes 327680 | tf_op jit(solution)/shard_map/all_to_all | solution.py:52
  166.8 4.2 %all-to-all-done.8 = f32[4,80,128]{2,1,0:T(8,128)S(1)} async-done(((f32[4,80,128]{2,1,0:T(8,128)}), f32[4,80,128]{2,1,0:T(8,128)S(1)}, u32[]{:S(2)}, u32[]{:S(2)}) %all-to-all-start.8) | async-done | bytes 163872 | tf_op jit(solution)/shard_map/all_to_all | solution.py:52
  171.8 15.2 %all_to_all.71 = f32[8,144,128]{2,1,0:T(8,128)S(1)} all-to-all(f32[8,144,128]{2,1,0:T(8,128)S(1)} %pad_maximum_fusion), channel_id=1, replica_groups=mesh['firm'=16,'worker'=8,'probe'=4] {'worker'}, dimensions={0} | all-to-all | bytes 1179648 | tf_op jit(solution)/shard_map/all_to_all | solution.py:93
  187.1 15.1 %all_to_all.72 = f32[16,24,128]{2,1,0:T(8,128)S(1)} all-to-all(f32[16,24,128]{2,1,0:T(8,128)S(1)} %pad_maximum_fusion.2), channel_id=1, replica_groups=mesh['firm'=16,'worker'=8,'probe'=4] {'firm'}, dimensions={0} | all-to-all | bytes 393216 | tf_op jit(solution)/shard_map/all_to_all | solution.py:99
  202.9 3.5 %all-to-all-start.11 = ((f32[4,24,128]{2,1,0:T(8,128)}), f32[4,24,128]{2,1,0:T(8,128)S(1)}, u32[]{:S(2)}, u32[]{:S(2)}) async-start(f32[4,24,128]{2,1,0:T(8,128)} %broadcast_in_dim.83), calls=%async_computation.11 | async-start | bytes 98304 | tf_op jit(solution)/shard_map/all_to_all | solution.py:52
  206.3 4.2 %all-to-all-done.11 = f32[4,24,128]{2,1,0:T(8,128)S(1)} async-done(((f32[4,24,128]{2,1,0:T(8,128)}), f32[4,24,128]{2,1,0:T(8,128)S(1)}, u32[]{:S(2)}, u32[]{:S(2)}) %all-to-all-start.11) | async-done | bytes 49184 | tf_op jit(solution)/shard_map/all_to_all | solution.py:52
  210.9 0.7 gather_fusion.6
  211.7 0.7 gather_fusion.7
  212.5 2.9 %cholesky.59 = f32[32,32]{1,0:T(8,128)S(1)} custom-call(f32[32,32]{1,0:T(8,128)S(1)} %fusion.53), custom_call_target="Cholesky" | custom-call | tf_op jit(solution)/shard_map/jit(cholesky)/cholesky | solution.py:45
  216.1 0.7 fusion.33
  216.8 2.4 custom-call.17
  220.2 2.9 %cholesky.70 = f32[32,32]{1,0:T(8,128)S(1)} custom-call(f32[32,32]{1,0:T(8,128)S(1)} %fusion.48), custom_call_target="Cholesky" | custom-call | tf_op jit(solution)/shard_map/jit(cholesky)/cholesky | solution.py:45
  223.8 0.7 fusion.34
  224.5 2.4 custom-call.19
  228.0 2.9 %cholesky.81 = f32[32,32]{1,0:T(8,128)S(1)} custom-call(f32[32,32]{1,0:T(8,128)S(1)} %fusion.42), custom_call_target="Cholesky" | custom-call | tf_op jit(solution)/shard_map/jit(cholesky)/cholesky | solution.py:45
  232.3 2.4 custom-call.21
  236.1 12.5 %all_to_all.73 = f32[8,16,128]{2,1,0:T(8,128)S(1)} all-to-all(f32[8,16,128]{2,1,0:T(8,128)S(1)} %broadcast_in_dim.84), channel_id=1, replica_groups=mesh['firm'=16,'worker'=8,'probe'=4] {'worker'}, dimensions={0} | all-to-all | bytes 131072 | tf_op jit(solution)/shard_map/all_to_all | solution.py:52
  (115 shorter events, 14.5 us)
Async XLA Ops:
  0.6 1.5 copy-start
  7.7 68.5 %copy-start.3 = (s32[1,128]{1,0:T(1,128)S(1)}, s32[1,128]{1,0:T(1,128)}, u32[]{:S(2)}) copy-start(s32[1,128]{1,0:T(1,128)} %param.15) | copy-start | bytes 1540
  11.8 76.0 %copy-start.1 = (s32[1,128]{1,0:T(1,128)S(1)}, s32[1,128]{1,0:T(1,128)}, u32[]{:S(2)}) copy-start(s32[1,128]{1,0:T(1,128)} %param.14) | copy-start | bytes 1540
  11.8 76.3 %copy-start.2 = (s32[1,512]{1,0:T(1,128)S(1)}, s32[1,512]{1,0:T(1,128)}, u32[]{:S(2)}) copy-start(s32[1,512]{1,0:T(1,128)} %param.16) | copy-start | bytes 6148
  31.1 23.0 %all-to-all-start.1 = ((f32[16,8,128]{2,1,0:T(8,128)}), f32[16,8,128]{2,1,0:T(8,128)S(1)}, u32[]{:S(2)}, u32[]{:S(2)}) async-start(f32[16,8,128]{2,1,0:T(8,128)} %bitcast.11), calls=%async_computation.1 | async-start | bytes 131072 | tf_op jit(solution)/shard_map/all_to_all | solution.py:99
  69.3 13.4 %all-to-all-start.3 = ((bf16[8,16,8,128]{3,2,1,0:T(8,128)(2,1)}), bf16[8,16,8,128]{3,2,1,0:T(8,128)(2,1)S(1)}, u32[]{:S(2)}, u32[]{:S(2)}) async-start(bf16[8,16,8,128]{3,2,1,0:T(8,128)(2,1)} %broadcast_in_dim.72), calls=%async_computation.3 | async-start | bytes 524288 | tf_op jit(solution)/shard_map/all_to_all | solution.py:52
  162.0 9.0 %all-to-all-start.8 = ((f32[4,80,128]{2,1,0:T(8,128)}), f32[4,80,128]{2,1,0:T(8,128)S(1)}, u32[]{:S(2)}, u32[]{:S(2)}) async-start(f32[4,80,128]{2,1,0:T(8,128)} %broadcast_in_dim.80), calls=%async_computation.8 | async-start | bytes 327680 | tf_op jit(solution)/shard_map/all_to_all | solution.py:52
  202.9 7.6 %all-to-all-start.11 = ((f32[4,24,128]{2,1,0:T(8,128)}), f32[4,24,128]{2,1,0:T(8,128)S(1)}, u32[]{:S(2)}, u32[]{:S(2)}) async-start(f32[4,24,128]{2,1,0:T(8,128)} %broadcast_in_dim.83), calls=%async_computation.11 | async-start | bytes 98304 | tf_op jit(solution)/shard_map/all_to_all | solution.py:52

commit v2 on v0

v2 whole, which is shorter than its diff:
```python
import jax
import jax.numpy as jnp
from jax import lax
from jax.experimental import pallas as pl
from jax.experimental.pallas import tpu as pltpu
from jax.sharding import PartitionSpec as P

TILE = 128
ROWB_DEV = 4
ROWS_DEV = 512
SHARD_WORKERS = 128
BITS = 30
CHUNKS = 8

largest_value = lax.Precision.HIGHEST
f32 = jnp.float32
bf16 = jnp.bfloat16


def dot(left, right, dims, precision=None):
    return lax.dot_general(
        left, right, ((dims[:1], dims[1:]), ((), ())), precision=precision, preferred_element_type=f32
    )


def exact(left, right, dims):
    return dot(left, right, dims, largest_value)


def three_parts(values):
    high = values.astype(bf16)
    rest = values - high.astype(f32)
    middle = rest.astype(bf16)
    low = (rest - middle.astype(f32)).astype(bf16)
    return high, middle, low


def demean(values, worker_ids):
    probes = values.shape[0]
    workers = lax.broadcasted_iota(jnp.int32, (SHARD_WORKERS, ROWS_DEV), 0)
    onehot = jnp.where(workers == worker_ids, 1.0, 0.0).astype(bf16)
    stacked = jnp.concatenate([*(part.astype(f32) for part in three_parts(values)), jnp.ones_like(values)], axis=0)
    sums = dot(stacked.astype(bf16), onehot, (1, 1))
    totals = (sums[2 * probes : 3 * probes] + sums[probes : 2 * probes]) + sums[:probes]
    means = totals / sums[3 * probes :]
    stacked = jnp.concatenate([part.astype(f32) for part in three_parts(means)], axis=0)
    spread = dot(stacked.astype(bf16), onehot, (1, 0))
    return values - ((spread[2 * probes : 3 * probes] + spread[probes : 2 * probes]) + spread[:probes])


def tile_copy(tiles_hbm, tiles, arrived, chunk):
    size = tiles.shape[0] // CHUNKS
    part = pl.ds(chunk * size, size)
    return pltpu.make_async_copy(tiles_hbm.at[part], tiles.at[part], arrived.at[chunk])


def forward(tile_rows, tile_firms, field, tiles, total, copies, workers, firms):
    size = tiles.shape[0] // CHUNKS
    total[...] = jnp.zeros_like(total)

    def chunk_step(chunk, carry):
        copies(chunk)
        for item in range(size):
            tile = chunk * size + item
            firm = tile_firms[0, tile]
            place = lax.rem(firm, workers) * firms + lax.div(firm, workers)
            image = dot(field[place], tiles[tile], (1, 1))
            row = tile_rows[0, tile]
            total[row] = total[row] + image
        return carry

    lax.fori_loop(0, CHUNKS, chunk_step, 0)


def adjoint(tile_rows, tile_firms, rows, tiles, out, copies, workers, stride):
    size = tiles.shape[0] // CHUNKS
    out[...] = jnp.zeros_like(out)

    def chunk_step(chunk, carry):
        copies(chunk)
        for item in range(size):
            tile = chunk * size + item
            firm = tile_firms[0, tile]
            place = lax.rem(firm, workers) * stride + lax.div(firm, workers)
            image = dot(rows[tile_rows[0, tile]], tiles[tile], (1, 0))
            out[place] = out[place] + image
        return carry

    lax.fori_loop(0, CHUNKS, chunk_step, 0)


def put_rows(rows, values):
    for block in range(ROWB_DEV):
        rows[block] = values[:, block * TILE : (block + 1) * TILE].astype(bf16)


def take_rows(total):
    return jnp.concatenate([total[block] for block in range(ROWB_DEV)], axis=1)


def start_body(workers, firms, tile_rows, tile_firms, words, worker_ids, tiles_hbm, out, tiles, rows, arrived):
    for chunk in range(CHUNKS):
        tile_copy(tiles_hbm, tiles, arrived, chunk).start()
    probes = words.shape[0]
    lanes = lax.broadcasted_iota(jnp.int32, (probes, TILE), 1)
    signs = []
    for block in range(ROWB_DEV):
        block_words = words[:, block, :]
        chosen = jnp.zeros((probes, TILE), jnp.int32)
        bit = lanes
        for word in range(block_words.shape[1]):
            here = (lanes >= word * BITS) & (lanes < (word + 1) * BITS)
            chosen = jnp.where(here, jnp.broadcast_to(block_words[:, word : word + 1], (probes, TILE)), chosen)
            bit = jnp.where(here, lanes - word * BITS, bit)
        signs.append((2 * (lax.shift_right_logical(chosen, bit) & 1) - 1).astype(f32))
    put_rows(rows, demean(jnp.concatenate(signs, axis=1), worker_ids[...]))
    wait = lambda chunk: tile_copy(tiles_hbm, tiles, arrived, chunk).wait()
    adjoint(tile_rows, tile_firms, rows, tiles, out, wait, workers, firms)


def middle_body(
    workers, firms, tile_rows, tile_firms, index, field, first, regular, worker_ids, tiles_hbm,
    out, tiles, rows, total, arrived,
):
    for chunk in range(CHUNKS):
        tile_copy(tiles_hbm, tiles, arrived, chunk).start()
    wait = lambda chunk: tile_copy(tiles_hbm, tiles, arrived, chunk).wait()
    forward(tile_rows, tile_firms, field, tiles, total, wait, workers, firms)
    values = demean(take_rows(total), worker_ids[...])
    put_rows(rows, values)
    adjoint(tile_rows, tile_firms, rows, tiles, out, lambda chunk: None, workers, firms + 1)
    own = first[...]
    squares = own * own
    above = jnp.sum(values * values, axis=1, keepdims=True)
    above = above + jnp.sum(squares * regular[pl.ds(index[0], 1), :], axis=1, keepdims=True)
    below = jnp.sum(squares, axis=1, keepdims=True)
    lanes = lax.broadcasted_iota(jnp.int32, own.shape, 1)
    extra = jnp.where(lanes < TILE // 2, above, below)
    for worker in range(workers):
        out[worker * (firms + 1) + firms] = extra


def rows_body(
    workers, firms, tile_rows, tile_firms, field, first, second, quotient, worker_ids, tiles_hbm,
    out, tiles, total, arrived,
):
    for chunk in range(CHUNKS):
        tile_copy(tiles_hbm, tiles, arrived, chunk).start()
    wait = lambda chunk: tile_copy(tiles_hbm, tiles, arrived, chunk).wait()
    forward(tile_rows, tile_firms, field, tiles, total, wait, workers, firms)
    values = demean(take_rows(total), worker_ids[...])
    for probe in range(out.shape[0]):
        out[probe, 0] = first[...]
        out[probe, 1] = second[...]
        out[probe, 2] = quotient[...]
        for block in range(ROWB_DEV):
            out[probe, 3 + block] = values[:, block * TILE : (block + 1) * TILE]


def last_body(
    workers, firms, tile_rows, tile_firms, index, given, regular, tiles_hbm, out, tiles, rows, arrived
):
    for chunk in range(CHUNKS):
        tile_copy(tiles_hbm, tiles, arrived, chunk).start()
    gather = lambda item: jnp.concatenate([given[probe, item] for probe in range(given.shape[0])], axis=0)
    own = lambda item: given[index[1], item]
    first, second = own(0), own(1)
    first_all, second_all = gather(0), gather(1)
    images = exact(second * regular[pl.ds(index[0], 1), :], second_all, (1, 1))
    for block in range(ROWB_DEV):
        mine = own(3 + block)
        rows[block] = mine.astype(bf16)
        images = images + exact(mine, gather(3 + block), (1, 1))
    extra = jnp.concatenate(
        [
            exact(first, first_all, (1, 1)),
            exact(first, second_all, (1, 1)),
            exact(second, second_all, (1, 1)),
            images,
        ],
        axis=1,
    )
    wait = lambda chunk: tile_copy(tiles_hbm, tiles, arrived, chunk).wait()
    adjoint(tile_rows, tile_firms, rows, tiles, out, wait, workers, firms + 1)
    for worker in range(workers):
        out[worker * (firms + 1) + firms] = extra


def eliminate(table, pivots):
    size, width = table.shape
    lanes = lax.broadcasted_iota(jnp.int32, (size, width), 1)
    lines = lax.broadcasted_iota(jnp.int32, (size, width), 0)
    for step in range(size):
        line = table[step : step + 1, :]
        column = jnp.broadcast_to(table[:, pivots[0] + step : pivots[0] + step + 1], (size, width))
        pivot = jnp.broadcast_to(line[:, pivots[0] + step : pivots[0] + step + 1], (1, width))
        for begin in pivots[1:]:
            at = begin + step
            column = jnp.where(lanes < begin, column, jnp.broadcast_to(table[:, at : at + 1], (size, width)))
            pivot = jnp.where(lanes[:1] < begin, pivot, jnp.broadcast_to(line[:, at : at + 1], (1, width)))
        line = line / pivot
        table = jnp.where(lines == step, line, table - column * line)
    return table


def final_body(index, given, last, out, scratch):
    size = given.shape[0] * given.shape[2]
    gather = lambda ref, item: jnp.concatenate([ref[probe, item] for probe in range(ref.shape[0])], axis=0)
    lines = lax.broadcasted_iota(jnp.int32, (size, size), 0)
    lanes = lax.broadcasted_iota(jnp.int32, (size, size), 1)
    unit = jnp.where(lines == lanes, 1.0, 0.0)
    turned = lambda matrix: exact(matrix, unit, (0, 0))
    tables = gather(last, 1)
    same = tables[:, :size]
    mixed = tables[:, size : 2 * size]
    other = tables[:, 2 * size : 3 * size]
    other_mapped = tables[:, 3 * size :]
    scale = gather(given, 2)[:, :size]
    current = 0.5 * (same + turned(same))
    other = 0.5 * (other + turned(other))
    other_mapped = 0.5 * (other_mapped + turned(other_mapped))
    same_mapped = scale * turned(current - mixed)
    same_mapped = 0.5 * (same_mapped + turned(same_mapped))
    mixed_mapped = scale * (mixed - other)
    solved = eliminate(jnp.concatenate([same_mapped, current, current, unit], axis=1), (0, 2 * size))
    step_first = solved[:, size : 2 * size]
    inverse = solved[:, 3 * size :]
    onto_second = scale * step_first
    onto_first = unit - onto_second

    def quadratic(upper, lower, one, cross, two):
        top = exact(one, upper, (1, 0)) + exact(cross, lower, (1, 0))
        bottom = exact(cross, upper, (0, 0)) + exact(two, lower, (1, 0))
        value = exact(upper, top, (0, 0)) + exact(lower, bottom, (0, 0))
        return 0.5 * (value + turned(value))

    following = quadratic(onto_first, onto_second, current, mixed, other)
    direction = onto_first + exact(inverse, following, (1, 0))
    curvature = quadratic(direction, onto_second, same_mapped, mixed_mapped, other_mapped)
    step_second = eliminate(jnp.concatenate([curvature, following], axis=1), (0,))[:, size:]
    moved_first = exact(direction, step_second, (1, 0))
    moved_second = exact(onto_second, step_second, (1, 0))
    image = scale * moved_first
    basis = jnp.concatenate([gather(given, 0), gather(given, 1), gather(last, 0)], axis=0)
    scratch[0] = exact(jnp.concatenate([step_first + moved_first, moved_second], axis=0), basis[: 2 * size], (0, 0))
    scratch[1] = exact(
        jnp.concatenate([onto_first - image, onto_second + image, -moved_second], axis=0), basis, (0, 0)
    )
    probes = given.shape[2]
    begin = pl.multiple_of(index[1] * probes, probes)
    for worker in range(out.shape[0]):
        out[worker, 0] = scratch[0, pl.ds(begin, probes), :]
        out[worker, 1] = scratch[1, pl.ds(begin, probes), :]


def kernel(body, shape, places, scratch, name, cost):
    return pl.pallas_call(
        body,
        out_shape=jax.ShapeDtypeStruct(shape, f32),
        in_specs=[pl.BlockSpec(memory_space=place) for place in places],
        out_specs=pl.BlockSpec(memory_space=pltpu.VMEM),
        scratch_shapes=scratch,
        cost_estimate=pl.CostEstimate(flops=cost, transcendentals=0, bytes_accessed=1 << 22),
        name=name,
    )


def exchange(chunks, axis, beside=()):
    chunks, beside = lax.optimization_barrier((chunks, beside))
    got = lax.all_to_all(chunks, axis, 0, 0, tiled=True)
    return lax.optimization_barrier((got, beside))


def copies(rows, size):
    return jnp.broadcast_to(rows[None], (size,) + rows.shape)


def local(tiles, tile_rows, tile_firms, worker_ids, sign_words, regular):
    probe_dev = sign_words.shape[0]
    firms = lax.axis_size("firm")
    workers = lax.axis_size("worker")
    probes = lax.axis_size("probe")
    count = tiles.shape[0]
    reg_blocks = regular.reshape(workers, TILE)
    index = jnp.stack([lax.axis_index("worker"), lax.axis_index("probe")]).astype(jnp.int32)
    reg_own = lax.dynamic_slice_in_dim(reg_blocks, index[0], 1, 0)
    beside = (index, reg_own)

    tiles_vmem = pltpu.VMEM(tiles.shape, bf16)
    rows_vmem = pltpu.VMEM((ROWB_DEV, probe_dev, TILE), bf16)
    total_vmem = pltpu.VMEM((ROWB_DEV, probe_dev, TILE), f32)
    arrived = pltpu.SemaphoreType.DMA((CHUNKS,))
    VMEM, SMEM, ANY = pltpu.VMEM, pltpu.SMEM, pl.ANY
    cost = 2 * count * probe_dev * TILE * TILE

    def owner_total(parts, beside):
        chunk = parts.reshape(workers, -1, TILE)
        got, beside = exchange(chunk, "worker", beside)
        got = jnp.sum(got, axis=0)
        kept = firms * probe_dev
        chunk = got[:kept].reshape(firms, probe_dev, TILE)
        if got.shape[0] > kept:
            chunk = jnp.concatenate([chunk, copies(got[kept:], firms)], axis=1)
        got, beside = exchange(chunk, "firm", beside)
        return jnp.sum(got, axis=0), beside

    def collect(own, beside):
        column, beside = exchange(copies(own.astype(bf16), firms), "firm", beside)
        field, beside = exchange(copies(column, workers), "worker", beside)
        return field.reshape(workers * firms, probe_dev, TILE), beside

    def bind(body):
        return lambda *refs: body(workers, firms, *refs)

    parts = kernel(
        bind(start_body), (workers * firms, probe_dev, TILE), [SMEM, SMEM, VMEM, VMEM, ANY],
        [tiles_vmem, rows_vmem, arrived], "start", cost,
    )(tile_rows, tile_firms, sign_words, worker_ids, tiles)
    first, beside = owner_total(parts, beside)

    field, (first, index, reg_own) = collect(first, (first, *beside))
    parts = kernel(
        bind(middle_body), (workers * (firms + 1), probe_dev, TILE),
        [SMEM, SMEM, SMEM, VMEM, VMEM, VMEM, VMEM, ANY],
        [tiles_vmem, rows_vmem, total_vmem, arrived], "middle", 2 * cost,
    )(tile_rows, tile_firms, index, field, first, reg_blocks, worker_ids, tiles)
    got, (first, index, reg_own) = owner_total(parts, (first, index, reg_own))
    quotient = got[probe_dev:, :1] / got[probe_dev:, TILE // 2 : TILE // 2 + 1]
    second = first - (got[:probe_dev] + reg_own * first) / quotient
    quotient = jnp.broadcast_to(quotient, second.shape)

    field, (first, second, quotient, index, reg_own) = collect(second, (first, second, quotient, index, reg_own))
    sent = kernel(
        bind(rows_body), (probes, 3 + ROWB_DEV, probe_dev, TILE),
        [SMEM, SMEM, VMEM, VMEM, VMEM, VMEM, VMEM, ANY],
        [tiles_vmem, total_vmem, arrived], "rows", cost,
    )(tile_rows, tile_firms, field, first, second, quotient, worker_ids, tiles)
    given, (second, index, reg_own) = exchange(sent, "probe", (second, index, reg_own))
    parts = kernel(
        bind(last_body), (workers * (firms + 1), probe_dev, TILE),
        [SMEM, SMEM, SMEM, VMEM, VMEM, ANY],
        [tiles_vmem, rows_vmem, arrived], "last", cost,
    )(tile_rows, tile_firms, index, given, reg_blocks, tiles)
    got, (second, index, reg_own, given) = owner_total(parts, (second, index, reg_own, given))
    third = got[:probe_dev] + reg_own * second
    sent = jnp.stack([third, got[probe_dev:]], axis=0)
    last, (index, given) = exchange(copies(sent, probes), "probe", (index, given))
    outs = kernel(
        final_body, (workers, 2, probe_dev, TILE), [SMEM, VMEM, VMEM],
        [pltpu.VMEM((2, probes * probe_dev, TILE), f32)], "final", cost // 4,
    )(index, given, last)
    outs, _ = exchange(outs, "worker")
    outs = jnp.transpose(outs, (1, 2, 0, 3)).reshape(2, probe_dev, workers * TILE)
    return (outs[0], outs[1])


def solution(mesh):
    placed = (
        P(("firm", "worker"), None, None),
        P(("firm", "worker"), None),
        P(("firm", "worker"), None),
        P(("firm", "worker"), None),
        P("probe", ("firm", "worker"), None),
        P("firm"),
    )
    return jax.shard_map(
        local,
        mesh=mesh,
        in_specs=placed,
        out_specs=(P("probe", "firm"), P("probe", "firm")),
        check_vma=False,
    )
```

time: 607 us -> 228 us (0.38)
  the two profiles are of different devices: /device:TPU:2 before, /device:TPU:1 now
where the time goes in v2:
time: 228 us; the launch traced here: 227 us
  blocking collectives  187 us (82%)
  Pallas kernels  34 us (15%)
  local copies, waits for them, and re-layouts  3.5 us (2%)
  other arithmetic  2.34 us (1%)
    all_to_all x13, blocking collectives, exchange(): got = lax.all_to_all(chunks, axis, 0, 0, tiled=True)  187 us
    pallas_call x1, Pallas kernels, local(): kernel(final_body, (workers, 2, probe_dev, TILE), [SMEM, VMEM, VMEM], [pl...  9.77 us
    pallas_call x1, Pallas kernels, local(): kernel(bind(middle_body), (workers * (firms + 1), probe_dev, TILE), [SMEM...  8.45 us
    pallas_call x1, Pallas kernels, local(): kernel(bind(rows_body), (probes, 3 + ROWB_DEV, probe_dev, TILE), [SMEM, S...  6.22 us
    pallas_call x1, Pallas kernels, local(): kernel(bind(last_body), (workers * (firms + 1), probe_dev, TILE), [SMEM,...  4.88 us
    pallas_call x1, Pallas kernels, local(): kernel(bind(start_body), (workers * firms, probe_dev, TILE), [SMEM, SMEM,...  4.7 us

profile of v2, /device:TPU:1, one launch (start us, length us, event | category | flops | bytes accessed | tf_op | source)
XLA Modules:
  0.0 227.3 jit_solution(16012383284119284189)
XLA Ops:
  0.6 1.4 copy.9.refs_2_
  2.0 0.6 pad_add_fusion.refs_2_.index
  2.6 0.7 constant_dynamic-slice_fusion
  3.3 4.7 %start.1 = f32[128,8,128]{2,1,0:T(8,128)} custom-call(s32[1,128]{1,0:T(1,128)} %refs_0_.7, s32[1,128]{1,0:T(1,128)} %refs_1_.7, s32[8,4,5]{2,1,0:T(4,128)} %copy.9.refs_2_, s32[1,512]{1,0:T(1,128)} %refs_6_.3, bf16[128,128,128]{2,1,0:T(8,128)(2,1)} %refs_5_.1), custom_call_target="tpu_custom_call" | custom-call | flops 33554432 | bytes 4194304 | tf_op jit(solution)/shard_map/start/pallas_call | solution.py:315
  8.0 19.6 %all_to_all.65 = f32[8,128,128]{2,1,0:T(8,128)S(1)} all-to-all(f32[8,128,128]{2,1,0:T(8,128)} %bitcast.26), channel_id=1, replica_groups=mesh['firm'=16,'worker'=8,'probe'=4] {'worker'}, dimensions={0} | all-to-all | bytes 1048576 | tf_op jit(solution)/shard_map/all_to_all | solution.py:270
  27.6 22.0 %all_to_all.66 = f32[16,8,128]{2,1,0:T(8,128)S(1)} all-to-all(f32[16,8,128]{2,1,0:T(8,128)S(1)} %bitcast.30), channel_id=1, replica_groups=mesh['firm'=16,'worker'=8,'probe'=4] {'firm'}, dimensions={0} | all-to-all | bytes 131072 | tf_op jit(solution)/shard_map/all_to_all | solution.py:270
  49.7 0.0 copy-start
  49.7 14.3 %all_to_all.67 = bf16[16,8,128]{2,1,0:T(8,128)(2,1)S(1)} all-to-all(bf16[16,8,128]{2,1,0:T(8,128)(2,1)S(1)} %broadcast_in_dim.14), channel_id=1, replica_groups=mesh['firm'=16,'worker'=8,'probe'=4] {'firm'}, dimensions={0} | all-to-all | bytes 65536 | tf_op jit(solution)/shard_map/all_to_all | solution.py:270
  64.0 13.1 %all_to_all.68 = bf16[8,16,8,128]{3,2,1,0:T(8,128)(2,1)} all-to-all(bf16[8,16,8,128]{3,2,1,0:T(8,128)(2,1)S(1)} %broadcast_in_dim.15), channel_id=1, replica_groups=mesh['firm'=16,'worker'=8,'probe'=4] {'worker'}, dimensions={0} | all-to-all | bytes 524288 | tf_op jit(solution)/shard_map/all_to_all | solution.py:270
  77.2 0.0 copy-done
  77.2 8.4 %middle.1 = f32[136,8,128]{2,1,0:T(8,128)} custom-call(s32[1,128]{1,0:T(1,128)} %refs_0_.7, s32[1,128]{1,0:T(1,128)} %refs_1_.7, s32[2]{0:T(128)} %pad_add_fusion.refs_2_.index, bf16[128,8,128]{2,1,0:T(8,128)(2,1)} %bitcast.28, f32[8,128]{1,0:T(8,128)} %copy-done, f32[8,128]{1,0:T(8,128)} %bitcast.32, s32[1,512]{1,0:T(1,128)} %refs_6_.3, ...), custom_call_target="tpu_custom_call" | custom-call | flops 67108864 | bytes 4194304 | tf_op jit(solution)/shard_map/middle/pallas_call | solution.py:322
  85.6 14.6 %all_to_all.69 = f32[8,136,128]{2,1,0:T(8,128)S(1)} all-to-all(f32[8,136,128]{2,1,0:T(8,128)} %bitcast.25), channel_id=1, replica_groups=mesh['firm'=16,'worker'=8,'probe'=4] {'worker'}, dimensions={0} | all-to-all | bytes 1114112 | tf_op jit(solution)/shard_map/all_to_all | solution.py:270
  100.4 14.7 %all_to_all.70 = f32[16,16,128]{2,1,0:T(8,128)S(1)} all-to-all(f32[16,16,128]{2,1,0:T(8,128)S(1)} %pad_maximum_fusion), channel_id=1, replica_groups=mesh['firm'=16,'worker'=8,'probe'=4] {'firm'}, dimensions={0} | all-to-all | bytes 262144 | tf_op jit(solution)/shard_map/all_to_all | solution.py:270
  115.1 0.2 fusion.3
  115.3 1.4 fusion.4
  116.6 0.7 div.15.refs_5_
  117.3 17.6 %all_to_all.71 = bf16[16,8,128]{2,1,0:T(8,128)(2,1)S(1)} all-to-all(bf16[16,8,128]{2,1,0:T(8,128)(2,1)S(1)} %broadcast_in_dim.17), channel_id=1, replica_groups=mesh['firm'=16,'worker'=8,'probe'=4] {'firm'}, dimensions={0} | all-to-all | bytes 65536 | tf_op jit(solution)/shard_map/all_to_all | solution.py:270
  134.9 11.6 %all_to_all.72 = bf16[8,16,8,128]{3,2,1,0:T(8,128)(2,1)} all-to-all(bf16[8,16,8,128]{3,2,1,0:T(8,128)(2,1)S(1)} %broadcast_in_dim.18), channel_id=1, replica_groups=mesh['firm'=16,'worker'=8,'probe'=4] {'worker'}, dimensions={0} | all-to-all | bytes 524288 | tf_op jit(solution)/shard_map/all_to_all | solution.py:270
  146.6 6.2 %rows.1 = f32[4,7,8,128]{3,2,1,0:T(8,128)} custom-call(s32[1,128]{1,0:T(1,128)} %refs_0_.7, s32[1,128]{1,0:T(1,128)} %refs_1_.7, bf16[128,8,128]{2,1,0:T(8,128)(2,1)} %bitcast.27, f32[8,128]{1,0:T(8,128)} %copy-done, f32[8,128]{1,0:T(8,128)} %get-tuple-element.197.refs_4_, f32[8,128]{1,0:T(8,128)} %div.15.refs_5_, s32[1,512]{1,0:T(1,128)} %refs_6_.3, ...), custom_call_target="tpu_custom_call" | custom-call | flops 33554432 | bytes 4194304 | tf_op jit(solution)/shard_map/rows/pallas_call | solution.py:333
  152.8 0.0 copy-start.1
  152.8 8.9 %all_to_all.73.refs_3_.given = f32[4,7,8,128]{3,2,1,0:T(8,128)} all-to-all(f32[4,7,8,128]{3,2,1,0:T(8,128)} %rows.1), channel_id=1, replica_groups=mesh['firm'=16,'worker'=8,'probe'=4] {'probe'}, dimensions={0} | all-to-all | bytes 229376 | tf_op jit(solution)/shard_map/all_to_all | solution.py:270
  161.7 4.9 %last.1 = f32[136,8,128]{2,1,0:T(8,128)} custom-call(s32[1,128]{1,0:T(1,128)} %refs_0_.7, s32[1,128]{1,0:T(1,128)} %refs_1_.7, s32[2]{0:T(128)} %pad_add_fusion.refs_2_.index, f32[4,7,8,128]{3,2,1,0:T(8,128)} %all_to_all.73.refs_3_.given, f32[8,128]{1,0:T(8,128)} %bitcast.33, bf16[128,128,128]{2,1,0:T(8,128)(2,1)} %refs_5_.1), custom_call_target="tpu_custom_call" | custom-call | flops 33554432 | bytes 4194304 | tf_op jit(solution)/shard_map/last/pallas_call | solution.py:339
  166.6 16.1 %all_to_all.74 = f32[8,136,128]{2,1,0:T(8,128)S(1)} all-to-all(f32[8,136,128]{2,1,0:T(8,128)} %bitcast.24), channel_id=1, replica_groups=mesh['firm'=16,'worker'=8,'probe'=4] {'worker'}, dimensions={0} | all-to-all | bytes 1114112 | tf_op jit(solution)/shard_map/all_to_all | solution.py:270
  182.7 14.7 %all_to_all.75 = f32[16,16,128]{2,1,0:T(8,128)S(1)} all-to-all(f32[16,16,128]{2,1,0:T(8,128)S(1)} %pad_maximum_fusion.1), channel_id=1, replica_groups=mesh['firm'=16,'worker'=8,'probe'=4] {'firm'}, dimensions={0} | all-to-all | bytes 262144 | tf_op jit(solution)/shard_map/all_to_all | solution.py:270
  197.4 0.0 copy-done.1
  197.5 7.3 %all_to_all.76.last = f32[4,2,8,128]{3,2,1,0:T(8,128)} all-to-all(f32[4,2,8,128]{3,2,1,0:T(8,128)S(1)} %broadcast_in_dim.20), channel_id=1, replica_groups=mesh['firm'=16,'worker'=8,'probe'=4] {'probe'}, dimensions={0} | all-to-all | bytes 65536 | tf_op jit(solution)/shard_map/all_to_all | solution.py:270
  204.8 9.8 %final.1 = f32[8,2,8,128]{3,2,1,0:T(8,128)} custom-call(s32[2]{0:T(128)} %pad_add_fusion.refs_2_.index, f32[4,7,8,128]{3,2,1,0:T(8,128)} %all_to_all.73.refs_3_.given, f32[4,2,8,128]{3,2,1,0:T(8,128)} %all_to_all.76.last), custom_call_target="tpu_custom_call" | custom-call | flops 8388608 | bytes 4194304 | tf_op jit(solution)/shard_map/final/pallas_call | solution.py:348
  214.6 12.1 %all_to_all.77 = f32[8,2,8,128]{3,2,1,0:T(8,128)S(1)} all-to-all(f32[8,2,8,128]{3,2,1,0:T(8,128)} %final.1), channel_id=1, replica_groups=mesh['firm'=16,'worker'=8,'probe'=4] {'worker'}, dimensions={0} | all-to-all | bytes 131072 | tf_op jit(solution)/shard_map/all_to_all | solution.py:270
  226.7 0.6 slice_bitcast_fusion.2
  (22 shorter events, 0.3 us)
Async XLA Ops:
  49.7 27.5 %copy-start = (f32[8,128]{1,0:T(8,128)}, f32[8,128]{1,0:T(8,128)S(1)}, u32[]{:S(2)}) copy-start(f32[8,128]{1,0:T(8,128)S(1)} %reduce_sum.55.refs_4_.refs_3_) | copy-start | bytes 12292
  152.8 44.6 %copy-start.1 = (f32[8,128]{1,0:T(8,128)S(1)}, f32[8,128]{1,0:T(8,128)}, u32[]{:S(2)}) copy-start(f32[8,128]{1,0:T(8,128)} %get-tuple-element.197.refs_4_) | copy-start | bytes 12292

commit v3 on v2

v3 whole, which is shorter than its diff:
```python
import jax
import jax.numpy as jnp
from jax import lax
from jax.experimental import pallas as pl
from jax.experimental.pallas import tpu as pltpu
from jax.sharding import PartitionSpec as P

TILE = 128
ROWB_DEV = 4
ROWS_DEV = 512
SHARD_WORKERS = 128
BITS = 30
CHUNKS = 8

largest_value = lax.Precision.HIGHEST
f32 = jnp.float32
bf16 = jnp.bfloat16


def dot(left, right, dims, precision=None):
    return lax.dot_general(
        left, right, ((dims[:1], dims[1:]), ((), ())), precision=precision, preferred_element_type=f32
    )


def exact(left, right, dims):
    return dot(left, right, dims, largest_value)


def three_parts(values):
    high = values.astype(bf16)
    rest = values - high.astype(f32)
    middle = rest.astype(bf16)
    low = (rest - middle.astype(f32)).astype(bf16)
    return high, middle, low


def demean(values, worker_ids):
    probes = values.shape[0]
    workers = lax.broadcasted_iota(jnp.int32, (SHARD_WORKERS, ROWS_DEV), 0)
    onehot = jnp.where(workers == worker_ids, 1.0, 0.0).astype(bf16)
    stacked = jnp.concatenate([*(part.astype(f32) for part in three_parts(values)), jnp.ones_like(values)], axis=0)
    sums = dot(stacked.astype(bf16), onehot, (1, 1))
    totals = (sums[2 * probes : 3 * probes] + sums[probes : 2 * probes]) + sums[:probes]
    means = totals / sums[3 * probes :]
    stacked = jnp.concatenate([part.astype(f32) for part in three_parts(means)], axis=0)
    spread = dot(stacked.astype(bf16), onehot, (1, 0))
    return values - ((spread[2 * probes : 3 * probes] + spread[probes : 2 * probes]) + spread[:probes])


def fetch(tiles_hbm, tiles, arrived):
    size = tiles.shape[0] // CHUNKS

    def copy(chunk):
        part = pl.ds(chunk * size, size)
        return pltpu.make_async_copy(tiles_hbm.at[part], tiles.at[part], arrived.at[chunk])

    for chunk in range(CHUNKS):
        copy(chunk).start()
    return lambda chunk: copy(chunk).wait()


def place_of(firm, workers, stride):
    return (firm & (workers - 1)) * stride + (firm >> (workers.bit_length() - 1))


def pair(upper, lower):
    return jnp.concatenate([upper.astype(f32), lower.astype(f32)], axis=0).astype(bf16)


def forward(tile_rows, tile_firms, field, tiles, workers, firms, wait):
    total = None
    size = tiles.shape[0] // CHUNKS
    for tile in range(0, tiles.shape[0], 2):
        if tile % size == 0:
            wait(tile // size)
        pieces = [field[place_of(tile_firms[0, tile + item], workers, firms)] for item in range(2)]
        probes = pieces[0].shape[0]
        weights = jnp.concatenate([tiles[tile], tiles[tile + 1]], axis=0)
        both = dot(pair(*pieces), weights, (1, 1))
        if total is None:
            total = [jnp.zeros((probes, TILE), f32) for block in range(ROWB_DEV)]
        for item in range(2):
            image = both[item * probes : (item + 1) * probes, item * TILE : (item + 1) * TILE]
            row = tile_rows[0, tile + item]
            total = [old + jnp.where(row == block, image, 0.0) for block, old in enumerate(total)]
    return total


def adjoint(tile_rows, tile_firms, rows, tiles, out, workers, stride, wait=None):
    out[...] = jnp.zeros_like(out)
    probes = rows.shape[1]
    size = tiles.shape[0] // CHUNKS
    for tile in range(0, tiles.shape[0], 2):
        if wait is not None and tile % size == 0:
            wait(tile // size)
        pieces = [rows[tile_rows[0, tile + item]] for item in range(2)]
        weights = jnp.concatenate([tiles[tile], tiles[tile + 1]], axis=1)
        both = dot(pair(*pieces), weights, (1, 0))
        for item in range(2):
            image = both[item * probes : (item + 1) * probes, item * TILE : (item + 1) * TILE]
            place = place_of(tile_firms[0, tile + item], workers, stride)
            out[place] = out[place] + image


def put_rows(rows, values):
    for block in range(ROWB_DEV):
        rows[block] = values[:, block * TILE : (block + 1) * TILE].astype(bf16).astype(f32)


def add_ridge(out, place, regular, worker, own):
    out[place] = out[place] + regular[pl.ds(worker, 1), :] * own


def start_body(workers, firms, tile_rows, tile_firms, words, worker_ids, tiles_hbm, out, tiles, rows, arrived):
    wait = fetch(tiles_hbm, tiles, arrived)
    words_row, blocks, probes = words.shape
    lanes = lax.broadcasted_iota(jnp.int32, (probes, TILE), 1)
    lines = lax.broadcasted_iota(jnp.int32, (probes, TILE), 0)
    word_of = lax.div(lanes, jnp.int32(BITS))
    bit = lanes - word_of * BITS
    chosen = [jnp.zeros((probes, TILE), jnp.int32) for block in range(blocks)]
    for word in range(words_row):
        for probe in range(probes):
            here = (word_of == word) & (lines == probe)
            chosen = [jnp.where(here, words[word, block, probe], old) for block, old in enumerate(chosen)]
    signs = [(2 * (lax.shift_right_logical(old, bit) & 1) - 1).astype(f32) for old in chosen]
    put_rows(rows, demean(jnp.concatenate(signs, axis=1), worker_ids[...]))
    adjoint(tile_rows, tile_firms, rows, tiles, out, workers, firms, wait)


def middle_body(
    workers, firms, tile_rows, tile_firms, worker, firm, field, first, regular, worker_ids, tiles_hbm,
    out, tiles, rows, arrived,
):
    wait = fetch(tiles_hbm, tiles, arrived)
    total = forward(tile_rows, tile_firms, field, tiles, workers, firms, wait)
    values = demean(jnp.concatenate(total, axis=1), worker_ids[...])
    put_rows(rows, values)
    adjoint(tile_rows, tile_firms, rows, tiles, out, workers, firms + 1)
    own = first[...]
    add_ridge(out, worker[0] * (firms + 1) + firm[0], regular, worker[0], own)
    squares = own * own
    above = jnp.sum(values * values, axis=1, keepdims=True)
    above = above + jnp.sum(squares * regular[pl.ds(worker[0], 1), :], axis=1, keepdims=True)
    below = jnp.sum(squares, axis=1, keepdims=True)
    lanes = lax.broadcasted_iota(jnp.int32, own.shape, 1)
    extra = jnp.where(lanes < TILE // 2, above, below)
    for other in range(workers):
        out[other * (firms + 1) + firms] = extra


def rows_body(
    workers, firms, tile_rows, tile_firms, field, first, second, quotient, worker_ids, tiles_hbm,
    out, tiles, rows, arrived,
):
    wait = fetch(tiles_hbm, tiles, arrived)
    total = forward(tile_rows, tile_firms, field, tiles, workers, firms, wait)
    values = demean(jnp.concatenate(total, axis=1), worker_ids[...])
    for probe in range(out.shape[0]):
        out[probe, 0] = first[...]
        out[probe, 1] = second[...]
        out[probe, 2] = quotient[...]
        for block in range(ROWB_DEV):
            out[probe, 3 + block] = values[:, block * TILE : (block + 1) * TILE]


def last_body(
    workers, firms, tile_rows, tile_firms, worker, firm, probe, given, regular, tiles_hbm,
    out, tiles, rows, arrived,
):
    wait = fetch(tiles_hbm, tiles, arrived)
    gather = lambda item: jnp.concatenate([given[other, item] for other in range(given.shape[0])], axis=0)
    own = lambda item: given[probe[0], item]
    first, second = own(0), own(1)
    first_all, second_all = gather(0), gather(1)
    mine = [own(3 + block) for block in range(ROWB_DEV)]
    for block in range(ROWB_DEV):
        rows[block] = mine[block].astype(bf16).astype(f32)
    adjoint(tile_rows, tile_firms, rows, tiles, out, workers, firms + 1, wait)
    add_ridge(out, worker[0] * (firms + 1) + firm[0], regular, worker[0], second)
    left = jnp.concatenate([*mine, second * regular[pl.ds(worker[0], 1), :]], axis=1)
    right = jnp.concatenate([*(gather(3 + block) for block in range(ROWB_DEV)), second_all], axis=1)
    extra = jnp.concatenate(
        [
            exact(first, first_all, (1, 1)),
            exact(first, second_all, (1, 1)),
            exact(second, second_all, (1, 1)),
            exact(left, right, (1, 1)),
        ],
        axis=1,
    )
    for other in range(workers):
        out[other * (firms + 1) + firms] = extra


def eliminate(table, pivots):
    size, width = table.shape
    lanes = lax.broadcasted_iota(jnp.int32, (size, width), 1)
    lines = lax.broadcasted_iota(jnp.int32, (size, width), 0)

    def spread(at):
        column = jnp.broadcast_to(table[:, pivots[0] + at : pivots[0] + at + 1], (size, width))
        for begin in pivots[1:]:
            other = jnp.broadcast_to(table[:, begin + at : begin + at + 1], (size, width))
            column = jnp.where(lanes < begin, column, other)
        return column

    for step in range(0, size, 2):
        one, two = spread(step), spread(step + 1)
        first, second = table[step : step + 1, :], table[step + 1 : step + 2, :]
        a, b = one[step : step + 1, :], two[step : step + 1, :]
        c, d = one[step + 1 : step + 2, :], two[step + 1 : step + 2, :]
        inverse = 1.0 / (a * d - b * c)
        upper = (d * first - b * second) * inverse
        lower = (a * second - c * first) * inverse
        table = table - one * upper - two * lower
        table = jnp.where(lines == step, upper, jnp.where(lines == step + 1, lower, table))
    return table


def final_body(probe, given, last, out, scratch):
    size = given.shape[0] * given.shape[2]
    gather = lambda ref, item: jnp.concatenate([ref[other, item] for other in range(ref.shape[0])], axis=0)
    half = lambda matrix: 0.5 * (matrix + matrix.T)
    lines = lax.broadcasted_iota(jnp.int32, (size, size), 0)
    lanes = lax.broadcasted_iota(jnp.int32, (size, size), 1)
    unit = jnp.where(lines == lanes, 1.0, 0.0)
    tables = gather(last, 1)
    current = half(tables[:, :size])
    mixed = tables[:, size : 2 * size]
    other = tables[:, 2 * size : 3 * size]
    other_mapped = tables[:, 3 * size :]
    scale = gather(given, 2)[:, :size]
    same_mapped = half(scale * (current - mixed).T)
    mixed_mapped = scale * (mixed - other)

    def whole(one, cross, two):
        return jnp.concatenate(
            [jnp.concatenate([one, cross], axis=1), jnp.concatenate([cross.T, two], axis=1)], axis=0
        )

    grams = whole(current, mixed, other)
    mapped_grams = whole(same_mapped, mixed_mapped, other_mapped)
    solved = eliminate(jnp.concatenate([same_mapped, current, current, unit], axis=1), (0, 2 * size))
    step_first = solved[:, size : 2 * size]
    inverse = solved[:, 3 * size :]
    onto_second = scale * step_first
    onto_first = unit - onto_second
    mix = jnp.concatenate([onto_first, onto_second], axis=0)
    following = half(exact(mix, exact(grams, mix, (1, 0)), (0, 0)))
    direction = onto_first + exact(inverse, following, (1, 0))
    mix = jnp.concatenate([direction, onto_second], axis=0)
    curvature = half(exact(mix, exact(mapped_grams, mix, (1, 0)), (0, 0)))
    step_second = eliminate(jnp.concatenate([curvature, following], axis=1), (0,))[:, size:]
    moved = exact(mix, step_second, (1, 0))
    moved_first, moved_second = moved[:size], moved[size:]
    image = scale * moved_first
    basis = jnp.concatenate([gather(given, 0), gather(given, 1), gather(last, 0)], axis=0)
    scratch[0] = exact(jnp.concatenate([step_first + moved_first, moved_second], axis=0), basis[: 2 * size], (0, 0))
    scratch[1] = exact(
        jnp.concatenate([onto_first - image, onto_second + image, -moved_second], axis=0), basis, (0, 0)
    )
    probes = given.shape[2]
    begin = pl.multiple_of(probe[0] * probes, probes)
    for worker in range(out.shape[0]):
        out[worker, 0] = scratch[0, pl.ds(begin, probes), :]
        out[worker, 1] = scratch[1, pl.ds(begin, probes), :]


def kernel(body, shapes, places, scratch, name, cost):
    return pl.pallas_call(
        body,
        out_shape=shapes,
        in_specs=[pl.BlockSpec(memory_space=place) for place in places],
        out_specs=jax.tree.map(lambda _: pl.BlockSpec(memory_space=pltpu.VMEM), shapes),
        scratch_shapes=scratch,
        compiler_params=pltpu.CompilerParams(vmem_limit_bytes=10 << 20),
        cost_estimate=pl.CostEstimate(flops=cost, transcendentals=0, bytes_accessed=1 << 22),
        name=name,
    )


def exchange(chunks, axis, beside=()):
    chunks, beside = lax.optimization_barrier((chunks, beside))
    got = lax.all_to_all(chunks, axis, 0, 0, tiled=True)
    return lax.optimization_barrier((got, beside))


def copies(rows, size):
    return jnp.broadcast_to(rows[None], (size,) + rows.shape)


def local(tiles, tile_rows, tile_firms, worker_ids, sign_words, regular):
    probe_dev = sign_words.shape[0]
    firms = lax.axis_size("firm")
    workers = lax.axis_size("worker")
    probes = lax.axis_size("probe")
    count = tiles.shape[0]
    reg_blocks = regular.reshape(workers, TILE)
    words = jnp.transpose(sign_words, (2, 1, 0))
    at = tuple(lax.axis_index(axis).reshape(1) for axis in ("firm", "worker", "probe"))

    VMEM, SMEM, HBM = pltpu.VMEM, pltpu.SMEM, pltpu.HBM
    scratch = [
        VMEM(tiles.shape, bf16), VMEM((ROWB_DEV, probe_dev, TILE), f32), pltpu.SemaphoreType.DMA((CHUNKS,))
    ]
    cost = 2 * count * probe_dev * TILE * TILE
    tiles = pltpu.with_memory_space_constraint(tiles, HBM)

    def shape(*dims):
        return jax.ShapeDtypeStruct(dims, f32)

    def owner_total(parts, beside):
        chunk = parts.reshape(workers, -1, TILE)
        got, beside = exchange(chunk, "worker", beside)
        got = jnp.sum(got, axis=0)
        kept = firms * probe_dev
        chunk = got[:kept].reshape(firms, probe_dev, TILE)
        if got.shape[0] > kept:
            chunk = jnp.concatenate([chunk, copies(got[kept:], firms)], axis=1)
        got, beside = exchange(chunk, "firm", beside)
        return jnp.sum(got, axis=0), beside

    def collect(own, beside):
        column, beside = exchange(copies(own.astype(bf16), firms), "firm", beside)
        field, beside = exchange(copies(column, workers), "worker", beside)
        return field.reshape(workers * firms, probe_dev, TILE), beside

    def bind(body):
        return lambda *refs: body(workers, firms, *refs)

    parts = kernel(
        bind(start_body), shape(workers * firms, probe_dev, TILE),
        [SMEM, SMEM, SMEM, VMEM, HBM], scratch, "start", cost,
    )(tile_rows, tile_firms, words, worker_ids, tiles)
    first, at = owner_total(parts, at)

    field, (first, *at) = collect(first, (first, *at))
    firm, worker, _ = at
    parts = kernel(
        bind(middle_body), shape(workers * (firms + 1), probe_dev, TILE),
        [SMEM, SMEM, SMEM, SMEM, VMEM, VMEM, VMEM, VMEM, HBM], scratch, "middle", 2 * cost,
    )(tile_rows, tile_firms, worker, firm, field, first, reg_blocks, worker_ids, tiles)
    got, (first, *at) = owner_total(parts, (first, *at))
    quotient = got[probe_dev:, :1] / got[probe_dev:, TILE // 2 : TILE // 2 + 1]
    quotient = jnp.broadcast_to(quotient, first.shape)
    second = first - got[:probe_dev] / quotient

    field, (first, second, quotient, *at) = collect(second, (first, second, quotient, *at))
    sent = kernel(
        bind(rows_body), shape(probes, 3 + ROWB_DEV, probe_dev, TILE),
        [SMEM, SMEM, VMEM, VMEM, VMEM, VMEM, VMEM, HBM], scratch, "rows", cost,
    )(tile_rows, tile_firms, field, first, second, quotient, worker_ids, tiles)
    given, at = exchange(sent, "probe", at)
    firm, worker, probe = at
    parts = kernel(
        bind(last_body), shape(workers * (firms + 1), probe_dev, TILE),
        [SMEM, SMEM, SMEM, SMEM, SMEM, VMEM, VMEM, HBM], scratch, "last", cost,
    )(tile_rows, tile_firms, worker, firm, probe, given, reg_blocks, tiles)
    got, (given, *at) = owner_total(parts, (given, *at))
    sent = copies(got.reshape(2, probe_dev, TILE), probes)
    last, (given, *at) = exchange(sent, "probe", (given, *at))
    outs = kernel(
        final_body, shape(workers, 2, probe_dev, TILE), [SMEM, VMEM, VMEM],
        [VMEM((2, probes * probe_dev, TILE), f32)], "final", cost // 4,
    )(at[2], given, last)
    outs, _ = exchange(outs, "worker")
    outs = jnp.transpose(outs, (1, 2, 0, 3)).reshape(2, probe_dev, workers * TILE)
    return (outs[0], outs[1])


def solution(mesh):
    placed = (
        P(("firm", "worker"), None, None),
        P(("firm", "worker"), None),
        P(("firm", "worker"), None),
        P(("firm", "worker"), None),
        P("probe", ("firm", "worker"), None),
        P("firm"),
    )
    return jax.shard_map(
        local,
        mesh=mesh,
        in_specs=placed,
        out_specs=(P("probe", "firm"), P("probe", "firm")),
        check_vma=False,
    )
```

time: 228 us -> 207 us (0.908)
  Pallas kernels: 34 us -> 20.8 us
  blocking collectives: 187 us -> 181 us
    pallas_call x5, Pallas kernels: 34 us -> 20.8 us  [the longest x1 5.01 us: local(): kernel(final_body, shape(workers, 2, probe_dev, TILE), [SMEM, VMEM, VMEM]...]
    all_to_all x13, blocking collectives: 187 us -> 181 us  [exchange(): got = lax.all_to_all(chunks, axis, 0, 0, tiled=True)]
where the time goes in v3:
time: 207 us
  blocking collectives  181 us (87%)
  Pallas kernels  20.8 us (10%)
  local copies, waits for them, and re-layouts  3.57 us (2%)
    all_to_all x13, blocking collectives, exchange(): got = lax.all_to_all(chunks, axis, 0, 0, tiled=True)  181 us
    pallas_call x1, Pallas kernels, local(): kernel(final_body, shape(workers, 2, probe_dev, TILE), [SMEM, VMEM, VMEM]...  5.01 us
    pallas_call x1, Pallas kernels, local(): kernel(bind(middle_body), shape(workers * (firms + 1), probe_dev, TILE),...  4.77 us

profile of v3, /device:TPU:1, one launch (start us, length us, event | category | flops | bytes accessed | tf_op | source)
XLA Modules:
  0.0 206.8 jit_solution(5173562748585789577)
XLA Ops:
  0.6 0.0 copy-start.7
  0.6 0.0 copy-start.5
  0.7 0.0 copy-start.1
  0.7 0.0 copy-start.2
  0.7 0.0 copy-start
  0.7 0.7 copy-done
  1.4 0.0 copy-start.3
  1.4 0.7 copy-done.3
  2.1 0.0 copy-start.4
  2.1 0.7 copy-done.4
  2.8 0.0 copy-start.6
  2.8 0.7 copy-done.6
  3.4 3.5 %start.1 = f32[128,8,128]{2,1,0:T(8,128)S(1)} custom-call(s32[1,128]{1,0:T(1,128)S(1)} %copy-done.4, s32[1,128]{1,0:T(1,128)S(1)} %copy-done.6, s32[5,4,8]{2,1,0:T(4,128)S(1)} %bitcast.28, s32[1,512]{1,0:T(1,128)S(1)} %copy-done, bf16[128,128,128]{2,1,0:T(8,128)(2,1)} %refs_7_.5), custom_call_target="tpu_custom_call" | custom-call | flops 33554432 | bytes 4194304 | tf_op jit(solution)/shard_map/start/pallas_call | solution.py:333
  6.9 18.6 %all_to_all.65 = f32[8,128,128]{2,1,0:T(8,128)S(1)} all-to-all(f32[8,128,128]{2,1,0:T(8,128)S(1)} %bitcast.23), channel_id=1, replica_groups=mesh['firm'=16,'worker'=8,'probe'=4] {'worker'}, dimensions={0} | all-to-all | bytes 1048576 | tf_op jit(solution)/shard_map/all_to_all | solution.py:286
  25.5 22.8 %all_to_all.66 = f32[16,8,128]{2,1,0:T(8,128)S(1)} all-to-all(f32[16,8,128]{2,1,0:T(8,128)S(1)} %bitcast.30), channel_id=1, replica_groups=mesh['firm'=16,'worker'=8,'probe'=4] {'firm'}, dimensions={0} | all-to-all | bytes 131072 | tf_op jit(solution)/shard_map/all_to_all | solution.py:286
  48.4 14.3 %all_to_all.67 = bf16[16,8,128]{2,1,0:T(8,128)(2,1)S(1)} all-to-all(bf16[16,8,128]{2,1,0:T(8,128)(2,1)S(1)} %broadcast_in_dim.20), channel_id=1, replica_groups=mesh['firm'=16,'worker'=8,'probe'=4] {'firm'}, dimensions={0} | all-to-all | bytes 65536 | tf_op jit(solution)/shard_map/all_to_all | solution.py:286
  62.7 12.5 %all_to_all.68 = bf16[8,16,8,128]{3,2,1,0:T(8,128)(2,1)S(1)} all-to-all(bf16[8,16,8,128]{3,2,1,0:T(8,128)(2,1)S(1)} %broadcast_in_dim.21), channel_id=1, replica_groups=mesh['firm'=16,'worker'=8,'probe'=4] {'worker'}, dimensions={0} | all-to-all | bytes 524288 | tf_op jit(solution)/shard_map/all_to_all | solution.py:286
  75.2 0.0 copy-done.7
  75.2 0.0 copy-done.5
  75.2 0.0 copy-done.1
  75.2 0.0 copy-done.2
  75.2 4.8 %middle.1 = f32[136,8,128]{2,1,0:T(8,128)S(1)} custom-call(s32[1,128]{1,0:T(1,128)S(1)} %copy-done.5, s32[1,128]{1,0:T(1,128)S(1)} %copy-done.7, s32[1]{0:T(128)} %bitcast.3.refs_2_, s32[1]{0:T(128)} %bitcast.2.refs_3_, bf16[128,8,128]{2,1,0:T(8,128)(2,1)S(1)} %bitcast.24, f32[8,128]{1,0:T(8,128)S(1)} %reduce_sum.55.refs_5_.refs_3_, f32[8,128]{1,0:T(8,128)S(1)} %bitcast.26, ...), custom_call_target="tpu_custom_call" | custom-call | flops 67108864 | bytes 4194304 | tf_op jit(solution)/shard_map/middle/pallas_call | solution.py:341
  80.0 13.6 %all_to_all.69 = f32[8,136,128]{2,1,0:T(8,128)S(1)} all-to-all(f32[8,136,128]{2,1,0:T(8,128)S(1)} %bitcast.22), channel_id=1, replica_groups=mesh['firm'=16,'worker'=8,'probe'=4] {'worker'}, dimensions={0} | all-to-all | bytes 1114112 | tf_op jit(solution)/shard_map/all_to_all | solution.py:286
  93.6 14.7 %all_to_all.70 = f32[16,16,128]{2,1,0:T(8,128)S(1)} all-to-all(f32[16,16,128]{2,1,0:T(8,128)S(1)} %pad_maximum_fusion), channel_id=1, replica_groups=mesh['firm'=16,'worker'=8,'probe'=4] {'firm'}, dimensions={0} | all-to-all | bytes 262144 | tf_op jit(solution)/shard_map/all_to_all | solution.py:286
  108.3 0.2 fusion.1
  108.5 0.1 fusion.2
  108.6 0.1 broadcast_in_dim.24.refs_5_
  108.7 17.6 %all_to_all.71 = bf16[16,8,128]{2,1,0:T(8,128)(2,1)S(1)} all-to-all(bf16[16,8,128]{2,1,0:T(8,128)(2,1)S(1)} %broadcast_in_dim.25), channel_id=1, replica_groups=mesh['firm'=16,'worker'=8,'probe'=4] {'firm'}, dimensions={0} | all-to-all | bytes 65536 | tf_op jit(solution)/shard_map/all_to_all | solution.py:286
  126.3 11.0 %all_to_all.72 = bf16[8,16,8,128]{3,2,1,0:T(8,128)(2,1)S(1)} all-to-all(bf16[8,16,8,128]{3,2,1,0:T(8,128)(2,1)S(1)} %broadcast_in_dim.26), channel_id=1, replica_groups=mesh['firm'=16,'worker'=8,'probe'=4] {'worker'}, dimensions={0} | all-to-all | bytes 524288 | tf_op jit(solution)/shard_map/all_to_all | solution.py:286
  137.3 4.0 %rows.1 = f32[4,7,8,128]{3,2,1,0:T(8,128)S(1)} custom-call(s32[1,128]{1,0:T(1,128)S(1)} %copy-done.5, s32[1,128]{1,0:T(1,128)S(1)} %copy-done.7, bf16[128,8,128]{2,1,0:T(8,128)(2,1)S(1)} %bitcast.25, f32[8,128]{1,0:T(8,128)S(1)} %reduce_sum.55.refs_5_.refs_3_, f32[8,128]{1,0:T(8,128)S(1)} %get-tuple-element.191.refs_4_, ...), custom_call_target="tpu_custom_call" | custom-call | flops 33554432 | bytes 4194304 | tf_op jit(solution)/shard_map/rows/pallas_call | solution.py:351
  141.3 8.6 %all_to_all.73.refs_5_.given = f32[4,7,8,128]{3,2,1,0:T(8,128)S(1)} all-to-all(f32[4,7,8,128]{3,2,1,0:T(8,128)S(1)} %rows.1), channel_id=1, replica_groups=mesh['firm'=16,'worker'=8,'probe'=4] {'probe'}, dimensions={0} | all-to-all | bytes 229376 | tf_op jit(solution)/shard_map/all_to_all | solution.py:286
  149.9 3.6 %last.1 = f32[136,8,128]{2,1,0:T(8,128)S(1)} custom-call(s32[1,128]{1,0:T(1,128)S(1)} %copy-done.5, s32[1,128]{1,0:T(1,128)S(1)} %copy-done.7, s32[1]{0:T(128)} %bitcast.3.refs_2_, s32[1]{0:T(128)} %bitcast.2.refs_3_, s32[1]{0:T(128)} %bitcast.4.refs_4_.probe, f32[4,7,8,128]{3,2,1,0:T(8,128)S(1)} %all_to_all.73.refs_5_.given, f32[8,128]{1,0:T(8,128)S(1)} %bitcast.27, ...), custom_call_target="tpu_custom_call" | custom-call | flops 33554432 | bytes 4194304 | tf_op jit(solution)/shard_map/last/pallas_call | solution.py:357
  153.4 15.0 %all_to_all.74 = f32[8,136,128]{2,1,0:T(8,128)S(1)} all-to-all(f32[8,136,128]{2,1,0:T(8,128)S(1)} %bitcast.21), channel_id=1, replica_groups=mesh['firm'=16,'worker'=8,'probe'=4] {'worker'}, dimensions={0} | all-to-all | bytes 1114112 | tf_op jit(solution)/shard_map/all_to_all | solution.py:286
  168.5 14.7 %all_to_all.75 = f32[16,16,128]{2,1,0:T(8,128)S(1)} all-to-all(f32[16,16,128]{2,1,0:T(8,128)S(1)} %pad_maximum_fusion.1), channel_id=1, replica_groups=mesh['firm'=16,'worker'=8,'probe'=4] {'firm'}, dimensions={0} | all-to-all | bytes 262144 | tf_op jit(solution)/shard_map/all_to_all | solution.py:286
  183.2 6.7 %all_to_all.76.last = f32[4,2,8,128]{3,2,1,0:T(8,128)S(1)} all-to-all(f32[4,2,8,128]{3,2,1,0:T(8,128)S(1)} %broadcast_in_dim.29), channel_id=1, replica_groups=mesh['firm'=16,'worker'=8,'probe'=4] {'probe'}, dimensions={0} | all-to-all | bytes 65536 | tf_op jit(solution)/shard_map/all_to_all | solution.py:286
  189.9 5.0 %final.1 = f32[8,2,8,128]{3,2,1,0:T(8,128)S(1)} custom-call(s32[1]{0:T(128)} %bitcast.4.refs_4_.probe, f32[4,7,8,128]{3,2,1,0:T(8,128)S(1)} %all_to_all.73.refs_5_.given, f32[4,2,8,128]{3,2,1,0:T(8,128)S(1)} %all_to_all.76.last), custom_call_target="tpu_custom_call" | custom-call | flops 8388608 | bytes 4194304 | tf_op jit(solution)/shard_map/final/pallas_call | solution.py:364
  194.9 11.2 %all_to_all.77 = f32[8,2,8,128]{3,2,1,0:T(8,128)S(1)} all-to-all(f32[8,2,8,128]{3,2,1,0:T(8,128)S(1)} %final.1), channel_id=1, replica_groups=mesh['firm'=16,'worker'=8,'probe'=4] {'worker'}, dimensions={0} | all-to-all | bytes 131072 | tf_op jit(solution)/shard_map/all_to_all | solution.py:286
  206.1 0.6 slice_bitcast_fusion.2
  (20 shorter events, 0.3 us)
Async XLA Ops:
  0.6 74.5 %copy-start.7 = (s32[1,128]{1,0:T(1,128)S(1)}, s32[1,128]{1,0:T(1,128)}, u32[]{:S(2)}) copy-start(s32[1,128]{1,0:T(1,128)} %refs_1_.7) | copy-start | bytes 1540
  0.6 74.5 %copy-start.5 = (s32[1,128]{1,0:T(1,128)S(1)}, s32[1,128]{1,0:T(1,128)}, u32[]{:S(2)}) copy-start(s32[1,128]{1,0:T(1,128)} %refs_0_.7) | copy-start | bytes 1540
  0.7 74.5 %copy-start.1 = (s32[1,512]{1,0:T(1,128)S(1)}, s32[1,512]{1,0:T(1,128)}, u32[]{:S(2)}) copy-start(s32[1,512]{1,0:T(1,128)} %refs_6_.1) | copy-start | bytes 6148
  0.7 74.5 %copy-start.2 = (f32[1024]{0:T(1024)S(1)}, f32[1024]{0:T(1024)}, u32[]{:S(2)}) copy-start(f32[1024]{0:T(1024)} %param.11) | copy-start | bytes 12292
  0.7 0.7 copy-start
  1.4 0.7 copy-start.3
  2.1 0.7 copy-start.4
  2.8 0.7 copy-start.6

commit v4 on v3

--- a/solution.py
+++ b/solution.py
@@ -10,7 +10,7 @@
 ROWS_DEV = 512
 SHARD_WORKERS = 128
 BITS = 30
-CHUNKS = 8
+CHUNKS = 4
 
 largest_value = lax.Precision.HIGHEST
 f32 = jnp.float32
@@ -48,8 +48,11 @@
     return values - ((spread[2 * probes : 3 * probes] + spread[probes : 2 * probes]) + spread[:probes])
 
 
-def fetch(tiles_hbm, tiles, arrived):
+def fetch(tiles_hbm, tiles, arrived, small):
     size = tiles.shape[0] // CHUNKS
+    tables = [pltpu.make_async_copy(*both, arrived.at[CHUNKS + item]) for item, both in enumerate(small)]
+    for table in tables:
+        table.start()
 
     def copy(chunk):
         part = pl.ds(chunk * size, size)
@@ -57,6 +60,8 @@
 
     for chunk in range(CHUNKS):
         copy(chunk).start()
+    for table in tables:
+        table.wait()
     return lambda chunk: copy(chunk).wait()
 
 
@@ -92,8 +97,9 @@
     probes = rows.shape[1]
     size = tiles.shape[0] // CHUNKS
     for tile in range(0, tiles.shape[0], 2):
-        if wait is not None and tile % size == 0:
+        if wait is not None and tile % (2 * size) == 0:
             wait(tile // size)
+            wait(tile // size + 1)
         pieces = [rows[tile_rows[0, tile + item]] for item in range(2)]
         weights = jnp.concatenate([tiles[tile], tiles[tile + 1]], axis=1)
         both = dot(pair(*pieces), weights, (1, 0))
@@ -112,8 +118,12 @@
     out[place] = out[place] + regular[pl.ds(worker, 1), :] * own
 
 
-def start_body(workers, firms, tile_rows, tile_firms, words, worker_ids, tiles_hbm, out, tiles, rows, arrived):
-    wait = fetch(tiles_hbm, tiles, arrived)
+def start_body(
+    workers, firms, rows_hbm, firms_hbm, words_hbm, ids_hbm, tiles_hbm,
+    out, tiles, rows, arrived, tile_rows, tile_firms, words, worker_ids,
+):
+    small = [(rows_hbm, tile_rows), (firms_hbm, tile_firms), (words_hbm, words), (ids_hbm, worker_ids)]
+    wait = fetch(tiles_hbm, tiles, arrived, small)
     words_row, blocks, probes = words.shape
     lanes = lax.broadcasted_iota(jnp.int32, (probes, TILE), 1)
     lines = lax.broadcasted_iota(jnp.int32, (probes, TILE), 0)
@@ -130,10 +140,10 @@
 
 
 def middle_body(
-    workers, firms, tile_rows, tile_firms, worker, firm, field, first, regular, worker_ids, tiles_hbm,
-    out, tiles, rows, arrived,
+    workers, firms, rows_hbm, firms_hbm, worker, firm, field, first, regular, worker_ids, tiles_hbm,
+    out, tiles, rows, arrived, tile_rows, tile_firms,
 ):
-    wait = fetch(tiles_hbm, tiles, arrived)
+    wait = fetch(tiles_hbm, tiles, arrived, [(rows_hbm, tile_rows), (firms_hbm, tile_firms)])
     total = forward(tile_rows, tile_firms, field, tiles, workers, firms, wait)
     values = demean(jnp.concatenate(total, axis=1), worker_ids[...])
     put_rows(rows, values)
@@ -151,10 +161,10 @@
 
 
 def rows_body(
-    workers, firms, tile_rows, tile_firms, field, first, second, quotient, worker_ids, tiles_hbm,
-    out, tiles, rows, arrived,
+    workers, firms, rows_hbm, firms_hbm, field, first, second, quotient, worker_ids, tiles_hbm,
+    out, tiles, rows, arrived, tile_rows, tile_firms,
 ):
-    wait = fetch(tiles_hbm, tiles, arrived)
+    wait = fetch(tiles_hbm, tiles, arrived, [(rows_hbm, tile_rows), (firms_hbm, tile_firms)])
     total = forward(tile_rows, tile_firms, field, tiles, workers, firms, wait)
     values = demean(jnp.concatenate(total, axis=1), worker_ids[...])
     for probe in range(out.shape[0]):
@@ -166,10 +176,10 @@
 
 
 def last_body(
-    workers, firms, tile_rows, tile_firms, worker, firm, probe, given, regular, tiles_hbm,
-    out, tiles, rows, arrived,
+    workers, firms, rows_hbm, firms_hbm, worker, firm, probe, given, regular, tiles_hbm,
+    out, tiles, rows, arrived, tile_rows, tile_firms,
 ):
-    wait = fetch(tiles_hbm, tiles, arrived)
+    wait = fetch(tiles_hbm, tiles, arrived, [(rows_hbm, tile_rows), (firms_hbm, tile_firms)])
     gather = lambda item: jnp.concatenate([given[other, item] for other in range(given.shape[0])], axis=0)
     own = lambda item: given[probe[0], item]
     first, second = own(0), own(1)
@@ -177,8 +187,6 @@
     mine = [own(3 + block) for block in range(ROWB_DEV)]
     for block in range(ROWB_DEV):
         rows[block] = mine[block].astype(bf16).astype(f32)
-    adjoint(tile_rows, tile_firms, rows, tiles, out, workers, firms + 1, wait)
-    add_ridge(out, worker[0] * (firms + 1) + firm[0], regular, worker[0], second)
     left = jnp.concatenate([*mine, second * regular[pl.ds(worker[0], 1), :]], axis=1)
     right = jnp.concatenate([*(gather(3 + block) for block in range(ROWB_DEV)), second_all], axis=1)
     extra = jnp.concatenate(
@@ -190,6 +198,8 @@
         ],
         axis=1,
     )
+    adjoint(tile_rows, tile_firms, rows, tiles, out, workers, firms + 1, wait)
+    add_ridge(out, worker[0] * (firms + 1) + firm[0], regular, worker[0], second)
     for other in range(workers):
         out[other * (firms + 1) + firms] = extra
 
@@ -303,10 +313,13 @@
 
     VMEM, SMEM, HBM = pltpu.VMEM, pltpu.SMEM, pltpu.HBM
     scratch = [
-        VMEM(tiles.shape, bf16), VMEM((ROWB_DEV, probe_dev, TILE), f32), pltpu.SemaphoreType.DMA((CHUNKS,))
+        VMEM(tiles.shape, bf16), VMEM((ROWB_DEV, probe_dev, TILE), f32), pltpu.SemaphoreType.DMA((CHUNKS + 4,)),
+        SMEM(tile_rows.shape, jnp.int32), SMEM(tile_firms.shape, jnp.int32),
     ]
     cost = 2 * count * probe_dev * TILE * TILE
-    tiles = pltpu.with_memory_space_constraint(tiles, HBM)
+    tiles, tile_rows, tile_firms = (
+        pltpu.with_memory_space_constraint(array, HBM) for array in (tiles, tile_rows, tile_firms)
+    )
 
     def shape(*dims):
         return jax.ShapeDtypeStruct(dims, f32)
@@ -332,15 +345,18 @@
 
     parts = kernel(
         bind(start_body), shape(workers * firms, probe_dev, TILE),
-        [SMEM, SMEM, SMEM, VMEM, HBM], scratch, "start", cost,
-    )(tile_rows, tile_firms, words, worker_ids, tiles)
+        [HBM] * 5, [*scratch, SMEM(words.shape, jnp.int32), VMEM(worker_ids.shape, jnp.int32)], "start", cost,
+    )(
+        tile_rows, tile_firms, pltpu.with_memory_space_constraint(words, HBM),
+        pltpu.with_memory_space_constraint(worker_ids, HBM), tiles,
+    )
     first, at = owner_total(parts, at)
 
     field, (first, *at) = collect(first, (first, *at))
     firm, worker, _ = at
     parts = kernel(
         bind(middle_body), shape(workers * (firms + 1), probe_dev, TILE),
-        [SMEM, SMEM, SMEM, SMEM, VMEM, VMEM, VMEM, VMEM, HBM], scratch, "middle", 2 * cost,
+        [HBM, HBM, SMEM, SMEM, VMEM, VMEM, VMEM, VMEM, HBM], scratch, "middle", 2 * cost,
     )(tile_rows, tile_firms, worker, firm, field, first, reg_blocks, worker_ids, tiles)
     got, (first, *at) = owner_total(parts, (first, *at))
     quotient = got[probe_dev:, :1] / got[probe_dev:, TILE // 2 : TILE // 2 + 1]
@@ -350,13 +366,13 @@
     field, (first, second, quotient, *at) = collect(second, (first, second, quotient, *at))
     sent = kernel(
         bind(rows_body), shape(probes, 3 + ROWB_DEV, probe_dev, TILE),
-        [SMEM, SMEM, VMEM, VMEM, VMEM, VMEM, VMEM, HBM], scratch, "rows", cost,
+        [HBM, HBM, VMEM, VMEM, VMEM, VMEM, VMEM, HBM], scratch, "rows", cost,
     )(tile_rows, tile_firms, field, first, second, quotient, worker_ids, tiles)
     given, at = exchange(sent, "probe", at)
     firm, worker, probe = at
     parts = kernel(
         bind(last_body), shape(workers * (firms + 1), probe_dev, TILE),
-        [SMEM, SMEM, SMEM, SMEM, SMEM, VMEM, VMEM, HBM], scratch, "last", cost,
+        [HBM, HBM, SMEM, SMEM, SMEM, VMEM, VMEM, HBM], scratch, "last", cost,
     )(tile_rows, tile_firms, worker, firm, probe, given, reg_blocks, tiles)
     got, (given, *at) = owner_total(parts, (given, *at))
     sent = copies(got.reshape(2, probe_dev, TILE), probes)

time: 207 us -> 201 us (0.971)
  Pallas kernels: 20.8 us -> 17.5 us
  local copies, waits for them, and re-layouts: 3.57 us -> 0.82 us
    unnamed x16 -> x4, local copies, waits for them, and re-layouts: 2.75 us -> 0.01 us
    pallas_call x3, Pallas kernels: 11.1 us -> 8.55 us  [the longest x1 3.18 us: local(): kernel(bind(rows_body), shape(probes, 3 + ROWB_DEV, probe_dev, TILE), [HB...]
where the time goes in v4:
time: 201 us
  blocking collectives  181 us (90%)
  Pallas kernels  17.5 us (9%)
    all_to_all x13, blocking collectives, exchange(): got = lax.all_to_all(chunks, axis, 0, 0, tiled=True)  181 us
    pallas_call x1, Pallas kernels, local(): kernel(final_body, shape(workers, 2, probe_dev, TILE), [SMEM, VMEM, VMEM]...  5 us

profile of v4, /device:TPU:1, one launch (start us, length us, event | category | flops | bytes accessed | tf_op | source)
XLA Modules:
  0.0 200.7 jit_solution(7057255318651667297)
XLA Ops:
  0.6 0.0 copy-start
  0.6 0.0 copy-start.1
  0.7 2.7 %start.1 = f32[128,8,128]{2,1,0:T(8,128)S(1)} custom-call(s32[1,128]{1,0:T(1,128)} %refs_0_.7, s32[1,128]{1,0:T(1,128)} %refs_1_.7, s32[5,4,8]{2,1,0:T(4,128)} %bitcast.31, s32[1,512]{1,0:T(1,128)} %refs_6_.1, bf16[128,128,128]{2,1,0:T(8,128)(2,1)} %refs_7_.5), custom_call_target="tpu_custom_call" | custom-call | flops 33554432 | bytes 4194304 | tf_op jit(solution)/shard_map/start/pallas_call | solution.py:346
  3.4 18.6 %all_to_all.65 = f32[8,128,128]{2,1,0:T(8,128)S(1)} all-to-all(f32[8,128,128]{2,1,0:T(8,128)S(1)} %bitcast.23), channel_id=1, replica_groups=mesh['firm'=16,'worker'=8,'probe'=4] {'worker'}, dimensions={0} | all-to-all | bytes 1048576 | tf_op jit(solution)/shard_map/all_to_all | solution.py:296
  22.0 22.8 %all_to_all.66 = f32[16,8,128]{2,1,0:T(8,128)S(1)} all-to-all(f32[16,8,128]{2,1,0:T(8,128)S(1)} %bitcast.29), channel_id=1, replica_groups=mesh['firm'=16,'worker'=8,'probe'=4] {'firm'}, dimensions={0} | all-to-all | bytes 131072 | tf_op jit(solution)/shard_map/all_to_all | solution.py:296
  44.8 14.3 %all_to_all.67 = bf16[16,8,128]{2,1,0:T(8,128)(2,1)S(1)} all-to-all(bf16[16,8,128]{2,1,0:T(8,128)(2,1)S(1)} %broadcast_in_dim.20), channel_id=1, replica_groups=mesh['firm'=16,'worker'=8,'probe'=4] {'firm'}, dimensions={0} | all-to-all | bytes 65536 | tf_op jit(solution)/shard_map/all_to_all | solution.py:296
  59.1 12.5 %all_to_all.68 = bf16[8,16,8,128]{3,2,1,0:T(8,128)(2,1)S(1)} all-to-all(bf16[8,16,8,128]{3,2,1,0:T(8,128)(2,1)S(1)} %broadcast_in_dim.21), channel_id=1, replica_groups=mesh['firm'=16,'worker'=8,'probe'=4] {'worker'}, dimensions={0} | all-to-all | bytes 524288 | tf_op jit(solution)/shard_map/all_to_all | solution.py:296
  71.6 0.0 copy-done
  71.6 0.0 copy-done.1
  71.6 3.9 %middle.1 = f32[136,8,128]{2,1,0:T(8,128)S(1)} custom-call(s32[1,128]{1,0:T(1,128)} %refs_0_.7, s32[1,128]{1,0:T(1,128)} %refs_1_.7, s32[1]{0:T(128)} %bitcast.3.refs_2_, s32[1]{0:T(128)} %bitcast.2.refs_3_, bf16[128,8,128]{2,1,0:T(8,128)(2,1)S(1)} %bitcast.24, f32[8,128]{1,0:T(8,128)S(1)} %reduce_sum.55.refs_5_.refs_3_, f32[8,128]{1,0:T(8,128)S(1)} %bitcast.26, ...), custom_call_target="tpu_custom_call" | custom-call | flops 67108864 | bytes 4194304 | tf_op jit(solution)/shard_map/middle/pallas_call | solution.py:357
  75.6 13.6 %all_to_all.69 = f32[8,136,128]{2,1,0:T(8,128)S(1)} all-to-all(f32[8,136,128]{2,1,0:T(8,128)S(1)} %bitcast.22), channel_id=1, replica_groups=mesh['firm'=16,'worker'=8,'probe'=4] {'worker'}, dimensions={0} | all-to-all | bytes 1114112 | tf_op jit(solution)/shard_map/all_to_all | solution.py:296
  89.2 14.7 %all_to_all.70 = f32[16,16,128]{2,1,0:T(8,128)S(1)} all-to-all(f32[16,16,128]{2,1,0:T(8,128)S(1)} %pad_maximum_fusion), channel_id=1, replica_groups=mesh['firm'=16,'worker'=8,'probe'=4] {'firm'}, dimensions={0} | all-to-all | bytes 262144 | tf_op jit(solution)/shard_map/all_to_all | solution.py:296
  103.9 0.2 fusion.1
  104.1 0.1 fusion.2
  104.2 0.1 broadcast_in_dim.24.refs_5_
  104.3 17.6 %all_to_all.71 = bf16[16,8,128]{2,1,0:T(8,128)(2,1)S(1)} all-to-all(bf16[16,8,128]{2,1,0:T(8,128)(2,1)S(1)} %broadcast_in_dim.25), channel_id=1, replica_groups=mesh['firm'=16,'worker'=8,'probe'=4] {'firm'}, dimensions={0} | all-to-all | bytes 65536 | tf_op jit(solution)/shard_map/all_to_all | solution.py:296
  121.9 11.0 %all_to_all.72 = bf16[8,16,8,128]{3,2,1,0:T(8,128)(2,1)S(1)} all-to-all(bf16[8,16,8,128]{3,2,1,0:T(8,128)(2,1)S(1)} %broadcast_in_dim.26), channel_id=1, replica_groups=mesh['firm'=16,'worker'=8,'probe'=4] {'worker'}, dimensions={0} | all-to-all | bytes 524288 | tf_op jit(solution)/shard_map/all_to_all | solution.py:296
  132.9 3.2 %rows.1 = f32[4,7,8,128]{3,2,1,0:T(8,128)S(1)} custom-call(s32[1,128]{1,0:T(1,128)} %refs_0_.7, s32[1,128]{1,0:T(1,128)} %refs_1_.7, bf16[128,8,128]{2,1,0:T(8,128)(2,1)S(1)} %bitcast.25, f32[8,128]{1,0:T(8,128)S(1)} %reduce_sum.55.refs_5_.refs_3_, f32[8,128]{1,0:T(8,128)S(1)} %get-tuple-element.191.refs_4_, f32[8,128]{1,0:T(8,128)S(1)} %broadcast_in_dim.24.refs_5_, ...), custom_call_target="tpu_custom_call" | custom-call | flops 33554432 | bytes 4194304 | tf_op jit(solution)/shard_map/rows/pallas_call | solution.py:367
  136.1 8.6 %all_to_all.73.refs_5_.given = f32[4,7,8,128]{3,2,1,0:T(8,128)S(1)} all-to-all(f32[4,7,8,128]{3,2,1,0:T(8,128)S(1)} %rows.1), channel_id=1, replica_groups=mesh['firm'=16,'worker'=8,'probe'=4] {'probe'}, dimensions={0} | all-to-all | bytes 229376 | tf_op jit(solution)/shard_map/all_to_all | solution.py:296
  144.6 2.7 %last.1 = f32[136,8,128]{2,1,0:T(8,128)S(1)} custom-call(s32[1,128]{1,0:T(1,128)} %refs_0_.7, s32[1,128]{1,0:T(1,128)} %refs_1_.7, s32[1]{0:T(128)} %bitcast.3.refs_2_, s32[1]{0:T(128)} %bitcast.2.refs_3_, s32[1]{0:T(128)} %bitcast.4.refs_4_.probe, f32[4,7,8,128]{3,2,1,0:T(8,128)S(1)} %all_to_all.73.refs_5_.given, f32[8,128]{1,0:T(8,128)S(1)} %bitcast.27, ...), custom_call_target="tpu_custom_call" | custom-call | flops 33554432 | bytes 4194304 | tf_op jit(solution)/shard_map/last/pallas_call | solution.py:373
  147.3 15.0 %all_to_all.74 = f32[8,136,128]{2,1,0:T(8,128)S(1)} all-to-all(f32[8,136,128]{2,1,0:T(8,128)S(1)} %bitcast.21), channel_id=1, replica_groups=mesh['firm'=16,'worker'=8,'probe'=4] {'worker'}, dimensions={0} | all-to-all | bytes 1114112 | tf_op jit(solution)/shard_map/all_to_all | solution.py:296
  162.4 14.7 %all_to_all.75 = f32[16,16,128]{2,1,0:T(8,128)S(1)} all-to-all(f32[16,16,128]{2,1,0:T(8,128)S(1)} %pad_maximum_fusion.1), channel_id=1, replica_groups=mesh['firm'=16,'worker'=8,'probe'=4] {'firm'}, dimensions={0} | all-to-all | bytes 262144 | tf_op jit(solution)/shard_map/all_to_all | solution.py:296
  177.1 6.7 %all_to_all.76.last = f32[4,2,8,128]{3,2,1,0:T(8,128)S(1)} all-to-all(f32[4,2,8,128]{3,2,1,0:T(8,128)S(1)} %broadcast_in_dim.29), channel_id=1, replica_groups=mesh['firm'=16,'worker'=8,'probe'=4] {'probe'}, dimensions={0} | all-to-all | bytes 65536 | tf_op jit(solution)/shard_map/all_to_all | solution.py:296
  183.8 5.0 %final.1 = f32[8,2,8,128]{3,2,1,0:T(8,128)S(1)} custom-call(s32[1]{0:T(128)} %bitcast.4.refs_4_.probe, f32[4,7,8,128]{3,2,1,0:T(8,128)S(1)} %all_to_all.73.refs_5_.given, f32[4,2,8,128]{3,2,1,0:T(8,128)S(1)} %all_to_all.76.last), custom_call_target="tpu_custom_call" | custom-call | flops 8388608 | bytes 4194304 | tf_op jit(solution)/shard_map/final/pallas_call | solution.py:380
  188.8 11.2 %all_to_all.77 = f32[8,2,8,128]{3,2,1,0:T(8,128)S(1)} all-to-all(f32[8,2,8,128]{3,2,1,0:T(8,128)S(1)} %final.1), channel_id=1, replica_groups=mesh['firm'=16,'worker'=8,'probe'=4] {'worker'}, dimensions={0} | all-to-all | bytes 131072 | tf_op jit(solution)/shard_map/all_to_all | solution.py:296
  200.0 0.6 slice_bitcast_fusion.2
  (20 shorter events, 0.3 us)
Async XLA Ops:
  0.6 71.0 %copy-start = (s32[1,512]{1,0:T(1,128)S(1)}, s32[1,512]{1,0:T(1,128)}, u32[]{:S(2)}) copy-start(s32[1,512]{1,0:T(1,128)} %refs_6_.1) | copy-start | bytes 6148
  0.6 71.0 %copy-start.1 = (f32[1024]{0:T(1024)S(1)}, f32[1024]{0:T(1024)}, u32[]{:S(2)}) copy-start(f32[1024]{0:T(1024)} %param.11) | copy-start | bytes 12292

commit v5 on v4

--- a/solution.py
+++ b/solution.py
@@ -50,14 +50,12 @@
 
 def fetch(tiles_hbm, tiles, arrived, small):
     size = tiles.shape[0] // CHUNKS
-    tables = [pltpu.make_async_copy(*both, arrived.at[CHUNKS + item]) for item, both in enumerate(small)]
-    for table in tables:
-        table.start()
 
     def copy(chunk):
         part = pl.ds(chunk * size, size)
         return pltpu.make_async_copy(tiles_hbm.at[part], tiles.at[part], arrived.at[chunk])
 
+    tables = fetch_small(arrived, small)
     for chunk in range(CHUNKS):
         copy(chunk).start()
     for table in tables:
@@ -65,6 +63,13 @@
     return lambda chunk: copy(chunk).wait()
 
 
+def fetch_small(arrived, small):
+    tables = [pltpu.make_async_copy(*both, arrived.at[CHUNKS + item]) for item, both in enumerate(small)]
+    for table in tables:
+        table.start()
+    return tables
+
+
 def place_of(firm, workers, stride):
     return (firm & (workers - 1)) * stride + (firm >> (workers.bit_length() - 1))
 
@@ -73,12 +78,9 @@
     return jnp.concatenate([upper.astype(f32), lower.astype(f32)], axis=0).astype(bf16)
 
 
-def forward(tile_rows, tile_firms, field, tiles, workers, firms, wait):
+def forward(tile_rows, tile_firms, field, tiles, workers, firms):
     total = None
-    size = tiles.shape[0] // CHUNKS
     for tile in range(0, tiles.shape[0], 2):
-        if tile % size == 0:
-            wait(tile // size)
         pieces = [field[place_of(tile_firms[0, tile + item], workers, firms)] for item in range(2)]
         probes = pieces[0].shape[0]
         weights = jnp.concatenate([tiles[tile], tiles[tile + 1]], axis=0)
@@ -140,11 +142,9 @@
 
 
 def middle_body(
-    workers, firms, rows_hbm, firms_hbm, worker, firm, field, first, regular, worker_ids, tiles_hbm,
-    out, tiles, rows, arrived, tile_rows, tile_firms,
+    workers, firms, tile_rows, tile_firms, worker, firm, field, first, regular, worker_ids, tiles, out, rows
 ):
-    wait = fetch(tiles_hbm, tiles, arrived, [(rows_hbm, tile_rows), (firms_hbm, tile_firms)])
-    total = forward(tile_rows, tile_firms, field, tiles, workers, firms, wait)
+    total = forward(tile_rows, tile_firms, field, tiles, workers, firms)
     values = demean(jnp.concatenate(total, axis=1), worker_ids[...])
     put_rows(rows, values)
     adjoint(tile_rows, tile_firms, rows, tiles, out, workers, firms + 1)
@@ -160,12 +160,8 @@
         out[other * (firms + 1) + firms] = extra
 
 
-def rows_body(
-    workers, firms, rows_hbm, firms_hbm, field, first, second, quotient, worker_ids, tiles_hbm,
-    out, tiles, rows, arrived, tile_rows, tile_firms,
-):
-    wait = fetch(tiles_hbm, tiles, arrived, [(rows_hbm, tile_rows), (firms_hbm, tile_firms)])
-    total = forward(tile_rows, tile_firms, field, tiles, workers, firms, wait)
+def rows_body(workers, firms, tile_rows, tile_firms, field, first, second, quotient, worker_ids, tiles, out):
+    total = forward(tile_rows, tile_firms, field, tiles, workers, firms)
     values = demean(jnp.concatenate(total, axis=1), worker_ids[...])
     for probe in range(out.shape[0]):
         out[probe, 0] = first[...]
@@ -176,10 +172,8 @@
 
 
 def last_body(
-    workers, firms, rows_hbm, firms_hbm, worker, firm, probe, given, regular, tiles_hbm,
-    out, tiles, rows, arrived, tile_rows, tile_firms,
+    workers, firms, tile_rows, tile_firms, worker, firm, probe, given, regular, tiles, out, rows
 ):
-    wait = fetch(tiles_hbm, tiles, arrived, [(rows_hbm, tile_rows), (firms_hbm, tile_firms)])
     gather = lambda item: jnp.concatenate([given[other, item] for other in range(given.shape[0])], axis=0)
     own = lambda item: given[probe[0], item]
     first, second = own(0), own(1)
@@ -198,7 +192,7 @@
         ],
         axis=1,
     )
-    adjoint(tile_rows, tile_firms, rows, tiles, out, workers, firms + 1, wait)
+    adjoint(tile_rows, tile_firms, rows, tiles, out, workers, firms + 1)
     add_ridge(out, worker[0] * (firms + 1) + firm[0], regular, worker[0], second)
     for other in range(workers):
         out[other * (firms + 1) + firms] = extra
@@ -278,15 +272,63 @@
         out[worker, 1] = scratch[1, pl.ds(begin, probes), :]
 
 
-def kernel(body, shapes, places, scratch, name, cost):
+def fold_body(got, out):
+    total = got[0]
+    for other in range(1, got.shape[0]):
+        total = total + got[other]
+    firms, lines = out.shape[0], out.shape[1]
+    extra = lines * firms - total.shape[0]
+    extra = extra // (firms - 1)
+    probes = lines - extra
+    for firm in range(firms):
+        out[firm, :probes, :] = total[firm * probes : (firm + 1) * probes]
+        if extra:
+            out[firm, probes:, :] = total[firms * probes :]
+
+
+def sum_of(got):
+    total = got[0]
+    for other in range(1, got.shape[0]):
+        total = total + got[other]
+    return total
+
+
+def send(out, values):
+    for other in range(out.shape[0]):
+        out[other] = values.astype(out.dtype)
+
+
+def first_body(got, first, sent):
+    first[...] = sum_of(got)
+    send(sent, first[...])
+
+
+def second_body(got, first, second, quotient, sent):
+    total = sum_of(got)
+    probes = first.shape[0]
+    ratio = total[probes:, :1] / total[probes:, TILE // 2 : TILE // 2 + 1]
+    quotient[...] = jnp.broadcast_to(ratio, quotient.shape)
+    second[...] = first[...] - total[:probes] / quotient[...]
+    send(sent, second[...])
+
+
+def send_body(values, sent):
+    send(sent, values[...])
+
+
+def third_body(got, sent):
+    send(sent, sum_of(got))
+
+
+def kernel(body, shapes, places, scratch, name, cost=1 << 16):
     return pl.pallas_call(
         body,
         out_shape=shapes,
         in_specs=[pl.BlockSpec(memory_space=place) for place in places],
         out_specs=jax.tree.map(lambda _: pl.BlockSpec(memory_space=pltpu.VMEM), shapes),
         scratch_shapes=scratch,
-        compiler_params=pltpu.CompilerParams(vmem_limit_bytes=10 << 20),
-        cost_estimate=pl.CostEstimate(flops=cost, transcendentals=0, bytes_accessed=1 << 22),
+        compiler_params=pltpu.CompilerParams(vmem_limit_bytes=6 << 20),
+        cost_estimate=pl.CostEstimate(flops=cost, transcendentals=0, bytes_accessed=1 << 20),
         name=name,
     )
 
@@ -295,10 +337,6 @@
     chunks, beside = lax.optimization_barrier((chunks, beside))
     got = lax.all_to_all(chunks, axis, 0, 0, tiled=True)
     return lax.optimization_barrier((got, beside))
-
-
-def copies(rows, size):
-    return jnp.broadcast_to(rows[None], (size,) + rows.shape)
 
 
 def local(tiles, tile_rows, tile_firms, worker_ids, sign_words, regular):
@@ -312,75 +350,72 @@
     at = tuple(lax.axis_index(axis).reshape(1) for axis in ("firm", "worker", "probe"))
 
     VMEM, SMEM, HBM = pltpu.VMEM, pltpu.SMEM, pltpu.HBM
-    scratch = [
-        VMEM(tiles.shape, bf16), VMEM((ROWB_DEV, probe_dev, TILE), f32), pltpu.SemaphoreType.DMA((CHUNKS + 4,)),
-        SMEM(tile_rows.shape, jnp.int32), SMEM(tile_firms.shape, jnp.int32),
-    ]
+    rows_vmem = VMEM((ROWB_DEV, probe_dev, TILE), f32)
     cost = 2 * count * probe_dev * TILE * TILE
-    tiles, tile_rows, tile_firms = (
-        pltpu.with_memory_space_constraint(array, HBM) for array in (tiles, tile_rows, tile_firms)
-    )
-
-    def shape(*dims):
-        return jax.ShapeDtypeStruct(dims, f32)
-
-    def owner_total(parts, beside):
+
+    def shape(*dims, dtype=f32):
+        return jax.ShapeDtypeStruct(dims, dtype)
+
+    def placed(array, where):
+        return pltpu.with_memory_space_constraint(array, where)
+
+    def owner_parts(parts, beside):
         chunk = parts.reshape(workers, -1, TILE)
         got, beside = exchange(chunk, "worker", beside)
-        got = jnp.sum(got, axis=0)
-        kept = firms * probe_dev
-        chunk = got[:kept].reshape(firms, probe_dev, TILE)
-        if got.shape[0] > kept:
-            chunk = jnp.concatenate([chunk, copies(got[kept:], firms)], axis=1)
-        got, beside = exchange(chunk, "firm", beside)
-        return jnp.sum(got, axis=0), beside
-
-    def collect(own, beside):
-        column, beside = exchange(copies(own.astype(bf16), firms), "firm", beside)
-        field, beside = exchange(copies(column, workers), "worker", beside)
+        extra = chunk.shape[1] - firms * probe_dev
+        chunk = kernel(fold_body, shape(firms, probe_dev + extra, TILE), [VMEM], [], "fold")(got)
+        return exchange(chunk, "firm", beside)
+
+    def collect(sent, beside):
+        column, beside = exchange(sent, "firm", beside)
+        dims = (workers, firms, probe_dev, TILE)
+        sent = kernel(send_body, shape(*dims, dtype=bf16), [VMEM], [], "spread")(column)
+        field, beside = exchange(sent, "worker", beside)
         return field.reshape(workers * firms, probe_dev, TILE), beside
 
     def bind(body):
         return lambda *refs: body(workers, firms, *refs)
 
-    parts = kernel(
-        bind(start_body), shape(workers * firms, probe_dev, TILE),
-        [HBM] * 5, [*scratch, SMEM(words.shape, jnp.int32), VMEM(worker_ids.shape, jnp.int32)], "start", cost,
-    )(
-        tile_rows, tile_firms, pltpu.with_memory_space_constraint(words, HBM),
-        pltpu.with_memory_space_constraint(worker_ids, HBM), tiles,
-    )
-    first, at = owner_total(parts, at)
-
-    field, (first, *at) = collect(first, (first, *at))
+    own = shape(probe_dev, TILE)
+    sent_own = shape(firms, probe_dev, TILE, dtype=bf16)
+    parts, tiles = kernel(
+        bind(start_body), (shape(workers * firms, probe_dev, TILE), VMEM(tiles.shape, bf16)), [HBM] * 5,
+        [
+            rows_vmem, pltpu.SemaphoreType.DMA((CHUNKS + 4,)), SMEM(tile_rows.shape, jnp.int32),
+            SMEM(tile_firms.shape, jnp.int32), SMEM(words.shape, jnp.int32), VMEM(worker_ids.shape, jnp.int32),
+        ],
+        "start", cost,
+    )(*(placed(array, HBM) for array in (tile_rows, tile_firms, words, worker_ids, tiles)))
+    got, at = owner_parts(parts, at)
+    first, sent = kernel(first_body, (own, sent_own), [VMEM], [], "first")(got)
+
+    field, (first, *at) = collect(sent, (first, *at))
     firm, worker, _ = at
     parts = kernel(
         bind(middle_body), shape(workers * (firms + 1), probe_dev, TILE),
-        [HBM, HBM, SMEM, SMEM, VMEM, VMEM, VMEM, VMEM, HBM], scratch, "middle", 2 * cost,
-    )(tile_rows, tile_firms, worker, firm, field, first, reg_blocks, worker_ids, tiles)
-    got, (first, *at) = owner_total(parts, (first, *at))
-    quotient = got[probe_dev:, :1] / got[probe_dev:, TILE // 2 : TILE // 2 + 1]
-    quotient = jnp.broadcast_to(quotient, first.shape)
-    second = first - got[:probe_dev] / quotient
-
-    field, (first, second, quotient, *at) = collect(second, (first, second, quotient, *at))
+        [SMEM, SMEM, SMEM, SMEM, VMEM, VMEM, VMEM, VMEM, VMEM], [rows_vmem], "middle", 2 * cost,
+    )(tile_rows, tile_firms, worker, firm, field, first, reg_blocks, worker_ids, placed(tiles, VMEM))
+    got, (first, *at) = owner_parts(parts, (first, *at))
+    second, quotient, sent = kernel(second_body, (own, own, sent_own), [VMEM, VMEM], [], "second")(got, first)
+
+    field, (first, second, quotient, *at) = collect(sent, (first, second, quotient, *at))
     sent = kernel(
         bind(rows_body), shape(probes, 3 + ROWB_DEV, probe_dev, TILE),
-        [HBM, HBM, VMEM, VMEM, VMEM, VMEM, VMEM, HBM], scratch, "rows", cost,
-    )(tile_rows, tile_firms, field, first, second, quotient, worker_ids, tiles)
+        [SMEM, SMEM, VMEM, VMEM, VMEM, VMEM, VMEM, VMEM], [], "rows", cost,
+    )(tile_rows, tile_firms, field, first, second, quotient, worker_ids, placed(tiles, VMEM))
     given, at = exchange(sent, "probe", at)
     firm, worker, probe = at
     parts = kernel(
         bind(last_body), shape(workers * (firms + 1), probe_dev, TILE),
-        [HBM, HBM, SMEM, SMEM, SMEM, VMEM, VMEM, HBM], scratch, "last", cost,
-    )(tile_rows, tile_firms, worker, firm, probe, given, reg_blocks, tiles)
-    got, (given, *at) = owner_total(parts, (given, *at))
-    sent = copies(got.reshape(2, probe_dev, TILE), probes)
+        [SMEM, SMEM, SMEM, SMEM, SMEM, VMEM, VMEM, VMEM], [rows_vmem], "last", cost,
+    )(tile_rows, tile_firms, worker, firm, probe, given, reg_blocks, placed(tiles, VMEM))
+    got, (given, *at) = owner_parts(parts, (given, *at))
+    sent = kernel(third_body, shape(probes, 2 * probe_dev, TILE), [VMEM], [], "third")(got)
     last, (given, *at) = exchange(sent, "probe", (given, *at))
     outs = kernel(
         final_body, shape(workers, 2, probe_dev, TILE), [SMEM, VMEM, VMEM],
         [VMEM((2, probes * probe_dev, TILE), f32)], "final", cost // 4,
-    )(at[2], given, last)
+    )(at[2], given, last.reshape(probes, 2, probe_dev, TILE))
     outs, _ = exchange(outs, "worker")
     outs = jnp.transpose(outs, (1, 2, 0, 3)).reshape(2, probe_dev, workers * TILE)
     return (outs[0], outs[1])

time: 201 us -> 197 us (0.980)
  Pallas kernels: 17.5 us -> 14.4 us
    pallas_call x3 -> x11, Pallas kernels: 8.55 us -> 6.59 us  [the longest x1 2.7 us: local(): kernel(bind(start_body), (shape(workers * firms, probe_dev, TILE), VMEM(t...]
where the time goes in v5:
time: 197 us
  blocking collectives  181 us (92%)
  Pallas kernels  14.4 us (7%)
    all_to_all x13, blocking collectives, exchange(): got = lax.all_to_all(chunks, axis, 0, 0, tiled=True)  181 us
    pallas_call x1, Pallas kernels, local(): kernel(final_body, shape(workers, 2, probe_dev, TILE), [SMEM, VMEM, VMEM]...  5 us

profile of v5, /device:TPU:1, one launch (start us, length us, event | category | flops | bytes accessed | tf_op | source)
XLA Modules:
  0.0 196.9 jit_solution(14577319878117782985)
XLA Ops:
  0.6 0.0 copy-start.3
  0.6 0.0 copy-start.2
  0.7 0.0 copy-start
  0.7 0.0 copy-start.1
  0.7 2.7 %start.1 = (f32[128,8,128]{2,1,0:T(8,128)S(1)}, bf16[128,128,128]{2,1,0:T(8,128)(2,1)S(1)}) custom-call(s32[1,128]{1,0:T(1,128)} %refs_0_.7, s32[1,128]{1,0:T(1,128)} %refs_1_.7, s32[5,4,8]{2,1,0:T(4,128)} %bitcast.25, s32[1,512]{1,0:T(1,128)} %refs_6_.1, bf16[128,128,128]{2,1,0:T(8,128)(2,1)} %refs_4_.1), custom_call_target="tpu_custom_call" | custom-call | flops 33554432 | bytes 1048576 | tf_op jit(solution)/shard_map/start/pallas_call | solution.py:381
  3.4 18.6 %all_to_all.65.got = f32[8,128,128]{2,1,0:T(8,128)S(1)} all-to-all(f32[8,128,128]{2,1,0:T(8,128)S(1)} %bitcast.20), channel_id=1, replica_groups=mesh['firm'=16,'worker'=8,'probe'=4] {'worker'}, dimensions={0} | all-to-all | bytes 1048576 | tf_op jit(solution)/shard_map/all_to_all | solution.py:338
  22.0 22.8 %all_to_all.66.got = f32[16,8,128]{2,1,0:T(8,128)S(1)} all-to-all(f32[16,8,128]{2,1,0:T(8,128)S(1)} %fold.3), channel_id=1, replica_groups=mesh['firm'=16,'worker'=8,'probe'=4] {'firm'}, dimensions={0} | all-to-all | bytes 131072 | tf_op jit(solution)/shard_map/all_to_all | solution.py:338
  44.8 14.3 %all_to_all.67.values = bf16[16,8,128]{2,1,0:T(8,128)(2,1)S(1)} all-to-all(bf16[16,8,128]{2,1,0:T(8,128)(2,1)S(1)} %get-tuple-element.138), channel_id=1, replica_groups=mesh['firm'=16,'worker'=8,'probe'=4] {'firm'}, dimensions={0} | all-to-all | bytes 65536 | tf_op jit(solution)/shard_map/all_to_all | solution.py:338
  59.1 12.5 %all_to_all.68 = bf16[8,16,8,128]{3,2,1,0:T(8,128)(2,1)S(1)} all-to-all(bf16[8,16,8,128]{3,2,1,0:T(8,128)(2,1)S(1)} %spread.2), channel_id=1, replica_groups=mesh['firm'=16,'worker'=8,'probe'=4] {'worker'}, dimensions={0} | all-to-all | bytes 524288 | tf_op jit(solution)/shard_map/all_to_all | solution.py:338
  71.6 0.0 copy-done.3
  71.6 0.0 copy-done.2
  71.6 0.0 copy-done
  71.6 0.0 copy-done.1
  71.6 2.8 %middle.1 = f32[136,8,128]{2,1,0:T(8,128)S(1)} custom-call(s32[1,128]{1,0:T(1,128)S(1)} %copy-done.2, s32[1,128]{1,0:T(1,128)S(1)} %copy-done.3, s32[1]{0:T(128)} %bitcast.3.refs_2_, s32[1]{0:T(128)} %bitcast.2.refs_3_, bf16[128,8,128]{2,1,0:T(8,128)(2,1)S(1)} %bitcast.18, f32[8,128]{1,0:T(8,128)S(1)} %get-tuple-element.204.refs_5_.first.refs_3_, ...), custom_call_target="tpu_custom_call" | custom-call | flops 67108864 | bytes 1048576 | tf_op jit(solution)/shard_map/middle/pallas_call | solution.py:394
  74.5 13.6 %all_to_all.69.got = f32[8,136,128]{2,1,0:T(8,128)S(1)} all-to-all(f32[8,136,128]{2,1,0:T(8,128)S(1)} %bitcast.17), channel_id=1, replica_groups=mesh['firm'=16,'worker'=8,'probe'=4] {'worker'}, dimensions={0} | all-to-all | bytes 1114112 | tf_op jit(solution)/shard_map/all_to_all | solution.py:338
  88.1 14.7 %all_to_all.70.got = f32[16,16,128]{2,1,0:T(8,128)S(1)} all-to-all(f32[16,16,128]{2,1,0:T(8,128)S(1)} %fold.4), channel_id=1, replica_groups=mesh['firm'=16,'worker'=8,'probe'=4] {'firm'}, dimensions={0} | all-to-all | bytes 262144 | tf_op jit(solution)/shard_map/all_to_all | solution.py:338
  102.8 0.2 second.1
  102.9 17.6 %all_to_all.71.values = bf16[16,8,128]{2,1,0:T(8,128)(2,1)S(1)} all-to-all(bf16[16,8,128]{2,1,0:T(8,128)(2,1)S(1)} %get-tuple-element.182), channel_id=1, replica_groups=mesh['firm'=16,'worker'=8,'probe'=4] {'firm'}, dimensions={0} | all-to-all | bytes 65536 | tf_op jit(solution)/shard_map/all_to_all | solution.py:338
  120.6 11.0 %all_to_all.72 = bf16[8,16,8,128]{3,2,1,0:T(8,128)(2,1)S(1)} all-to-all(bf16[8,16,8,128]{3,2,1,0:T(8,128)(2,1)S(1)} %spread.3), channel_id=1, replica_groups=mesh['firm'=16,'worker'=8,'probe'=4] {'worker'}, dimensions={0} | all-to-all | bytes 524288 | tf_op jit(solution)/shard_map/all_to_all | solution.py:338
  131.6 2.0 %rows.1 = f32[4,7,8,128]{3,2,1,0:T(8,128)S(1)} custom-call(s32[1,128]{1,0:T(1,128)S(1)} %copy-done.2, s32[1,128]{1,0:T(1,128)S(1)} %copy-done.3, bf16[128,8,128]{2,1,0:T(8,128)(2,1)S(1)} %bitcast.19, f32[8,128]{1,0:T(8,128)S(1)} %get-tuple-element.204.refs_5_.first.refs_3_, f32[8,128]{1,0:T(8,128)S(1)} %get-tuple-element.205.refs_4_, ...), custom_call_target="tpu_custom_call" | custom-call | flops 33554432 | bytes 1048576 | tf_op jit(solution)/shard_map/rows/pallas_call | solution.py:402
  133.6 8.6 %all_to_all.73.refs_5_.given = f32[4,7,8,128]{3,2,1,0:T(8,128)S(1)} all-to-all(f32[4,7,8,128]{3,2,1,0:T(8,128)S(1)} %rows.1), channel_id=1, replica_groups=mesh['firm'=16,'worker'=8,'probe'=4] {'probe'}, dimensions={0} | all-to-all | bytes 229376 | tf_op jit(solution)/shard_map/all_to_all | solution.py:338
  142.2 1.5 last.1
  143.7 15.0 %all_to_all.74.got = f32[8,136,128]{2,1,0:T(8,128)S(1)} all-to-all(f32[8,136,128]{2,1,0:T(8,128)S(1)} %bitcast.16), channel_id=1, replica_groups=mesh['firm'=16,'worker'=8,'probe'=4] {'worker'}, dimensions={0} | all-to-all | bytes 1114112 | tf_op jit(solution)/shard_map/all_to_all | solution.py:338
  158.7 14.7 %all_to_all.75.got = f32[16,16,128]{2,1,0:T(8,128)S(1)} all-to-all(f32[16,16,128]{2,1,0:T(8,128)S(1)} %fold.5), channel_id=1, replica_groups=mesh['firm'=16,'worker'=8,'probe'=4] {'firm'}, dimensions={0} | all-to-all | bytes 262144 | tf_op jit(solution)/shard_map/all_to_all | solution.py:338
  173.4 6.7 %all_to_all.76 = f32[4,16,128]{2,1,0:T(8,128)S(1)} all-to-all(f32[4,16,128]{2,1,0:T(8,128)S(1)} %third.1), channel_id=1, replica_groups=mesh['firm'=16,'worker'=8,'probe'=4] {'probe'}, dimensions={0} | all-to-all | bytes 65536 | tf_op jit(solution)/shard_map/all_to_all | solution.py:338
  180.0 5.0 %final.1 = f32[8,2,8,128]{3,2,1,0:T(8,128)S(1)} custom-call(s32[1]{0:T(128)} %bitcast.4.refs_4_.probe, f32[4,7,8,128]{3,2,1,0:T(8,128)S(1)} %all_to_all.73.refs_5_.given, f32[4,2,8,128]{3,2,1,0:T(8,128)S(1)} %bitcast.21), custom_call_target="tpu_custom_call" | custom-call | flops 8388608 | bytes 1048576 | tf_op jit(solution)/shard_map/final/pallas_call | solution.py:415
  185.1 11.2 %all_to_all.77 = f32[8,2,8,128]{3,2,1,0:T(8,128)S(1)} all-to-all(f32[8,2,8,128]{3,2,1,0:T(8,128)S(1)} %final.1), channel_id=1, replica_groups=mesh['firm'=16,'worker'=8,'probe'=4] {'worker'}, dimensions={0} | all-to-all | bytes 131072 | tf_op jit(solution)/shard_map/all_to_all | solution.py:338
  196.3 0.6 slice_bitcast_fusion
  (7 shorter events, 0.2 us)
Async XLA Ops:
  0.6 71.0 %copy-start.3 = (s32[1,128]{1,0:T(1,128)S(1)}, s32[1,128]{1,0:T(1,128)}, u32[]{:S(2)}) copy-start(s32[1,128]{1,0:T(1,128)} %refs_1_.7) | copy-start | bytes 1540
  0.6 71.0 %copy-start.2 = (s32[1,128]{1,0:T(1,128)S(1)}, s32[1,128]{1,0:T(1,128)}, u32[]{:S(2)}) copy-start(s32[1,128]{1,0:T(1,128)} %refs_0_.7) | copy-start | bytes 1540
  0.7 71.0 %copy-start = (s32[1,512]{1,0:T(1,128)S(1)}, s32[1,512]{1,0:T(1,128)}, u32[]{:S(2)}) copy-start(s32[1,512]{1,0:T(1,128)} %refs_6_.1) | copy-start | bytes 6148
  0.7 71.0 %copy-start.1 = (f32[1024]{0:T(1024)S(1)}, f32[1024]{0:T(1024)}, u32[]{:S(2)}) copy-start(f32[1024]{0:T(1024)} %param.11) | copy-start | bytes 12292

commit v6 on v5

--- a/solution.py
+++ b/solution.py
@@ -114,6 +114,15 @@
 def put_rows(rows, values):
     for block in range(ROWB_DEV):
         rows[block] = values[:, block * TILE : (block + 1) * TILE].astype(bf16).astype(f32)
+
+
+def put_parts(out, total, extras):
+    workers, firms = out.shape[0], out.shape[1] - len(extras)
+    for worker in range(workers):
+        for firm in range(firms):
+            out[worker, firm] = total[worker * firms + firm].astype(out.dtype)
+        for item, extra in enumerate(extras):
+            out[worker, firms + item] = extra.astype(out.dtype)
 
 
 def add_ridge(out, place, regular, worker, own):
@@ -142,22 +151,21 @@
 
 
 def middle_body(
-    workers, firms, tile_rows, tile_firms, worker, firm, field, first, regular, worker_ids, tiles, out, rows
+    workers, firms, tile_rows, tile_firms, worker, firm, field, first, regular, worker_ids, tiles,
+    out, rows, feature_sums,
 ):
     total = forward(tile_rows, tile_firms, field, tiles, workers, firms)
     values = demean(jnp.concatenate(total, axis=1), worker_ids[...])
     put_rows(rows, values)
-    adjoint(tile_rows, tile_firms, rows, tiles, out, workers, firms + 1)
+    adjoint(tile_rows, tile_firms, rows, tiles, feature_sums, workers, firms)
     own = first[...]
-    add_ridge(out, worker[0] * (firms + 1) + firm[0], regular, worker[0], own)
+    add_ridge(feature_sums, worker[0] * firms + firm[0], regular, worker[0], own)
     squares = own * own
     above = jnp.sum(values * values, axis=1, keepdims=True)
     above = above + jnp.sum(squares * regular[pl.ds(worker[0], 1), :], axis=1, keepdims=True)
     below = jnp.sum(squares, axis=1, keepdims=True)
     lanes = lax.broadcasted_iota(jnp.int32, own.shape, 1)
-    extra = jnp.where(lanes < TILE // 2, above, below)
-    for other in range(workers):
-        out[other * (firms + 1) + firms] = extra
+    put_parts(out, feature_sums, [jnp.where(lanes < TILE // 2, above, below)])
 
 
 def rows_body(workers, firms, tile_rows, tile_firms, field, first, second, quotient, worker_ids, tiles, out):
@@ -172,7 +180,8 @@
 
 
 def last_body(
-    workers, firms, tile_rows, tile_firms, worker, firm, probe, given, regular, tiles, out, rows
+    workers, firms, tile_rows, tile_firms, worker, firm, probe, given, regular, tiles,
+    out, rows, feature_sums,
 ):
     gather = lambda item: jnp.concatenate([given[other, item] for other in range(given.shape[0])], axis=0)
     own = lambda item: given[probe[0], item]
@@ -192,10 +201,9 @@
         ],
         axis=1,
     )
-    adjoint(tile_rows, tile_firms, rows, tiles, out, workers, firms + 1)
-    add_ridge(out, worker[0] * (firms + 1) + firm[0], regular, worker[0], second)
-    for other in range(workers):
-        out[other * (firms + 1) + firms] = extra
+    adjoint(tile_rows, tile_firms, rows, tiles, feature_sums, workers, firms)
+    add_ridge(feature_sums, worker[0] * firms + firm[0], regular, worker[0], second)
+    put_parts(out, feature_sums, three_parts(extra))
 
 
 def eliminate(table, pivots):
@@ -273,23 +281,22 @@
 
 
 def fold_body(got, out):
-    total = got[0]
+    total = sum_of(got)
+    firms, probes = out.shape[0], total.shape[1]
+    for firm in range(firms):
+        out[firm, :probes, :] = total[firm]
+    if out.shape[1] > probes:
+        extra = total[firms]
+        for item in range(firms + 1, total.shape[0]):
+            extra = extra + total[item]
+        for firm in range(firms):
+            out[firm, probes:, :] = extra
+
+
+def sum_of(got):
+    total = got[0].astype(f32)
     for other in range(1, got.shape[0]):
-        total = total + got[other]
-    firms, lines = out.shape[0], out.shape[1]
-    extra = lines * firms - total.shape[0]
-    extra = extra // (firms - 1)
-    probes = lines - extra
-    for firm in range(firms):
-        out[firm, :probes, :] = total[firm * probes : (firm + 1) * probes]
-        if extra:
-            out[firm, probes:, :] = total[firms * probes :]
-
-
-def sum_of(got):
-    total = got[0]
-    for other in range(1, got.shape[0]):
-        total = total + got[other]
+        total = total + got[other].astype(f32)
     return total
 
 
@@ -351,6 +358,7 @@
 
     VMEM, SMEM, HBM = pltpu.VMEM, pltpu.SMEM, pltpu.HBM
     rows_vmem = VMEM((ROWB_DEV, probe_dev, TILE), f32)
+    sums_vmem = VMEM((workers * firms, probe_dev, TILE), f32)
     cost = 2 * count * probe_dev * TILE * TILE
 
     def shape(*dims, dtype=f32):
@@ -360,9 +368,8 @@
         return pltpu.with_memory_space_constraint(array, where)
 
     def owner_parts(parts, beside):
-        chunk = parts.reshape(workers, -1, TILE)
-        got, beside = exchange(chunk, "worker", beside)
-        extra = chunk.shape[1] - firms * probe_dev
+        got, beside = exchange(parts.reshape(workers, -1, probe_dev, TILE), "worker", beside)
+        extra = probe_dev if got.shape[1] > firms else 0
         chunk = kernel(fold_body, shape(firms, probe_dev + extra, TILE), [VMEM], [], "fold")(got)
         return exchange(chunk, "firm", beside)
 
@@ -392,8 +399,8 @@
     field, (first, *at) = collect(sent, (first, *at))
     firm, worker, _ = at
     parts = kernel(
-        bind(middle_body), shape(workers * (firms + 1), probe_dev, TILE),
-        [SMEM, SMEM, SMEM, SMEM, VMEM, VMEM, VMEM, VMEM, VMEM], [rows_vmem], "middle", 2 * cost,
+        bind(middle_body), shape(workers, firms + 1, probe_dev, TILE, dtype=bf16),
+        [SMEM, SMEM, SMEM, SMEM, VMEM, VMEM, VMEM, VMEM, VMEM], [rows_vmem, sums_vmem], "middle", 2 * cost,
     )(tile_rows, tile_firms, worker, firm, field, first, reg_blocks, worker_ids, placed(tiles, VMEM))
     got, (first, *at) = owner_parts(parts, (first, *at))
     second, quotient, sent = kernel(second_body, (own, own, sent_own), [VMEM, VMEM], [], "second")(got, first)
@@ -406,8 +413,8 @@
     given, at = exchange(sent, "probe", at)
     firm, worker, probe = at
     parts = kernel(
-        bind(last_body), shape(workers * (firms + 1), probe_dev, TILE),
-        [SMEM, SMEM, SMEM, SMEM, SMEM, VMEM, VMEM, VMEM], [rows_vmem], "last", cost,
+        bind(last_body), shape(workers, firms + 3, probe_dev, TILE, dtype=bf16),
+        [SMEM, SMEM, SMEM, SMEM, SMEM, VMEM, VMEM, VMEM], [rows_vmem, sums_vmem], "last", cost,
     )(tile_rows, tile_firms, worker, firm, probe, given, reg_blocks, placed(tiles, VMEM))
     got, (given, *at) = owner_parts(parts, (given, *at))
     sent = kernel(third_body, shape(probes, 2 * probe_dev, TILE), [VMEM], [], "third")(got)

time: 197 us -> 192 us (0.975)
  blocking collectives: 181 us -> 176 us
    all_to_all x13, blocking collectives: 181 us -> 176 us  [exchange(): got = lax.all_to_all(chunks, axis, 0, 0, tiled=True)]
where the time goes in v6:
time: 192 us
  blocking collectives  176 us (92%)
  Pallas kernels  14.5 us (8%)
    all_to_all x13, blocking collectives, exchange(): got = lax.all_to_all(chunks, axis, 0, 0, tiled=True)  176 us
    pallas_call x1, Pallas kernels, local(): kernel(final_body, shape(workers, 2, probe_dev, TILE), [SMEM, VMEM, VMEM]...  5.01 us

profile of v6, /device:TPU:1, one launch (start us, length us, event | category | flops | bytes accessed | tf_op | source)
XLA Modules:
  0.0 191.7 jit_solution(13394117522995538528)
XLA Ops:
  0.6 0.0 copy-start.3
  0.6 0.0 copy-start.2
  0.7 0.0 copy-start
  0.7 0.0 copy-start.1
  0.7 2.7 %start.1 = (f32[128,8,128]{2,1,0:T(8,128)S(1)}, bf16[128,128,128]{2,1,0:T(8,128)(2,1)S(1)}) custom-call(s32[1,128]{1,0:T(1,128)} %refs_0_.7, s32[1,128]{1,0:T(1,128)} %refs_1_.7, s32[5,4,8]{2,1,0:T(4,128)} %bitcast.21, s32[1,512]{1,0:T(1,128)} %refs_6_.1, bf16[128,128,128]{2,1,0:T(8,128)(2,1)} %refs_4_.1), custom_call_target="tpu_custom_call" | custom-call | flops 33554432 | bytes 1048576 | tf_op jit(solution)/shard_map/start/pallas_call | solution.py:388
  3.4 18.6 %all_to_all.65.got = f32[8,16,8,128]{3,2,1,0:T(8,128)S(1)} all-to-all(f32[8,16,8,128]{3,2,1,0:T(8,128)S(1)} %bitcast.16), channel_id=1, replica_groups=mesh['firm'=16,'worker'=8,'probe'=4] {'worker'}, dimensions={0} | all-to-all | bytes 1048576 | tf_op jit(solution)/shard_map/all_to_all | solution.py:345
  22.0 22.8 %all_to_all.66.got = f32[16,8,128]{2,1,0:T(8,128)S(1)} all-to-all(f32[16,8,128]{2,1,0:T(8,128)S(1)} %fold.3), channel_id=1, replica_groups=mesh['firm'=16,'worker'=8,'probe'=4] {'firm'}, dimensions={0} | all-to-all | bytes 131072 | tf_op jit(solution)/shard_map/all_to_all | solution.py:345
  44.8 14.3 %all_to_all.67.values = bf16[16,8,128]{2,1,0:T(8,128)(2,1)S(1)} all-to-all(bf16[16,8,128]{2,1,0:T(8,128)(2,1)S(1)} %get-tuple-element.138), channel_id=1, replica_groups=mesh['firm'=16,'worker'=8,'probe'=4] {'firm'}, dimensions={0} | all-to-all | bytes 65536 | tf_op jit(solution)/shard_map/all_to_all | solution.py:345
  59.1 12.5 %all_to_all.68 = bf16[8,16,8,128]{3,2,1,0:T(8,128)(2,1)S(1)} all-to-all(bf16[8,16,8,128]{3,2,1,0:T(8,128)(2,1)S(1)} %spread.2), channel_id=1, replica_groups=mesh['firm'=16,'worker'=8,'probe'=4] {'worker'}, dimensions={0} | all-to-all | bytes 524288 | tf_op jit(solution)/shard_map/all_to_all | solution.py:345
  71.6 0.0 copy-done.3
  71.6 0.0 copy-done.2
  71.6 0.0 copy-done
  71.6 0.0 copy-done.1
  71.6 2.9 %middle.1 = bf16[8,17,8,128]{3,2,1,0:T(8,128)(2,1)S(1)} custom-call(s32[1,128]{1,0:T(1,128)S(1)} %copy-done.2, s32[1,128]{1,0:T(1,128)S(1)} %copy-done.3, s32[1]{0:T(128)} %bitcast.3.refs_2_, s32[1]{0:T(128)} %bitcast.2.refs_3_, bf16[128,8,128]{2,1,0:T(8,128)(2,1)S(1)} %bitcast.15, f32[8,128]{1,0:T(8,128)S(1)} %get-tuple-element.204.refs_5_.first.refs_3_, ...), custom_call_target="tpu_custom_call" | custom-call | flops 67108864 | bytes 1048576 | tf_op jit(solution)/shard_map/middle/pallas_call | solution.py:401
  74.5 10.7 %all_to_all.69.got = bf16[8,17,8,128]{3,2,1,0:T(8,128)(2,1)S(1)} all-to-all(bf16[8,17,8,128]{3,2,1,0:T(8,128)(2,1)S(1)} %middle.1), channel_id=1, replica_groups=mesh['firm'=16,'worker'=8,'probe'=4] {'worker'}, dimensions={0} | all-to-all | bytes 557056 | tf_op jit(solution)/shard_map/all_to_all | solution.py:345
  85.2 14.6 %all_to_all.70.got = f32[16,16,128]{2,1,0:T(8,128)S(1)} all-to-all(f32[16,16,128]{2,1,0:T(8,128)S(1)} %fold.4), channel_id=1, replica_groups=mesh['firm'=16,'worker'=8,'probe'=4] {'firm'}, dimensions={0} | all-to-all | bytes 262144 | tf_op jit(solution)/shard_map/all_to_all | solution.py:345
  99.8 0.2 second.1
  100.0 17.7 %all_to_all.71.values = bf16[16,8,128]{2,1,0:T(8,128)(2,1)S(1)} all-to-all(bf16[16,8,128]{2,1,0:T(8,128)(2,1)S(1)} %get-tuple-element.182), channel_id=1, replica_groups=mesh['firm'=16,'worker'=8,'probe'=4] {'firm'}, dimensions={0} | all-to-all | bytes 65536 | tf_op jit(solution)/shard_map/all_to_all | solution.py:345
  117.7 11.0 %all_to_all.72 = bf16[8,16,8,128]{3,2,1,0:T(8,128)(2,1)S(1)} all-to-all(bf16[8,16,8,128]{3,2,1,0:T(8,128)(2,1)S(1)} %spread.3), channel_id=1, replica_groups=mesh['firm'=16,'worker'=8,'probe'=4] {'worker'}, dimensions={0} | all-to-all | bytes 524288 | tf_op jit(solution)/shard_map/all_to_all | solution.py:345
  128.7 2.0 %rows.1 = f32[4,7,8,128]{3,2,1,0:T(8,128)S(1)} custom-call(s32[1,128]{1,0:T(1,128)S(1)} %copy-done.2, s32[1,128]{1,0:T(1,128)S(1)} %copy-done.3, bf16[128,8,128]{2,1,0:T(8,128)(2,1)S(1)} %bitcast.14, f32[8,128]{1,0:T(8,128)S(1)} %get-tuple-element.204.refs_5_.first.refs_3_, f32[8,128]{1,0:T(8,128)S(1)} %get-tuple-element.205.refs_4_, ...), custom_call_target="tpu_custom_call" | custom-call | flops 33554432 | bytes 1048576 | tf_op jit(solution)/shard_map/rows/pallas_call | solution.py:409
  130.7 8.6 %all_to_all.73.refs_5_.given = f32[4,7,8,128]{3,2,1,0:T(8,128)S(1)} all-to-all(f32[4,7,8,128]{3,2,1,0:T(8,128)S(1)} %rows.1), channel_id=1, replica_groups=mesh['firm'=16,'worker'=8,'probe'=4] {'probe'}, dimensions={0} | all-to-all | bytes 229376 | tf_op jit(solution)/shard_map/all_to_all | solution.py:345
  139.3 1.5 last.1
  140.8 12.2 %all_to_all.74.got = bf16[8,19,8,128]{3,2,1,0:T(8,128)(2,1)S(1)} all-to-all(bf16[8,19,8,128]{3,2,1,0:T(8,128)(2,1)S(1)} %last.1), channel_id=1, replica_groups=mesh['firm'=16,'worker'=8,'probe'=4] {'worker'}, dimensions={0} | all-to-all | bytes 622592 | tf_op jit(solution)/shard_map/all_to_all | solution.py:345
  153.1 14.6 %all_to_all.75.got = f32[16,16,128]{2,1,0:T(8,128)S(1)} all-to-all(f32[16,16,128]{2,1,0:T(8,128)S(1)} %fold.5), channel_id=1, replica_groups=mesh['firm'=16,'worker'=8,'probe'=4] {'firm'}, dimensions={0} | all-to-all | bytes 262144 | tf_op jit(solution)/shard_map/all_to_all | solution.py:345
  167.7 6.7 %all_to_all.76 = f32[4,16,128]{2,1,0:T(8,128)S(1)} all-to-all(f32[4,16,128]{2,1,0:T(8,128)S(1)} %third.1), channel_id=1, replica_groups=mesh['firm'=16,'worker'=8,'probe'=4] {'probe'}, dimensions={0} | all-to-all | bytes 65536 | tf_op jit(solution)/shard_map/all_to_all | solution.py:345
  174.3 5.0 %final.1 = f32[8,2,8,128]{3,2,1,0:T(8,128)S(1)} custom-call(s32[1]{0:T(128)} %bitcast.4.refs_4_.probe, f32[4,7,8,128]{3,2,1,0:T(8,128)S(1)} %all_to_all.73.refs_5_.given, f32[4,2,8,128]{3,2,1,0:T(8,128)S(1)} %bitcast.17), custom_call_target="tpu_custom_call" | custom-call | flops 8388608 | bytes 1048576 | tf_op jit(solution)/shard_map/final/pallas_call | solution.py:422
  179.4 11.7 %all_to_all.77 = f32[8,2,8,128]{3,2,1,0:T(8,128)S(1)} all-to-all(f32[8,2,8,128]{3,2,1,0:T(8,128)S(1)} %final.1), channel_id=1, replica_groups=mesh['firm'=16,'worker'=8,'probe'=4] {'worker'}, dimensions={0} | all-to-all | bytes 131072 | tf_op jit(solution)/shard_map/all_to_all | solution.py:345
  191.1 0.6 slice_bitcast_fusion
  (7 shorter events, 0.2 us)
Async XLA Ops:
  0.6 71.0 %copy-start.3 = (s32[1,128]{1,0:T(1,128)S(1)}, s32[1,128]{1,0:T(1,128)}, u32[]{:S(2)}) copy-start(s32[1,128]{1,0:T(1,128)} %refs_1_.7) | copy-start | bytes 1540
  0.6 71.0 %copy-start.2 = (s32[1,128]{1,0:T(1,128)S(1)}, s32[1,128]{1,0:T(1,128)}, u32[]{:S(2)}) copy-start(s32[1,128]{1,0:T(1,128)} %refs_0_.7) | copy-start | bytes 1540
  0.7 71.0 %copy-start = (s32[1,512]{1,0:T(1,128)S(1)}, s32[1,512]{1,0:T(1,128)}, u32[]{:S(2)}) copy-start(s32[1,512]{1,0:T(1,128)} %refs_6_.1) | copy-start | bytes 6148
  0.7 71.0 %copy-start.1 = (f32[1024]{0:T(1024)S(1)}, f32[1024]{0:T(1024)}, u32[]{:S(2)}) copy-start(f32[1024]{0:T(1024)} %param.11) | copy-start | bytes 12292

commit v7 on v6

--- a/solution.py
+++ b/solution.py
@@ -11,6 +11,11 @@
 SHARD_WORKERS = 128
 BITS = 30
 CHUNKS = 4
+WORKERS = 8
+FIRMS = 16
+NEAR_FIRST = 2
+NEAR_SECOND = 4
+FIRM_AXES = ("firm_far", "firm_middle", "firm_near")
 
 largest_value = lax.Precision.HIGHEST
 f32 = jnp.float32
@@ -70,21 +75,23 @@
     return tables
 
 
-def place_of(firm, workers, stride):
-    return (firm & (workers - 1)) * stride + (firm >> (workers.bit_length() - 1))
-
-
-def pair(upper, lower):
-    return jnp.concatenate([upper.astype(f32), lower.astype(f32)], axis=0).astype(bf16)
-
-
-def forward(tile_rows, tile_firms, field, tiles, workers, firms):
+def place_of(block, near):
+    firm, worker = block >> (WORKERS.bit_length() - 1), block & (WORKERS - 1)
+    shift = near.bit_length() - 1
+    return ((firm & (near - 1)) * WORKERS + worker) * (FIRMS // near) + (firm >> shift)
+
+
+def stack(pieces):
+    return jnp.concatenate([piece.astype(f32) for piece in pieces], axis=0).astype(bf16)
+
+
+def forward(tile_rows, tile_firms, field, tiles, near):
     total = None
     for tile in range(0, tiles.shape[0], 2):
-        pieces = [field[place_of(tile_firms[0, tile + item], workers, firms)] for item in range(2)]
+        pieces = [field[place_of(tile_firms[0, tile + item], near)] for item in range(2)]
         probes = pieces[0].shape[0]
         weights = jnp.concatenate([tiles[tile], tiles[tile + 1]], axis=0)
-        both = dot(pair(*pieces), weights, (1, 1))
+        both = dot(stack(pieces), weights, (1, 1))
         if total is None:
             total = [jnp.zeros((probes, TILE), f32) for block in range(ROWB_DEV)]
         for item in range(2):
@@ -94,21 +101,22 @@
     return total
 
 
-def adjoint(tile_rows, tile_firms, rows, tiles, out, workers, stride, wait=None):
+def adjoint(tile_rows, tile_firms, rows, tiles, out, near, wait=None):
     out[...] = jnp.zeros_like(out)
-    probes = rows.shape[1]
+    probes, lines = out.shape[1], rows.shape[1]
     size = tiles.shape[0] // CHUNKS
     for tile in range(0, tiles.shape[0], 2):
         if wait is not None and tile % (2 * size) == 0:
             wait(tile // size)
             wait(tile // size + 1)
-        pieces = [rows[tile_rows[0, tile + item]] for item in range(2)]
         weights = jnp.concatenate([tiles[tile], tiles[tile + 1]], axis=1)
-        both = dot(pair(*pieces), weights, (1, 0))
+        both = dot(stack([rows[tile_rows[0, tile + item]] for item in range(2)]), weights, (1, 0))
         for item in range(2):
-            image = both[item * probes : (item + 1) * probes, item * TILE : (item + 1) * TILE]
-            place = place_of(tile_firms[0, tile + item], workers, stride)
-            out[place] = out[place] + image
+            place = place_of(tile_firms[0, tile + item], near)
+            image = out[place]
+            for begin in range(item * lines, (item + 1) * lines, probes):
+                image = image + both[begin : begin + probes, item * TILE : (item + 1) * TILE]
+            out[place] = image
 
 
 def put_rows(rows, values):
@@ -116,21 +124,27 @@
         rows[block] = values[:, block * TILE : (block + 1) * TILE].astype(bf16).astype(f32)
 
 
+def put_two_terms(rows, values):
+    high = values.astype(bf16).astype(f32)
+    rows[...] = jnp.concatenate([high, (values - high).astype(bf16).astype(f32)], axis=0)
+
+
 def put_parts(out, total, extras):
-    workers, firms = out.shape[0], out.shape[1] - len(extras)
-    for worker in range(workers):
-        for firm in range(firms):
-            out[worker, firm] = total[worker * firms + firm].astype(out.dtype)
+    peers, blocks = out.shape[0], out.shape[1] - len(extras)
+    for peer in range(peers):
+        for block in range(blocks):
+            out[peer, block] = total[peer * blocks + block].astype(out.dtype)
         for item, extra in enumerate(extras):
-            out[worker, firms + item] = extra.astype(out.dtype)
-
-
-def add_ridge(out, place, regular, worker, own):
+            out[peer, blocks + item] = extra.astype(out.dtype)
+
+
+def add_ridge(out, firm, worker, near, regular, own):
+    place = place_of(firm * WORKERS + worker, near)
     out[place] = out[place] + regular[pl.ds(worker, 1), :] * own
 
 
 def start_body(
-    workers, firms, rows_hbm, firms_hbm, words_hbm, ids_hbm, tiles_hbm,
+    rows_hbm, firms_hbm, words_hbm, ids_hbm, tiles_hbm,
     out, tiles, rows, arrived, tile_rows, tile_firms, words, worker_ids,
 ):
     small = [(rows_hbm, tile_rows), (firms_hbm, tile_firms), (words_hbm, words), (ids_hbm, worker_ids)]
@@ -147,19 +161,19 @@
             chosen = [jnp.where(here, words[word, block, probe], old) for block, old in enumerate(chosen)]
     signs = [(2 * (lax.shift_right_logical(old, bit) & 1) - 1).astype(f32) for old in chosen]
     put_rows(rows, demean(jnp.concatenate(signs, axis=1), worker_ids[...]))
-    adjoint(tile_rows, tile_firms, rows, tiles, out, workers, firms, wait)
+    adjoint(tile_rows, tile_firms, rows, tiles, out, NEAR_FIRST, wait)
 
 
 def middle_body(
-    workers, firms, tile_rows, tile_firms, worker, firm, field, first, regular, worker_ids, tiles,
+    tile_rows, tile_firms, worker, firm, field, firsts, regular, worker_ids, tiles,
     out, rows, feature_sums,
 ):
-    total = forward(tile_rows, tile_firms, field, tiles, workers, firms)
+    total = forward(tile_rows, tile_firms, field, tiles, NEAR_FIRST)
     values = demean(jnp.concatenate(total, axis=1), worker_ids[...])
     put_rows(rows, values)
-    adjoint(tile_rows, tile_firms, rows, tiles, feature_sums, workers, firms)
-    own = first[...]
-    add_ridge(feature_sums, worker[0] * firms + firm[0], regular, worker[0], own)
+    adjoint(tile_rows, tile_firms, rows, tiles, feature_sums, NEAR_SECOND)
+    own = firsts[lax.div(firm[0], NEAR_FIRST)]
+    add_ridge(feature_sums, firm[0], worker[0], NEAR_SECOND, regular, own)
     squares = own * own
     above = jnp.sum(values * values, axis=1, keepdims=True)
     above = above + jnp.sum(squares * regular[pl.ds(worker[0], 1), :], axis=1, keepdims=True)
@@ -168,8 +182,8 @@
     put_parts(out, feature_sums, [jnp.where(lanes < TILE // 2, above, below)])
 
 
-def rows_body(workers, firms, tile_rows, tile_firms, field, first, second, quotient, worker_ids, tiles, out):
-    total = forward(tile_rows, tile_firms, field, tiles, workers, firms)
+def rows_body(tile_rows, tile_firms, field, first, second, quotient, worker_ids, tiles, out):
+    total = forward(tile_rows, tile_firms, field, tiles, NEAR_SECOND)
     values = demean(jnp.concatenate(total, axis=1), worker_ids[...])
     for probe in range(out.shape[0]):
         out[probe, 0] = first[...]
@@ -180,7 +194,7 @@
 
 
 def last_body(
-    workers, firms, tile_rows, tile_firms, worker, firm, probe, given, regular, tiles,
+    tile_rows, tile_firms, worker, firm, probe, given, regular, tiles,
     out, rows, feature_sums,
 ):
     gather = lambda item: jnp.concatenate([given[other, item] for other in range(given.shape[0])], axis=0)
@@ -189,7 +203,7 @@
     first_all, second_all = gather(0), gather(1)
     mine = [own(3 + block) for block in range(ROWB_DEV)]
     for block in range(ROWB_DEV):
-        rows[block] = mine[block].astype(bf16).astype(f32)
+        put_two_terms(rows.at[block], mine[block])
     left = jnp.concatenate([*mine, second * regular[pl.ds(worker[0], 1), :]], axis=1)
     right = jnp.concatenate([*(gather(3 + block) for block in range(ROWB_DEV)), second_all], axis=1)
     extra = jnp.concatenate(
@@ -201,8 +215,8 @@
         ],
         axis=1,
     )
-    adjoint(tile_rows, tile_firms, rows, tiles, feature_sums, workers, firms)
-    add_ridge(feature_sums, worker[0] * firms + firm[0], regular, worker[0], second)
+    adjoint(tile_rows, tile_firms, rows, tiles, feature_sums, 1)
+    add_ridge(feature_sums, firm[0], worker[0], 1, regular, second)
     put_parts(out, feature_sums, three_parts(extra))
 
 
@@ -305,22 +319,27 @@
         out[other] = values.astype(out.dtype)
 
 
-def first_body(got, first, sent):
-    first[...] = sum_of(got)
-    send(sent, first[...])
-
-
-def second_body(got, first, second, quotient, sent):
+def gather_fold_body(got, out):
+    send(out, sum_of(got))
+
+
+def first_body(got, firsts, sent):
+    firsts[...] = sum_of(got)
+    send(sent, firsts[...])
+
+
+def second_body(firm, got, firsts, first, second, quotient, sent, seconds):
     total = sum_of(got)
-    probes = first.shape[0]
-    ratio = total[probes:, :1] / total[probes:, TILE // 2 : TILE // 2 + 1]
+    blocks = total.shape[0] - 1
+    ratio = total[blocks, :, :1] / total[blocks, :, TILE // 2 : TILE // 2 + 1]
     quotient[...] = jnp.broadcast_to(ratio, quotient.shape)
-    second[...] = first[...] - total[:probes] / quotient[...]
-    send(sent, second[...])
-
-
-def send_body(values, sent):
-    send(sent, values[...])
+    step = NEAR_SECOND // NEAR_FIRST
+    near = lax.div(firm[0], NEAR_FIRST) & (step - 1)
+    for block in range(blocks):
+        seconds[block] = firsts[block * step + near] - total[block] / quotient[...]
+    first[...] = firsts[lax.div(firm[0], NEAR_FIRST)]
+    second[...] = seconds[lax.div(firm[0], NEAR_SECOND)]
+    send(sent, seconds[...])
 
 
 def third_body(got, sent):
@@ -348,99 +367,111 @@
 
 def local(tiles, tile_rows, tile_firms, worker_ids, sign_words, regular):
     probe_dev = sign_words.shape[0]
-    firms = lax.axis_size("firm")
-    workers = lax.axis_size("worker")
     probes = lax.axis_size("probe")
     count = tiles.shape[0]
-    reg_blocks = regular.reshape(workers, TILE)
+    blocks = WORKERS * FIRMS
+    reg_blocks = regular.reshape(WORKERS, TILE)
     words = jnp.transpose(sign_words, (2, 1, 0))
-    at = tuple(lax.axis_index(axis).reshape(1) for axis in ("firm", "worker", "probe"))
+    at = tuple(lax.axis_index(axis).reshape(1) for axis in (FIRM_AXES, "worker", "probe"))
 
     VMEM, SMEM, HBM = pltpu.VMEM, pltpu.SMEM, pltpu.HBM
     rows_vmem = VMEM((ROWB_DEV, probe_dev, TILE), f32)
-    sums_vmem = VMEM((workers * firms, probe_dev, TILE), f32)
+    sums_vmem = VMEM((blocks, probe_dev, TILE), f32)
     cost = 2 * count * probe_dev * TILE * TILE
 
     def shape(*dims, dtype=f32):
-        return jax.ShapeDtypeStruct(dims, dtype)
+        return jax.ShapeDtypeStruct((*dims, probe_dev, TILE), dtype)
 
     def placed(array, where):
         return pltpu.with_memory_space_constraint(array, where)
 
-    def owner_parts(parts, beside):
-        got, beside = exchange(parts.reshape(workers, -1, probe_dev, TILE), "worker", beside)
-        extra = probe_dev if got.shape[1] > firms else 0
-        chunk = kernel(fold_body, shape(firms, probe_dev + extra, TILE), [VMEM], [], "fold")(got)
-        return exchange(chunk, "firm", beside)
-
-    def collect(sent, beside):
-        column, beside = exchange(sent, "firm", beside)
-        dims = (workers, firms, probe_dev, TILE)
-        sent = kernel(send_body, shape(*dims, dtype=bf16), [VMEM], [], "spread")(column)
-        field, beside = exchange(sent, "worker", beside)
-        return field.reshape(workers * firms, probe_dev, TILE), beside
-
-    def bind(body):
-        return lambda *refs: body(workers, firms, *refs)
-
-    own = shape(probe_dev, TILE)
-    sent_own = shape(firms, probe_dev, TILE, dtype=bf16)
+    near_first, far_first = (*FIRM_AXES[2:], "worker"), FIRM_AXES[:2]
+    near_second, far_second = (*FIRM_AXES[1:], "worker"), FIRM_AXES[:1]
+    peers_first, held_first = NEAR_FIRST * WORKERS, FIRMS // NEAR_FIRST
+    peers_second, held_second = NEAR_SECOND * WORKERS, FIRMS // NEAR_SECOND
+
     parts, tiles = kernel(
-        bind(start_body), (shape(workers * firms, probe_dev, TILE), VMEM(tiles.shape, bf16)), [HBM] * 5,
+        start_body, (shape(blocks), VMEM(tiles.shape, bf16)), [HBM] * 5,
         [
             rows_vmem, pltpu.SemaphoreType.DMA((CHUNKS + 4,)), SMEM(tile_rows.shape, jnp.int32),
             SMEM(tile_firms.shape, jnp.int32), SMEM(words.shape, jnp.int32), VMEM(worker_ids.shape, jnp.int32),
         ],
         "start", cost,
     )(*(placed(array, HBM) for array in (tile_rows, tile_firms, words, worker_ids, tiles)))
-    got, at = owner_parts(parts, at)
-    first, sent = kernel(first_body, (own, sent_own), [VMEM], [], "first")(got)
-
-    field, (first, *at) = collect(sent, (first, *at))
+    got, at = exchange(parts.reshape(peers_first, held_first, probe_dev, TILE), near_first, at)
+    sent = kernel(gather_fold_body, shape(held_first, held_first), [VMEM], [], "fold")(got)
+    got, at = exchange(sent, far_first, at)
+    firsts, sent = kernel(
+        first_body, (shape(held_first), shape(peers_first, held_first, dtype=bf16)), [VMEM], [], "first"
+    )(got)
+
+    field, (firsts, *at) = exchange(sent, near_first, (firsts, *at))
     firm, worker, _ = at
     parts = kernel(
-        bind(middle_body), shape(workers, firms + 1, probe_dev, TILE, dtype=bf16),
+        middle_body, shape(peers_second, held_second + 1, dtype=bf16),
         [SMEM, SMEM, SMEM, SMEM, VMEM, VMEM, VMEM, VMEM, VMEM], [rows_vmem, sums_vmem], "middle", 2 * cost,
-    )(tile_rows, tile_firms, worker, firm, field, first, reg_blocks, worker_ids, placed(tiles, VMEM))
-    got, (first, *at) = owner_parts(parts, (first, *at))
-    second, quotient, sent = kernel(second_body, (own, own, sent_own), [VMEM, VMEM], [], "second")(got, first)
-
-    field, (first, second, quotient, *at) = collect(sent, (first, second, quotient, *at))
+    )(
+        tile_rows, tile_firms, worker, firm, field.reshape(blocks, probe_dev, TILE), firsts, reg_blocks,
+        worker_ids, placed(tiles, VMEM),
+    )
+    got, (firsts, *at) = exchange(parts, near_second, (firsts, *at))
+    sent = kernel(gather_fold_body, shape(held_second, held_second + 1), [VMEM], [], "fold")(got)
+    got, (firsts, *at) = exchange(sent, far_second, (firsts, *at))
+    first, second, quotient, sent = kernel(
+        second_body, (shape(), shape(), shape(), shape(peers_second, held_second, dtype=bf16)),
+        [SMEM, VMEM, VMEM], [VMEM((held_second, probe_dev, TILE), f32)], "second",
+    )(at[0], got, firsts)
+
+    field, (first, second, quotient, *at) = exchange(sent, near_second, (first, second, quotient, *at))
     sent = kernel(
-        bind(rows_body), shape(probes, 3 + ROWB_DEV, probe_dev, TILE),
-        [SMEM, SMEM, VMEM, VMEM, VMEM, VMEM, VMEM, VMEM], [], "rows", cost,
-    )(tile_rows, tile_firms, field, first, second, quotient, worker_ids, placed(tiles, VMEM))
+        rows_body, shape(probes, 3 + ROWB_DEV), [SMEM, SMEM, VMEM, VMEM, VMEM, VMEM, VMEM, VMEM], [], "rows", cost
+    )(
+        tile_rows, tile_firms, field.reshape(blocks, probe_dev, TILE), first, second, quotient, worker_ids,
+        placed(tiles, VMEM),
+    )
     given, at = exchange(sent, "probe", at)
     firm, worker, probe = at
     parts = kernel(
-        bind(last_body), shape(workers, firms + 3, probe_dev, TILE, dtype=bf16),
-        [SMEM, SMEM, SMEM, SMEM, SMEM, VMEM, VMEM, VMEM], [rows_vmem, sums_vmem], "last", cost,
+        last_body, shape(WORKERS, FIRMS + 3, dtype=bf16),
+        [SMEM, SMEM, SMEM, SMEM, SMEM, VMEM, VMEM, VMEM],
+        [VMEM((ROWB_DEV, 2 * probe_dev, TILE), f32), sums_vmem], "last", cost,
     )(tile_rows, tile_firms, worker, firm, probe, given, reg_blocks, placed(tiles, VMEM))
-    got, (given, *at) = owner_parts(parts, (given, *at))
-    sent = kernel(third_body, shape(probes, 2 * probe_dev, TILE), [VMEM], [], "third")(got)
+    got, (given, *at) = exchange(parts, "worker", (given, *at))
+    sent = kernel(
+        fold_body, jax.ShapeDtypeStruct((FIRMS, 2 * probe_dev, TILE), f32), [VMEM], [], "fold_last"
+    )(got)
+    got, (given, *at) = exchange(sent, FIRM_AXES, (given, *at))
+    sent = kernel(
+        third_body, jax.ShapeDtypeStruct((probes, 2 * probe_dev, TILE), f32), [VMEM], [], "third"
+    )(got)
     last, (given, *at) = exchange(sent, "probe", (given, *at))
     outs = kernel(
-        final_body, shape(workers, 2, probe_dev, TILE), [SMEM, VMEM, VMEM],
+        final_body, shape(WORKERS, 2), [SMEM, VMEM, VMEM],
         [VMEM((2, probes * probe_dev, TILE), f32)], "final", cost // 4,
     )(at[2], given, last.reshape(probes, 2, probe_dev, TILE))
     outs, _ = exchange(outs, "worker")
-    outs = jnp.transpose(outs, (1, 2, 0, 3)).reshape(2, probe_dev, workers * TILE)
+    outs = jnp.transpose(outs, (1, 2, 0, 3)).reshape(2, probe_dev, WORKERS * TILE)
     return (outs[0], outs[1])
 
 
 def solution(mesh):
+    sizes = (FIRMS // NEAR_SECOND, NEAR_SECOND // NEAR_FIRST, NEAR_FIRST)
+    split = jax.sharding.Mesh(
+        mesh.devices.reshape(*sizes, WORKERS, mesh.shape["probe"]), (*FIRM_AXES, "worker", "probe")
+    )
+    shard = (*FIRM_AXES, "worker")
     placed = (
-        P(("firm", "worker"), None, None),
-        P(("firm", "worker"), None),
-        P(("firm", "worker"), None),
-        P(("firm", "worker"), None),
-        P("probe", ("firm", "worker"), None),
-        P("firm"),
+        P(shard, None, None),
+        P(shard, None),
+        P(shard, None),
+        P(shard, None),
+        P("probe", shard, None),
+        P(FIRM_AXES),
     )
     return jax.shard_map(
         local,
-        mesh=mesh,
+        mesh=split,
         in_specs=placed,
-        out_specs=(P("probe", "firm"), P("probe", "firm")),
+        out_specs=(P("probe", FIRM_AXES), P("probe", FIRM_AXES)),
         check_vma=False,
     )

time: 192 us -> 181 us (0.943)
  blocking collectives: 176 us -> 165 us
    all_to_all x13 -> x11, blocking collectives: 176 us -> 165 us  [exchange(): got = lax.all_to_all(chunks, axis, 0, 0, tiled=True)]
    pallas_call x13 -> x11, Pallas kernels: 14.5 us -> 14.6 us  [the longest x1 5.01 us: local(): kernel(final_body, shape(WORKERS, 2), [SMEM, VMEM, VMEM], [VMEM((2, probe...]
where the time goes in v7:
time: 181 us
  blocking collectives  165 us (91%)
  Pallas kernels  14.6 us (8%)
    all_to_all x11, blocking collectives, exchange(): got = lax.all_to_all(chunks, axis, 0, 0, tiled=True)  165 us
    pallas_call x1, Pallas kernels, local(): kernel(final_body, shape(WORKERS, 2), [SMEM, VMEM, VMEM], [VMEM((2, probe...  5.01 us

profile of v7, /device:TPU:1, one launch (start us, length us, event | category | flops | bytes accessed | tf_op | source)
XLA Modules:
  0.0 181.0 jit_solution(16972769049325994578)
XLA Ops:
  0.6 0.0 copy-start.3
  0.6 0.0 copy-start.2
  0.7 0.0 copy-start
  0.7 0.0 copy-start.1
  0.7 2.7 %start.1 = (f32[128,8,128]{2,1,0:T(8,128)S(1)}, bf16[128,128,128]{2,1,0:T(8,128)(2,1)S(1)}) custom-call(s32[1,128]{1,0:T(1,128)} %tile_rows.5, s32[1,128]{1,0:T(1,128)} %tile_firms.5, s32[5,4,8]{2,1,0:T(4,128)} %bitcast.21, s32[1,512]{1,0:T(1,128)} %worker_ids.3, bf16[128,128,128]{2,1,0:T(8,128)(2,1)} %tiles_hbm.1), custom_call_target="tpu_custom_call" | custom-call | flops 33554432 | bytes 1048576 | tf_op jit(solution)/shard_map/start/pallas_call | solution.py:393
  3.4 19.0 %all_to_all.55.got = f32[16,8,8,128]{3,2,1,0:T(8,128)S(1)} all-to-all(f32[16,8,8,128]{3,2,1,0:T(8,128)S(1)} %bitcast.16), channel_id=1, replica_groups=mesh['firm_far'=4,'firm_middle'=2,'firm_near'=2,'worker'=8,'probe'=4] {'..., dimensions={0} | all-to-all | bytes 1048576 | tf_op jit(solution)/shard_map/all_to_all | solution.py:364
  22.5 28.5 %all_to_all.56.got = f32[8,8,8,128]{3,2,1,0:T(8,128)S(1)} all-to-all(f32[8,8,8,128]{3,2,1,0:T(8,128)S(1)} %fold.2), channel_id=1, replica_groups=mesh['firm_far'=4,'firm_middle'=2,'firm_near'=2,'worker'=8,'probe'=4] {'..., dimensions={0} | all-to-all | bytes 524288 | tf_op jit(solution)/shard_map/all_to_all | solution.py:364
  51.0 15.3 %all_to_all.57 = bf16[16,8,8,128]{3,2,1,0:T(8,128)(2,1)S(1)} all-to-all(bf16[16,8,8,128]{3,2,1,0:T(8,128)(2,1)S(1)} %get-tuple-element.115), channel_id=1, replica_groups=mesh['firm_far'=4,'firm_middle'=2,'firm_near'=2,'worker'=8,'probe'=4] {'..., dimensions={0} | all-to-all | bytes 524288 | tf_op jit(solution)/shard_map/all_to_all | solution.py:364
  66.3 0.0 copy-done.3
  66.3 0.0 copy-done.2
  66.3 0.0 copy-done
  66.3 0.0 copy-done.1
  66.4 2.9 %middle.1 = bf16[32,5,8,128]{3,2,1,0:T(8,128)(2,1)S(1)} custom-call(s32[1,128]{1,0:T(1,128)S(1)} %copy-done.2, s32[1,128]{1,0:T(1,128)S(1)} %copy-done.3, s32[1]{0:T(128)} %bitcast.3.worker, s32[1]{0:T(128)} %bitcast.2.firm, bf16[128,8,128]{2,1,0:T(8,128)(2,1)S(1)} %bitcast.14, f32[8,8,128]{2,1,0:T(8,128)S(1)} %get-tuple-element.143.firsts, ...), custom_call_target="tpu_custom_call" | custom-call | flops 67108864 | bytes 1048576 | tf_op jit(solution)/shard_map/middle/pallas_call | solution.py:410
  69.2 17.0 %all_to_all.58.got = bf16[32,5,8,128]{3,2,1,0:T(8,128)(2,1)S(1)} all-to-all(bf16[32,5,8,128]{3,2,1,0:T(8,128)(2,1)S(1)} %middle.1), channel_id=1, replica_groups=mesh['firm_far'=4,'firm_middle'=2,'firm_near'=2,'worker'=8,'probe'=4] {'..., dimensions={0} | all-to-all | bytes 655360 | tf_op jit(solution)/shard_map/all_to_all | solution.py:364
  86.2 0.1 fold.3
  86.3 14.9 %all_to_all.59.got = f32[4,5,8,128]{3,2,1,0:T(8,128)S(1)} all-to-all(f32[4,5,8,128]{3,2,1,0:T(8,128)S(1)} %fold.3), channel_id=1, replica_groups=mesh['firm_far'=4,'firm_middle'=2,'firm_near'=2,'worker'=8,'probe'=4] {'..., dimensions={0} | all-to-all | bytes 163840 | tf_op jit(solution)/shard_map/all_to_all | solution.py:364
  101.2 0.2 second.1
  101.4 17.1 %all_to_all.60 = bf16[32,4,8,128]{3,2,1,0:T(8,128)(2,1)S(1)} all-to-all(bf16[32,4,8,128]{3,2,1,0:T(8,128)(2,1)S(1)} %get-tuple-element.150), channel_id=1, replica_groups=mesh['firm_far'=4,'firm_middle'=2,'firm_near'=2,'worker'=8,'probe'=4] {'..., dimensions={0} | all-to-all | bytes 524288 | tf_op jit(solution)/shard_map/all_to_all | solution.py:364
  118.5 2.0 %rows.1 = f32[4,7,8,128]{3,2,1,0:T(8,128)S(1)} custom-call(s32[1,128]{1,0:T(1,128)S(1)} %copy-done.2, s32[1,128]{1,0:T(1,128)S(1)} %copy-done.3, bf16[128,8,128]{2,1,0:T(8,128)(2,1)S(1)} %bitcast.15, f32[8,128]{1,0:T(8,128)S(1)} %get-tuple-element.158.first, f32[8,128]{1,0:T(8,128)S(1)} %get-tuple-element.159.second, ...), custom_call_target="tpu_custom_call" | custom-call | flops 33554432 | bytes 1048576 | tf_op jit(solution)/shard_map/rows/pallas_call | solution.py:426
  120.6 8.6 %all_to_all.61.given = f32[4,7,8,128]{3,2,1,0:T(8,128)S(1)} all-to-all(f32[4,7,8,128]{3,2,1,0:T(8,128)S(1)} %rows.1), channel_id=1, replica_groups=mesh['firm_far'=4,'firm_middle'=2,'firm_near'=2,'worker'=8,'probe'=4] {'..., dimensions={0} | all-to-all | bytes 229376 | tf_op jit(solution)/shard_map/all_to_all | solution.py:364
  129.1 1.6 last.1
  130.8 11.4 %all_to_all.62.got = bf16[8,19,8,128]{3,2,1,0:T(8,128)(2,1)S(1)} all-to-all(bf16[8,19,8,128]{3,2,1,0:T(8,128)(2,1)S(1)} %last.1), channel_id=1, replica_groups=mesh['firm_far'=4,'firm_middle'=2,'firm_near'=2,'worker'=8,'probe'=4] {'..., dimensions={0} | all-to-all | bytes 622592 | tf_op jit(solution)/shard_map/all_to_all | solution.py:364
  142.2 14.6 %all_to_all.63.got = f32[16,16,128]{2,1,0:T(8,128)S(1)} all-to-all(f32[16,16,128]{2,1,0:T(8,128)S(1)} %fold_last.1), channel_id=1, replica_groups=mesh['firm_far'=4,'firm_middle'=2,'firm_near'=2,'worker'=8,'probe'=4] {'..., dimensions={0} | all-to-all | bytes 262144 | tf_op jit(solution)/shard_map/all_to_all | solution.py:364
  156.9 6.7 %all_to_all.64 = f32[4,16,128]{2,1,0:T(8,128)S(1)} all-to-all(f32[4,16,128]{2,1,0:T(8,128)S(1)} %third.1), channel_id=1, replica_groups=mesh['firm_far'=4,'firm_middle'=2,'firm_near'=2,'worker'=8,'probe'=4] {'..., dimensions={0} | all-to-all | bytes 65536 | tf_op jit(solution)/shard_map/all_to_all | solution.py:364
  163.5 5.0 %final.1 = f32[8,2,8,128]{3,2,1,0:T(8,128)S(1)} custom-call(s32[1]{0:T(128)} %bitcast.4.probe, f32[4,7,8,128]{3,2,1,0:T(8,128)S(1)} %all_to_all.61.given, f32[4,2,8,128]{3,2,1,0:T(8,128)S(1)} %bitcast.17), custom_call_target="tpu_custom_call" | custom-call | flops 8388608 | bytes 1048576 | tf_op jit(solution)/shard_map/final/pallas_call | solution.py:448
  168.5 11.8 %all_to_all.65 = f32[8,2,8,128]{3,2,1,0:T(8,128)S(1)} all-to-all(f32[8,2,8,128]{3,2,1,0:T(8,128)S(1)} %final.1), channel_id=1, replica_groups=mesh['firm_far'=4,'firm_middle'=2,'firm_near'=2,'worker'=8,'probe'=4] {'..., dimensions={0} | all-to-all | bytes 131072 | tf_op jit(solution)/shard_map/all_to_all | solution.py:364
  180.3 0.6 slice_bitcast_fusion
  (4 shorter events, 0.1 us)
Async XLA Ops:
  0.6 65.7 %copy-start.3 = (s32[1,128]{1,0:T(1,128)S(1)}, s32[1,128]{1,0:T(1,128)}, u32[]{:S(2)}) copy-start(s32[1,128]{1,0:T(1,128)} %tile_firms.5) | copy-start | bytes 1540
  0.6 65.7 %copy-start.2 = (s32[1,128]{1,0:T(1,128)S(1)}, s32[1,128]{1,0:T(1,128)}, u32[]{:S(2)}) copy-start(s32[1,128]{1,0:T(1,128)} %tile_rows.5) | copy-start | bytes 1540
  0.7 65.7 %copy-start = (s32[1,512]{1,0:T(1,128)S(1)}, s32[1,512]{1,0:T(1,128)}, u32[]{:S(2)}) copy-start(s32[1,512]{1,0:T(1,128)} %worker_ids.3) | copy-start | bytes 6148
  0.7 65.7 %copy-start.1 = (f32[1024]{0:T(1024)S(1)}, f32[1024]{0:T(1024)}, u32[]{:S(2)}) copy-start(f32[1024]{0:T(1024)} %param.11) | copy-start | bytes 12292

commit v8 on v7

--- a/solution.py
+++ b/solution.py
@@ -11,6 +11,7 @@
 SHARD_WORKERS = 128
 BITS = 30
 CHUNKS = 4
+PANEL = 16
 WORKERS = 8
 FIRMS = 16
 NEAR_FIRST = 2
@@ -106,9 +107,8 @@
     probes, lines = out.shape[1], rows.shape[1]
     size = tiles.shape[0] // CHUNKS
     for tile in range(0, tiles.shape[0], 2):
-        if wait is not None and tile % (2 * size) == 0:
+        if wait is not None and tile % size == 0:
             wait(tile // size)
-            wait(tile // size + 1)
         weights = jnp.concatenate([tiles[tile], tiles[tile + 1]], axis=1)
         both = dot(stack([rows[tile_rows[0, tile + item]] for item in range(2)]), weights, (1, 0))
         for item in range(2):
@@ -232,16 +232,16 @@
             column = jnp.where(lanes < begin, column, other)
         return column
 
-    for step in range(0, size, 2):
-        one, two = spread(step), spread(step + 1)
-        first, second = table[step : step + 1, :], table[step + 1 : step + 2, :]
-        a, b = one[step : step + 1, :], two[step : step + 1, :]
-        c, d = one[step + 1 : step + 2, :], two[step + 1 : step + 2, :]
-        inverse = 1.0 / (a * d - b * c)
-        upper = (d * first - b * second) * inverse
-        lower = (a * second - c * first) * inverse
-        table = table - one * upper - two * lower
-        table = jnp.where(lines == step, upper, jnp.where(lines == step + 1, lower, table))
+    for start in range(0, size, PANEL):
+        columns = [spread(start + item) for item in range(PANEL)]
+        for item, column in enumerate(columns):
+            at = start + item
+            inverse = 1.0 / column[at : at + 1, :]
+            line = table[at : at + 1, :] * inverse
+            table = jnp.where(lines == at, line, table - column * line)
+            for later in range(item + 1, PANEL):
+                factor = columns[later][at : at + 1, :] * inverse
+                columns[later] = jnp.where(lines == at, factor, columns[later] - column * factor)
     return table
 
 

time: 181 us -> 180 us (level)
  Pallas kernels: 14.6 us -> 12.6 us
    pallas_call x1, Pallas kernels: 5.01 us -> 3.18 us  [local(): kernel(final_body, shape(WORKERS, 2), [SMEM, VMEM, VMEM], [VMEM((2, probe...]
where the time goes in v8:
time: 180 us; the launch traced here: 179 us
  blocking collectives  165 us (92%)
  Pallas kernels  12.6 us (7%)
    all_to_all x11, blocking collectives, exchange(): got = lax.all_to_all(chunks, axis, 0, 0, tiled=True)  165 us

profile of v8, /device:TPU:1, one launch (start us, length us, event | category | flops | bytes accessed | tf_op | source)
XLA Modules:
  0.0 179.0 jit_solution(16088775421678761355)
XLA Ops:
  0.6 0.0 copy-start.3
  0.6 0.0 copy-start.2
  0.7 0.0 copy-start
  0.7 0.0 copy-start.1
  0.7 2.6 %start.1 = (f32[128,8,128]{2,1,0:T(8,128)S(1)}, bf16[128,128,128]{2,1,0:T(8,128)(2,1)S(1)}) custom-call(s32[1,128]{1,0:T(1,128)} %tile_rows.5, s32[1,128]{1,0:T(1,128)} %tile_firms.5, s32[5,4,8]{2,1,0:T(4,128)} %bitcast.21, s32[1,512]{1,0:T(1,128)} %worker_ids.3, bf16[128,128,128]{2,1,0:T(8,128)(2,1)} %tiles_hbm.1), custom_call_target="tpu_custom_call" | custom-call | flops 33554432 | bytes 1048576 | tf_op jit(solution)/shard_map/start/pallas_call | solution.py:393
  3.2 19.0 %all_to_all.55.got = f32[16,8,8,128]{3,2,1,0:T(8,128)S(1)} all-to-all(f32[16,8,8,128]{3,2,1,0:T(8,128)S(1)} %bitcast.16), channel_id=1, replica_groups=mesh['firm_far'=4,'firm_middle'=2,'firm_near'=2,'worker'=8,'probe'=4] {'..., dimensions={0} | all-to-all | bytes 1048576 | tf_op jit(solution)/shard_map/all_to_all | solution.py:364
  22.3 28.5 %all_to_all.56.got = f32[8,8,8,128]{3,2,1,0:T(8,128)S(1)} all-to-all(f32[8,8,8,128]{3,2,1,0:T(8,128)S(1)} %fold.2), channel_id=1, replica_groups=mesh['firm_far'=4,'firm_middle'=2,'firm_near'=2,'worker'=8,'probe'=4] {'..., dimensions={0} | all-to-all | bytes 524288 | tf_op jit(solution)/shard_map/all_to_all | solution.py:364
  50.9 15.3 %all_to_all.57 = bf16[16,8,8,128]{3,2,1,0:T(8,128)(2,1)S(1)} all-to-all(bf16[16,8,8,128]{3,2,1,0:T(8,128)(2,1)S(1)} %get-tuple-element.115), channel_id=1, replica_groups=mesh['firm_far'=4,'firm_middle'=2,'firm_near'=2,'worker'=8,'probe'=4] {'..., dimensions={0} | all-to-all | bytes 524288 | tf_op jit(solution)/shard_map/all_to_all | solution.py:364
  66.2 0.0 copy-done.3
  66.2 0.0 copy-done.2
  66.2 0.0 copy-done
  66.2 0.0 copy-done.1
  66.2 2.9 %middle.1 = bf16[32,5,8,128]{3,2,1,0:T(8,128)(2,1)S(1)} custom-call(s32[1,128]{1,0:T(1,128)S(1)} %copy-done.2, s32[1,128]{1,0:T(1,128)S(1)} %copy-done.3, s32[1]{0:T(128)} %bitcast.3.worker, s32[1]{0:T(128)} %bitcast.2.firm, bf16[128,8,128]{2,1,0:T(8,128)(2,1)S(1)} %bitcast.14, f32[8,8,128]{2,1,0:T(8,128)S(1)} %get-tuple-element.143.firsts, ...), custom_call_target="tpu_custom_call" | custom-call | flops 67108864 | bytes 1048576 | tf_op jit(solution)/shard_map/middle/pallas_call | solution.py:410
  69.1 17.0 %all_to_all.58.got = bf16[32,5,8,128]{3,2,1,0:T(8,128)(2,1)S(1)} all-to-all(bf16[32,5,8,128]{3,2,1,0:T(8,128)(2,1)S(1)} %middle.1), channel_id=1, replica_groups=mesh['firm_far'=4,'firm_middle'=2,'firm_near'=2,'worker'=8,'probe'=4] {'..., dimensions={0} | all-to-all | bytes 655360 | tf_op jit(solution)/shard_map/all_to_all | solution.py:364
  86.1 0.1 fold.3
  86.2 14.9 %all_to_all.59.got = f32[4,5,8,128]{3,2,1,0:T(8,128)S(1)} all-to-all(f32[4,5,8,128]{3,2,1,0:T(8,128)S(1)} %fold.3), channel_id=1, replica_groups=mesh['firm_far'=4,'firm_middle'=2,'firm_near'=2,'worker'=8,'probe'=4] {'..., dimensions={0} | all-to-all | bytes 163840 | tf_op jit(solution)/shard_map/all_to_all | solution.py:364
  101.1 0.2 second.1
  101.3 17.1 %all_to_all.60 = bf16[32,4,8,128]{3,2,1,0:T(8,128)(2,1)S(1)} all-to-all(bf16[32,4,8,128]{3,2,1,0:T(8,128)(2,1)S(1)} %get-tuple-element.150), channel_id=1, replica_groups=mesh['firm_far'=4,'firm_middle'=2,'firm_near'=2,'worker'=8,'probe'=4] {'..., dimensions={0} | all-to-all | bytes 524288 | tf_op jit(solution)/shard_map/all_to_all | solution.py:364
  118.4 2.0 %rows.1 = f32[4,7,8,128]{3,2,1,0:T(8,128)S(1)} custom-call(s32[1,128]{1,0:T(1,128)S(1)} %copy-done.2, s32[1,128]{1,0:T(1,128)S(1)} %copy-done.3, bf16[128,8,128]{2,1,0:T(8,128)(2,1)S(1)} %bitcast.15, f32[8,128]{1,0:T(8,128)S(1)} %get-tuple-element.158.first, f32[8,128]{1,0:T(8,128)S(1)} %get-tuple-element.159.second, ...), custom_call_target="tpu_custom_call" | custom-call | flops 33554432 | bytes 1048576 | tf_op jit(solution)/shard_map/rows/pallas_call | solution.py:426
  120.4 8.6 %all_to_all.61.given = f32[4,7,8,128]{3,2,1,0:T(8,128)S(1)} all-to-all(f32[4,7,8,128]{3,2,1,0:T(8,128)S(1)} %rows.1), channel_id=1, replica_groups=mesh['firm_far'=4,'firm_middle'=2,'firm_near'=2,'worker'=8,'probe'=4] {'..., dimensions={0} | all-to-all | bytes 229376 | tf_op jit(solution)/shard_map/all_to_all | solution.py:364
  129.0 1.6 last.1
  130.6 11.4 %all_to_all.62.got = bf16[8,19,8,128]{3,2,1,0:T(8,128)(2,1)S(1)} all-to-all(bf16[8,19,8,128]{3,2,1,0:T(8,128)(2,1)S(1)} %last.1), channel_id=1, replica_groups=mesh['firm_far'=4,'firm_middle'=2,'firm_near'=2,'worker'=8,'probe'=4] {'..., dimensions={0} | all-to-all | bytes 622592 | tf_op jit(solution)/shard_map/all_to_all | solution.py:364
  142.1 14.6 %all_to_all.63.got = f32[16,16,128]{2,1,0:T(8,128)S(1)} all-to-all(f32[16,16,128]{2,1,0:T(8,128)S(1)} %fold_last.1), channel_id=1, replica_groups=mesh['firm_far'=4,'firm_middle'=2,'firm_near'=2,'worker'=8,'probe'=4] {'..., dimensions={0} | all-to-all | bytes 262144 | tf_op jit(solution)/shard_map/all_to_all | solution.py:364
  156.7 6.7 %all_to_all.64 = f32[4,16,128]{2,1,0:T(8,128)S(1)} all-to-all(f32[4,16,128]{2,1,0:T(8,128)S(1)} %third.1), channel_id=1, replica_groups=mesh['firm_far'=4,'firm_middle'=2,'firm_near'=2,'worker'=8,'probe'=4] {'..., dimensions={0} | all-to-all | bytes 65536 | tf_op jit(solution)/shard_map/all_to_all | solution.py:364
  163.4 3.2 %final.1 = f32[8,2,8,128]{3,2,1,0:T(8,128)S(1)} custom-call(s32[1]{0:T(128)} %bitcast.4.probe, f32[4,7,8,128]{3,2,1,0:T(8,128)S(1)} %all_to_all.61.given, f32[4,2,8,128]{3,2,1,0:T(8,128)S(1)} %bitcast.17), custom_call_target="tpu_custom_call" | custom-call | flops 8388608 | bytes 1048576 | tf_op jit(solution)/shard_map/final/pallas_call | solution.py:448
  166.6 11.8 %all_to_all.65 = f32[8,2,8,128]{3,2,1,0:T(8,128)S(1)} all-to-all(f32[8,2,8,128]{3,2,1,0:T(8,128)S(1)} %final.1), channel_id=1, replica_groups=mesh['firm_far'=4,'firm_middle'=2,'firm_near'=2,'worker'=8,'probe'=4] {'..., dimensions={0} | all-to-all | bytes 131072 | tf_op jit(solution)/shard_map/all_to_all | solution.py:364
  178.4 0.6 slice_bitcast_fusion
  (4 shorter events, 0.1 us)
Async XLA Ops:
  0.6 65.6 %copy-start.3 = (s32[1,128]{1,0:T(1,128)S(1)}, s32[1,128]{1,0:T(1,128)}, u32[]{:S(2)}) copy-start(s32[1,128]{1,0:T(1,128)} %tile_firms.5) | copy-start | bytes 1540
  0.6 65.6 %copy-start.2 = (s32[1,128]{1,0:T(1,128)S(1)}, s32[1,128]{1,0:T(1,128)}, u32[]{:S(2)}) copy-start(s32[1,128]{1,0:T(1,128)} %tile_rows.5) | copy-start | bytes 1540
  0.7 65.5 %copy-start = (s32[1,512]{1,0:T(1,128)S(1)}, s32[1,512]{1,0:T(1,128)}, u32[]{:S(2)}) copy-start(s32[1,512]{1,0:T(1,128)} %worker_ids.3) | copy-start | bytes 6148
  0.7 65.5 %copy-start.1 = (f32[1024]{0:T(1024)S(1)}, f32[1024]{0:T(1024)}, u32[]{:S(2)}) copy-start(f32[1024]{0:T(1024)} %param.11) | copy-start | bytes 12292

commit v9 on v8

--- a/solution.py
+++ b/solution.py
@@ -15,7 +15,7 @@
 WORKERS = 8
 FIRMS = 16
 NEAR_FIRST = 2
-NEAR_SECOND = 4
+NEAR_SECOND = 2
 FIRM_AXES = ("firm_far", "firm_middle", "firm_near")
 
 largest_value = lax.Precision.HIGHEST
@@ -408,14 +408,14 @@
     field, (firsts, *at) = exchange(sent, near_first, (firsts, *at))
     firm, worker, _ = at
     parts = kernel(
-        middle_body, shape(peers_second, held_second + 1, dtype=bf16),
+        middle_body, shape(peers_second, held_second + 1),
         [SMEM, SMEM, SMEM, SMEM, VMEM, VMEM, VMEM, VMEM, VMEM], [rows_vmem, sums_vmem], "middle", 2 * cost,
     )(
         tile_rows, tile_firms, worker, firm, field.reshape(blocks, probe_dev, TILE), firsts, reg_blocks,
         worker_ids, placed(tiles, VMEM),
     )
     got, (firsts, *at) = exchange(parts, near_second, (firsts, *at))
-    sent = kernel(gather_fold_body, shape(held_second, held_second + 1), [VMEM], [], "fold")(got)
+    sent = kernel(gather_fold_body, shape(held_second, held_second + 1, dtype=bf16), [VMEM], [], "fold")(got)
     got, (firsts, *at) = exchange(sent, far_second, (firsts, *at))
     first, second, quotient, sent = kernel(
         second_body, (shape(), shape(), shape(), shape(peers_second, held_second, dtype=bf16)),

time: 180 us -> 176 us (0.978)
  blocking collectives: 165 us -> 161 us
    all_to_all x11, blocking collectives: 165 us -> 161 us  [exchange(): got = lax.all_to_all(chunks, axis, 0, 0, tiled=True)]
where the time goes in v9:
time: 176 us; the launch traced here: 175 us
  blocking collectives  161 us (91%)
  Pallas kernels  12.6 us (7%)
    all_to_all x11, blocking collectives, exchange(): got = lax.all_to_all(chunks, axis, 0, 0, tiled=True)  161 us

profile of v9, /device:TPU:1, one launch (start us, length us, event | category | flops | bytes accessed | tf_op | source)
XLA Modules:
  0.0 175.1 jit_solution(8493270169703207857)
XLA Ops:
  0.6 0.0 copy-start.3
  0.6 0.0 copy-start.2
  0.7 0.0 copy-start
  0.7 0.0 copy-start.1
  0.7 2.6 %start.1 = (f32[128,8,128]{2,1,0:T(8,128)S(1)}, bf16[128,128,128]{2,1,0:T(8,128)(2,1)S(1)}) custom-call(s32[1,128]{1,0:T(1,128)} %tile_rows.5, s32[1,128]{1,0:T(1,128)} %tile_firms.5, s32[5,4,8]{2,1,0:T(4,128)} %bitcast.21, s32[1,512]{1,0:T(1,128)} %worker_ids.3, bf16[128,128,128]{2,1,0:T(8,128)(2,1)} %tiles_hbm.1), custom_call_target="tpu_custom_call" | custom-call | flops 33554432 | bytes 1048576 | tf_op jit(solution)/shard_map/start/pallas_call | solution.py:393
  3.2 19.0 %all_to_all.55.got = f32[16,8,8,128]{3,2,1,0:T(8,128)S(1)} all-to-all(f32[16,8,8,128]{3,2,1,0:T(8,128)S(1)} %bitcast.16), channel_id=1, replica_groups=mesh['firm_far'=8,'firm_middle'=1,'firm_near'=2,'worker'=8,'probe'=4] {'..., dimensions={0} | all-to-all | bytes 1048576 | tf_op jit(solution)/shard_map/all_to_all | solution.py:364
  22.3 28.5 %all_to_all.56.got = f32[8,8,8,128]{3,2,1,0:T(8,128)S(1)} all-to-all(f32[8,8,8,128]{3,2,1,0:T(8,128)S(1)} %fold.2), channel_id=1, replica_groups=mesh['firm_far'=8,'firm_middle'=1,'firm_near'=2,'worker'=8,'probe'=4] {'..., dimensions={0} | all-to-all | bytes 524288 | tf_op jit(solution)/shard_map/all_to_all | solution.py:364
  50.9 15.3 %all_to_all.57 = bf16[16,8,8,128]{3,2,1,0:T(8,128)(2,1)S(1)} all-to-all(bf16[16,8,8,128]{3,2,1,0:T(8,128)(2,1)S(1)} %get-tuple-element.115), channel_id=1, replica_groups=mesh['firm_far'=8,'firm_middle'=1,'firm_near'=2,'worker'=8,'probe'=4] {'..., dimensions={0} | all-to-all | bytes 524288 | tf_op jit(solution)/shard_map/all_to_all | solution.py:364
  66.2 0.0 copy-done.3
  66.2 0.0 copy-done.2
  66.2 0.0 copy-done
  66.2 0.0 copy-done.1
  66.2 2.9 %middle.1 = f32[16,9,8,128]{3,2,1,0:T(8,128)S(1)} custom-call(s32[1,128]{1,0:T(1,128)S(1)} %copy-done.2, s32[1,128]{1,0:T(1,128)S(1)} %copy-done.3, s32[1]{0:T(128)} %bitcast.3.worker, s32[1]{0:T(128)} %bitcast.2.firm, bf16[128,8,128]{2,1,0:T(8,128)(2,1)S(1)} %bitcast.14, f32[8,8,128]{2,1,0:T(8,128)S(1)} %get-tuple-element.143.firsts, ...), custom_call_target="tpu_custom_call" | custom-call | flops 67108864 | bytes 1048576 | tf_op jit(solution)/shard_map/middle/pallas_call | solution.py:410
  69.1 14.6 %all_to_all.58.got = f32[16,9,8,128]{3,2,1,0:T(8,128)S(1)} all-to-all(f32[16,9,8,128]{3,2,1,0:T(8,128)S(1)} %middle.1), channel_id=1, replica_groups=mesh['firm_far'=8,'firm_middle'=1,'firm_near'=2,'worker'=8,'probe'=4] {'..., dimensions={0} | all-to-all | bytes 1179648 | tf_op jit(solution)/shard_map/all_to_all | solution.py:364
  83.8 16.2 %all_to_all.59.got = bf16[8,9,8,128]{3,2,1,0:T(8,128)(2,1)S(1)} all-to-all(bf16[8,9,8,128]{3,2,1,0:T(8,128)(2,1)S(1)} %fold.3), channel_id=1, replica_groups=mesh['firm_far'=8,'firm_middle'=1,'firm_near'=2,'worker'=8,'probe'=4] {'..., dimensions={0} | all-to-all | bytes 294912 | tf_op jit(solution)/shard_map/all_to_all | solution.py:364
  100.0 0.2 second.1
  100.1 13.7 %all_to_all.60 = bf16[16,8,8,128]{3,2,1,0:T(8,128)(2,1)S(1)} all-to-all(bf16[16,8,8,128]{3,2,1,0:T(8,128)(2,1)S(1)} %get-tuple-element.150), channel_id=1, replica_groups=mesh['firm_far'=8,'firm_middle'=1,'firm_near'=2,'worker'=8,'probe'=4] {'..., dimensions={0} | all-to-all | bytes 524288 | tf_op jit(solution)/shard_map/all_to_all | solution.py:364
  113.9 2.0 %rows.1 = f32[4,7,8,128]{3,2,1,0:T(8,128)S(1)} custom-call(s32[1,128]{1,0:T(1,128)S(1)} %copy-done.2, s32[1,128]{1,0:T(1,128)S(1)} %copy-done.3, bf16[128,8,128]{2,1,0:T(8,128)(2,1)S(1)} %bitcast.15, f32[8,128]{1,0:T(8,128)S(1)} %get-tuple-element.158.first, f32[8,128]{1,0:T(8,128)S(1)} %get-tuple-element.159.second, ...), custom_call_target="tpu_custom_call" | custom-call | flops 33554432 | bytes 1048576 | tf_op jit(solution)/shard_map/rows/pallas_call | solution.py:426
  115.9 8.6 %all_to_all.61.given = f32[4,7,8,128]{3,2,1,0:T(8,128)S(1)} all-to-all(f32[4,7,8,128]{3,2,1,0:T(8,128)S(1)} %rows.1), channel_id=1, replica_groups=mesh['firm_far'=8,'firm_middle'=1,'firm_near'=2,'worker'=8,'probe'=4] {'..., dimensions={0} | all-to-all | bytes 229376 | tf_op jit(solution)/shard_map/all_to_all | solution.py:364
  124.5 1.6 last.1
  126.1 12.1 %all_to_all.62.got = bf16[8,19,8,128]{3,2,1,0:T(8,128)(2,1)S(1)} all-to-all(bf16[8,19,8,128]{3,2,1,0:T(8,128)(2,1)S(1)} %last.1), channel_id=1, replica_groups=mesh['firm_far'=8,'firm_middle'=1,'firm_near'=2,'worker'=8,'probe'=4] {'..., dimensions={0} | all-to-all | bytes 622592 | tf_op jit(solution)/shard_map/all_to_all | solution.py:364
  138.3 14.6 %all_to_all.63.got = f32[16,16,128]{2,1,0:T(8,128)S(1)} all-to-all(f32[16,16,128]{2,1,0:T(8,128)S(1)} %fold_last.1), channel_id=1, replica_groups=mesh['firm_far'=8,'firm_middle'=1,'firm_near'=2,'worker'=8,'probe'=4] {'..., dimensions={0} | all-to-all | bytes 262144 | tf_op jit(solution)/shard_map/all_to_all | solution.py:364
  152.9 6.7 %all_to_all.64 = f32[4,16,128]{2,1,0:T(8,128)S(1)} all-to-all(f32[4,16,128]{2,1,0:T(8,128)S(1)} %third.1), channel_id=1, replica_groups=mesh['firm_far'=8,'firm_middle'=1,'firm_near'=2,'worker'=8,'probe'=4] {'..., dimensions={0} | all-to-all | bytes 65536 | tf_op jit(solution)/shard_map/all_to_all | solution.py:364
  159.5 3.2 %final.1 = f32[8,2,8,128]{3,2,1,0:T(8,128)S(1)} custom-call(s32[1]{0:T(128)} %bitcast.4.probe, f32[4,7,8,128]{3,2,1,0:T(8,128)S(1)} %all_to_all.61.given, f32[4,2,8,128]{3,2,1,0:T(8,128)S(1)} %bitcast.17), custom_call_target="tpu_custom_call" | custom-call | flops 8388608 | bytes 1048576 | tf_op jit(solution)/shard_map/final/pallas_call | solution.py:448
  162.7 11.7 %all_to_all.65 = f32[8,2,8,128]{3,2,1,0:T(8,128)S(1)} all-to-all(f32[8,2,8,128]{3,2,1,0:T(8,128)S(1)} %final.1), channel_id=1, replica_groups=mesh['firm_far'=8,'firm_middle'=1,'firm_near'=2,'worker'=8,'probe'=4] {'..., dimensions={0} | all-to-all | bytes 131072 | tf_op jit(solution)/shard_map/all_to_all | solution.py:364
  174.4 0.6 slice_bitcast_fusion
  (5 shorter events, 0.2 us)
Async XLA Ops:
  0.6 65.6 %copy-start.3 = (s32[1,128]{1,0:T(1,128)S(1)}, s32[1,128]{1,0:T(1,128)}, u32[]{:S(2)}) copy-start(s32[1,128]{1,0:T(1,128)} %tile_firms.5) | copy-start | bytes 1540
  0.6 65.5 %copy-start.2 = (s32[1,128]{1,0:T(1,128)S(1)}, s32[1,128]{1,0:T(1,128)}, u32[]{:S(2)}) copy-start(s32[1,128]{1,0:T(1,128)} %tile_rows.5) | copy-start | bytes 1540
  0.7 65.5 %copy-start = (s32[1,512]{1,0:T(1,128)S(1)}, s32[1,512]{1,0:T(1,128)}, u32[]{:S(2)}) copy-start(s32[1,512]{1,0:T(1,128)} %worker_ids.3) | copy-start | bytes 6148
  0.7 65.5 %copy-start.1 = (f32[1024]{0:T(1024)S(1)}, f32[1024]{0:T(1024)}, u32[]{:S(2)}) copy-start(f32[1024]{0:T(1024)} %param.11) | copy-start | bytes 12292

commit v10 on v9

--- a/solution.py
+++ b/solution.py
@@ -245,9 +245,9 @@
     return table
 
 
-def final_body(probe, given, last, out, scratch):
+def final_body(probe, given, last, solution_out, residual_out, basis, mixes):
     size = given.shape[0] * given.shape[2]
-    gather = lambda ref, item: jnp.concatenate([ref[other, item] for other in range(ref.shape[0])], axis=0)
+    gather = lambda ref, item: jnp.concatenate([ref[other, item] for other in range(given.shape[0])], axis=0)
     half = lambda matrix: 0.5 * (matrix + matrix.T)
     lines = lax.broadcasted_iota(jnp.int32, (size, size), 0)
     lanes = lax.broadcasted_iota(jnp.int32, (size, size), 1)
@@ -282,16 +282,20 @@
     moved = exact(mix, step_second, (1, 0))
     moved_first, moved_second = moved[:size], moved[size:]
     image = scale * moved_first
-    basis = jnp.concatenate([gather(given, 0), gather(given, 1), gather(last, 0)], axis=0)
-    scratch[0] = exact(jnp.concatenate([step_first + moved_first, moved_second], axis=0), basis[: 2 * size], (0, 0))
-    scratch[1] = exact(
-        jnp.concatenate([onto_first - image, onto_second + image, -moved_second], axis=0), basis, (0, 0)
-    )
     probes = given.shape[2]
+    for other in range(last.shape[0]):
+        worker, part = other // given.shape[0], other % given.shape[0]
+        for item, kind in enumerate((2, 3, 0)):
+            line = item * size + part * probes
+            basis[line : line + probes, worker * TILE : (worker + 1) * TILE] = last[other, kind]
+    empty = jnp.zeros((size, size), f32)
+    mixes[0] = jnp.concatenate([step_first + moved_first, moved_second, empty, empty], axis=0).T
+    mixes[1] = jnp.concatenate([onto_first - image, onto_second + image, -moved_second, empty], axis=0).T
     begin = pl.multiple_of(probe[0] * probes, probes)
-    for worker in range(out.shape[0]):
-        out[worker, 0] = scratch[0, pl.ds(begin, probes), :]
-        out[worker, 1] = scratch[1, pl.ds(begin, probes), :]
+    both = jnp.concatenate([mixes[item, pl.ds(begin, probes), :][:, : 3 * size] for item in range(2)], axis=0)
+    outs = exact(both, basis[...], (1, 0))
+    solution_out[...] = outs[:probes]
+    residual_out[...] = outs[probes:]
 
 
 def fold_body(got, out):
@@ -342,8 +346,14 @@
     send(sent, seconds[...])
 
 
-def third_body(got, sent):
-    send(sent, sum_of(got))
+def third_body(got, first, second, sent):
+    total = sum_of(got)
+    probes = first.shape[0]
+    for other in range(sent.shape[0]):
+        sent[other, 0] = total[:probes]
+        sent[other, 1] = total[probes:]
+        sent[other, 2] = first[...]
+        sent[other, 3] = second[...]
 
 
 def kernel(body, shapes, places, scratch, name, cost=1 << 16):
@@ -429,29 +439,26 @@
         tile_rows, tile_firms, field.reshape(blocks, probe_dev, TILE), first, second, quotient, worker_ids,
         placed(tiles, VMEM),
     )
-    given, at = exchange(sent, "probe", at)
+    given, (first, second, *at) = exchange(sent, "probe", (first, second, *at))
     firm, worker, probe = at
     parts = kernel(
         last_body, shape(WORKERS, FIRMS + 3, dtype=bf16),
         [SMEM, SMEM, SMEM, SMEM, SMEM, VMEM, VMEM, VMEM],
         [VMEM((ROWB_DEV, 2 * probe_dev, TILE), f32), sums_vmem], "last", cost,
     )(tile_rows, tile_firms, worker, firm, probe, given, reg_blocks, placed(tiles, VMEM))
-    got, (given, *at) = exchange(parts, "worker", (given, *at))
+    got, (first, second, given, *at) = exchange(parts, "worker", (first, second, given, *at))
     sent = kernel(
         fold_body, jax.ShapeDtypeStruct((FIRMS, 2 * probe_dev, TILE), f32), [VMEM], [], "fold_last"
     )(got)
-    got, (given, *at) = exchange(sent, FIRM_AXES, (given, *at))
-    sent = kernel(
-        third_body, jax.ShapeDtypeStruct((probes, 2 * probe_dev, TILE), f32), [VMEM], [], "third"
-    )(got)
-    last, (given, *at) = exchange(sent, "probe", (given, *at))
-    outs = kernel(
-        final_body, shape(WORKERS, 2), [SMEM, VMEM, VMEM],
-        [VMEM((2, probes * probe_dev, TILE), f32)], "final", cost // 4,
-    )(at[2], given, last.reshape(probes, 2, probe_dev, TILE))
-    outs, _ = exchange(outs, "worker")
-    outs = jnp.transpose(outs, (1, 2, 0, 3)).reshape(2, probe_dev, WORKERS * TILE)
-    return (outs[0], outs[1])
+    got, (first, second, given, *at) = exchange(sent, FIRM_AXES, (first, second, given, *at))
+    sent = kernel(third_body, shape(WORKERS * probes, 4), [VMEM, VMEM, VMEM], [], "third")(got, first, second)
+    last, (given, *at) = exchange(sent, ("worker", "probe"), (given, *at))
+    out = jax.ShapeDtypeStruct((probe_dev, WORKERS * TILE), f32)
+    total = probes * probe_dev
+    return kernel(
+        final_body, (out, out), [SMEM, VMEM, VMEM],
+        [VMEM((3 * total, WORKERS * TILE), f32), VMEM((2, total, 4 * total), f32)], "final", cost // 4,
+    )(at[2], given, last)
 
 
 def solution(mesh):

time: 176 us -> 175 us (level)
    all_to_all x11 -> x10, blocking collectives: 161 us -> 160 us  [exchange(): got = lax.all_to_all(chunks, axis, 0, 0, tiled=True)]
where the time goes in v10:
time: 175 us
  blocking collectives  160 us (91%)
  Pallas kernels  13.5 us (8%)
    all_to_all x10, blocking collectives, exchange(): got = lax.all_to_all(chunks, axis, 0, 0, tiled=True)  160 us
    pallas_call x1, Pallas kernels, local(): kernel(final_body, (out, out), [SMEM, VMEM, VMEM], [VMEM((3 * total, WORK...  4 us

profile of v10, /device:TPU:1, one launch (start us, length us, event | category | flops | bytes accessed | tf_op | source)
XLA Modules:
  0.0 174.7 jit_solution(14463140480654459217)
XLA Ops:
  0.6 0.0 copy-start.3
  0.6 0.0 copy-start.2
  0.7 0.0 copy-start
  0.7 0.0 copy-start.1
  0.7 2.6 %start.1 = (f32[128,8,128]{2,1,0:T(8,128)S(1)}, bf16[128,128,128]{2,1,0:T(8,128)(2,1)S(1)}) custom-call(s32[1,128]{1,0:T(1,128)} %tile_rows.5, s32[1,128]{1,0:T(1,128)} %tile_firms.5, s32[5,4,8]{2,1,0:T(4,128)} %bitcast.13, s32[1,512]{1,0:T(1,128)} %worker_ids.3, bf16[128,128,128]{2,1,0:T(8,128)(2,1)} %tiles_hbm.1), custom_call_target="tpu_custom_call" | custom-call | flops 33554432 | bytes 1048576 | tf_op jit(solution)/shard_map/start/pallas_call | solution.py:403
  3.3 19.0 %all_to_all.50.got = f32[16,8,8,128]{3,2,1,0:T(8,128)S(1)} all-to-all(f32[16,8,8,128]{3,2,1,0:T(8,128)S(1)} %bitcast.10), channel_id=1, replica_groups=mesh['firm_far'=8,'firm_middle'=1,'firm_near'=2,'worker'=8,'probe'=4] {'..., dimensions={0} | all-to-all | bytes 1048576 | tf_op jit(solution)/shard_map/all_to_all | solution.py:374
  22.3 28.5 %all_to_all.51.got = f32[8,8,8,128]{3,2,1,0:T(8,128)S(1)} all-to-all(f32[8,8,8,128]{3,2,1,0:T(8,128)S(1)} %fold.2), channel_id=1, replica_groups=mesh['firm_far'=8,'firm_middle'=1,'firm_near'=2,'worker'=8,'probe'=4] {'..., dimensions={0} | all-to-all | bytes 524288 | tf_op jit(solution)/shard_map/all_to_all | solution.py:374
  50.9 15.3 %all_to_all.52 = bf16[16,8,8,128]{3,2,1,0:T(8,128)(2,1)S(1)} all-to-all(bf16[16,8,8,128]{3,2,1,0:T(8,128)(2,1)S(1)} %get-tuple-element.127), channel_id=1, replica_groups=mesh['firm_far'=8,'firm_middle'=1,'firm_near'=2,'worker'=8,'probe'=4] {'..., dimensions={0} | all-to-all | bytes 524288 | tf_op jit(solution)/shard_map/all_to_all | solution.py:374
  66.2 0.0 copy-done.3
  66.2 0.0 copy-done.2
  66.2 0.0 copy-done
  66.2 0.0 copy-done.1
  66.2 2.9 %middle.1 = f32[16,9,8,128]{3,2,1,0:T(8,128)S(1)} custom-call(s32[1,128]{1,0:T(1,128)S(1)} %copy-done.2, s32[1,128]{1,0:T(1,128)S(1)} %copy-done.3, s32[1]{0:T(128)} %bitcast.3.worker, s32[1]{0:T(128)} %bitcast.2.firm, bf16[128,8,128]{2,1,0:T(8,128)(2,1)S(1)} %bitcast.8, f32[8,8,128]{2,1,0:T(8,128)S(1)} %get-tuple-element.155.firsts, f32[8,128]{1,0:T(8,128)S(1)} %bitcast.11, ...), custom_call_target="tpu_custom_call" | custom-call | flops 67108864 | bytes 1048576 | tf_op jit(solution)/shard_map/middle/pallas_call | solution.py:420
  69.1 14.6 %all_to_all.53.got = f32[16,9,8,128]{3,2,1,0:T(8,128)S(1)} all-to-all(f32[16,9,8,128]{3,2,1,0:T(8,128)S(1)} %middle.1), channel_id=1, replica_groups=mesh['firm_far'=8,'firm_middle'=1,'firm_near'=2,'worker'=8,'probe'=4] {'..., dimensions={0} | all-to-all | bytes 1179648 | tf_op jit(solution)/shard_map/all_to_all | solution.py:374
  83.8 16.2 %all_to_all.54.got = bf16[8,9,8,128]{3,2,1,0:T(8,128)(2,1)S(1)} all-to-all(bf16[8,9,8,128]{3,2,1,0:T(8,128)(2,1)S(1)} %fold.3), channel_id=1, replica_groups=mesh['firm_far'=8,'firm_middle'=1,'firm_near'=2,'worker'=8,'probe'=4] {'..., dimensions={0} | all-to-all | bytes 294912 | tf_op jit(solution)/shard_map/all_to_all | solution.py:374
  100.0 0.2 second.1
  100.1 13.7 %all_to_all.55 = bf16[16,8,8,128]{3,2,1,0:T(8,128)(2,1)S(1)} all-to-all(bf16[16,8,8,128]{3,2,1,0:T(8,128)(2,1)S(1)} %get-tuple-element.162), channel_id=1, replica_groups=mesh['firm_far'=8,'firm_middle'=1,'firm_near'=2,'worker'=8,'probe'=4] {'..., dimensions={0} | all-to-all | bytes 524288 | tf_op jit(solution)/shard_map/all_to_all | solution.py:374
  113.9 2.0 %rows.1 = f32[4,7,8,128]{3,2,1,0:T(8,128)S(1)} custom-call(s32[1,128]{1,0:T(1,128)S(1)} %copy-done.2, s32[1,128]{1,0:T(1,128)S(1)} %copy-done.3, bf16[128,8,128]{2,1,0:T(8,128)(2,1)S(1)} %bitcast.9, f32[8,128]{1,0:T(8,128)S(1)} %get-tuple-element.204.first, f32[8,128]{1,0:T(8,128)S(1)} %get-tuple-element.205.second, ...), custom_call_target="tpu_custom_call" | custom-call | flops 33554432 | bytes 1048576 | tf_op jit(solution)/shard_map/rows/pallas_call | solution.py:436
  115.9 8.6 %all_to_all.56.given = f32[4,7,8,128]{3,2,1,0:T(8,128)S(1)} all-to-all(f32[4,7,8,128]{3,2,1,0:T(8,128)S(1)} %rows.1), channel_id=1, replica_groups=mesh['firm_far'=8,'firm_middle'=1,'firm_near'=2,'worker'=8,'probe'=4] {'..., dimensions={0} | all-to-all | bytes 229376 | tf_op jit(solution)/shard_map/all_to_all | solution.py:374
  124.5 1.6 last.1
  126.1 12.1 %all_to_all.57.got = bf16[8,19,8,128]{3,2,1,0:T(8,128)(2,1)S(1)} all-to-all(bf16[8,19,8,128]{3,2,1,0:T(8,128)(2,1)S(1)} %last.1), channel_id=1, replica_groups=mesh['firm_far'=8,'firm_middle'=1,'firm_near'=2,'worker'=8,'probe'=4] {'..., dimensions={0} | all-to-all | bytes 622592 | tf_op jit(solution)/shard_map/all_to_all | solution.py:374
  138.3 14.6 %all_to_all.58.got = f32[16,16,128]{2,1,0:T(8,128)S(1)} all-to-all(f32[16,16,128]{2,1,0:T(8,128)S(1)} %fold_last.1), channel_id=1, replica_groups=mesh['firm_far'=8,'firm_middle'=1,'firm_near'=2,'worker'=8,'probe'=4] {'..., dimensions={0} | all-to-all | bytes 262144 | tf_op jit(solution)/shard_map/all_to_all | solution.py:374
  152.9 0.1 third.1
  152.9 17.7 %all_to_all.59.last = f32[32,4,8,128]{3,2,1,0:T(8,128)S(1)} all-to-all(f32[32,4,8,128]{3,2,1,0:T(8,128)S(1)} %third.1), channel_id=1, replica_groups=mesh['firm_far'=8,'firm_middle'=1,'firm_near'=2,'worker'=8,'probe'=4] {'..., dimensions={0} | all-to-all | bytes 1048576 | tf_op jit(solution)/shard_map/all_to_all | solution.py:374
  170.7 4.0 %final.1 = (f32[8,1024]{1,0:T(8,128)}, f32[8,1024]{1,0:T(8,128)}) custom-call(s32[1]{0:T(128)} %bitcast.4.probe, f32[4,7,8,128]{3,2,1,0:T(8,128)S(1)} %all_to_all.56.given, f32[32,4,8,128]{3,2,1,0:T(8,128)S(1)} %all_to_all.59.last), custom_call_target="tpu_custom_call" | custom-call | flops 8388608 | bytes 1048576 | tf_op jit(solution)/shard_map/final/pallas_call | solution.py:458
  (4 shorter events, 0.2 us)
Async XLA Ops:
  0.6 65.6 %copy-start.3 = (s32[1,128]{1,0:T(1,128)S(1)}, s32[1,128]{1,0:T(1,128)}, u32[]{:S(2)}) copy-start(s32[1,128]{1,0:T(1,128)} %tile_firms.5) | copy-start | bytes 1540
  0.6 65.5 %copy-start.2 = (s32[1,128]{1,0:T(1,128)S(1)}, s32[1,128]{1,0:T(1,128)}, u32[]{:S(2)}) copy-start(s32[1,128]{1,0:T(1,128)} %tile_rows.5) | copy-start | bytes 1540
  0.7 65.5 %copy-start = (s32[1,512]{1,0:T(1,128)S(1)}, s32[1,512]{1,0:T(1,128)}, u32[]{:S(2)}) copy-start(s32[1,512]{1,0:T(1,128)} %worker_ids.3) | copy-start | bytes 6148
  0.7 65.5 %copy-start.1 = (f32[1024]{0:T(1024)S(1)}, f32[1024]{0:T(1024)}, u32[]{:S(2)}) copy-start(f32[1024]{0:T(1024)} %param.11) | copy-start | bytes 12292

commit v11 on v10

--- a/solution.py
+++ b/solution.py
@@ -215,9 +215,9 @@
         ],
         axis=1,
     )
-    adjoint(tile_rows, tile_firms, rows, tiles, feature_sums, 1)
-    add_ridge(feature_sums, firm[0], worker[0], 1, regular, second)
-    put_parts(out, feature_sums, three_parts(extra))
+    adjoint(tile_rows, tile_firms, rows, tiles, feature_sums, NEAR_FIRST)
+    add_ridge(feature_sums, firm[0], worker[0], NEAR_FIRST, regular, second)
+    put_parts(out, feature_sums, [extra])
 
 
 def eliminate(table, pivots):
@@ -442,15 +442,15 @@
     given, (first, second, *at) = exchange(sent, "probe", (first, second, *at))
     firm, worker, probe = at
     parts = kernel(
-        last_body, shape(WORKERS, FIRMS + 3, dtype=bf16),
+        last_body, shape(peers_first, held_first + 1),
         [SMEM, SMEM, SMEM, SMEM, SMEM, VMEM, VMEM, VMEM],
         [VMEM((ROWB_DEV, 2 * probe_dev, TILE), f32), sums_vmem], "last", cost,
     )(tile_rows, tile_firms, worker, firm, probe, given, reg_blocks, placed(tiles, VMEM))
-    got, (first, second, given, *at) = exchange(parts, "worker", (first, second, given, *at))
+    got, (first, second, given, *at) = exchange(parts, near_first, (first, second, given, *at))
     sent = kernel(
-        fold_body, jax.ShapeDtypeStruct((FIRMS, 2 * probe_dev, TILE), f32), [VMEM], [], "fold_last"
+        fold_body, jax.ShapeDtypeStruct((held_first, 2 * probe_dev, TILE), f32), [VMEM], [], "fold_last"
     )(got)
-    got, (first, second, given, *at) = exchange(sent, FIRM_AXES, (first, second, given, *at))
+    got, (first, second, given, *at) = exchange(sent, far_first, (first, second, given, *at))
     sent = kernel(third_body, shape(WORKERS * probes, 4), [VMEM, VMEM, VMEM], [], "third")(got, first, second)
     last, (given, *at) = exchange(sent, ("worker", "probe"), (given, *at))
     out = jax.ShapeDtypeStruct((probe_dev, WORKERS * TILE), f32)

time: 175 us -> 178 us (1.017)
  blocking collectives: 160 us -> 163 us
    all_to_all x10, blocking collectives: 160 us -> 163 us  [exchange(): got = lax.all_to_all(chunks, axis, 0, 0, tiled=True)]
where the time goes in v11:
time: 178 us; the launch traced here: 177 us
  blocking collectives  163 us (92%)
  Pallas kernels  13.5 us (8%)
    all_to_all x10, blocking collectives, exchange(): got = lax.all_to_all(chunks, axis, 0, 0, tiled=True)  163 us
    pallas_call x1, Pallas kernels, local(): kernel(final_body, (out, out), [SMEM, VMEM, VMEM], [VMEM((3 * total, WORK...  4 us

profile of v11, /device:TPU:1, one launch (start us, length us, event | category | flops | bytes accessed | tf_op | source)
XLA Modules:
  0.0 177.4 jit_solution(6950620670937085029)
XLA Ops:
  0.6 0.0 copy-start.3
  0.6 0.0 copy-start.2
  0.7 0.0 copy-start
  0.7 0.0 copy-start.1
  0.7 2.6 %start.1 = (f32[128,8,128]{2,1,0:T(8,128)S(1)}, bf16[128,128,128]{2,1,0:T(8,128)(2,1)S(1)}) custom-call(s32[1,128]{1,0:T(1,128)} %tile_rows.5, s32[1,128]{1,0:T(1,128)} %tile_firms.5, s32[5,4,8]{2,1,0:T(4,128)} %bitcast.13, s32[1,512]{1,0:T(1,128)} %worker_ids.3, bf16[128,128,128]{2,1,0:T(8,128)(2,1)} %tiles_hbm.1), custom_call_target="tpu_custom_call" | custom-call | flops 33554432 | bytes 1048576 | tf_op jit(solution)/shard_map/start/pallas_call | solution.py:403
  3.2 19.0 %all_to_all.50.got = f32[16,8,8,128]{3,2,1,0:T(8,128)S(1)} all-to-all(f32[16,8,8,128]{3,2,1,0:T(8,128)S(1)} %bitcast.10), channel_id=1, replica_groups=mesh['firm_far'=8,'firm_middle'=1,'firm_near'=2,'worker'=8,'probe'=4] {'..., dimensions={0} | all-to-all | bytes 1048576 | tf_op jit(solution)/shard_map/all_to_all | solution.py:374
  22.3 28.5 %all_to_all.51.got = f32[8,8,8,128]{3,2,1,0:T(8,128)S(1)} all-to-all(f32[8,8,8,128]{3,2,1,0:T(8,128)S(1)} %fold.2), channel_id=1, replica_groups=mesh['firm_far'=8,'firm_middle'=1,'firm_near'=2,'worker'=8,'probe'=4] {'..., dimensions={0} | all-to-all | bytes 524288 | tf_op jit(solution)/shard_map/all_to_all | solution.py:374
  50.9 15.3 %all_to_all.52 = bf16[16,8,8,128]{3,2,1,0:T(8,128)(2,1)S(1)} all-to-all(bf16[16,8,8,128]{3,2,1,0:T(8,128)(2,1)S(1)} %get-tuple-element.127), channel_id=1, replica_groups=mesh['firm_far'=8,'firm_middle'=1,'firm_near'=2,'worker'=8,'probe'=4] {'..., dimensions={0} | all-to-all | bytes 524288 | tf_op jit(solution)/shard_map/all_to_all | solution.py:374
  66.2 0.0 copy-done.3
  66.2 0.0 copy-done.2
  66.2 0.0 copy-done
  66.2 0.0 copy-done.1
  66.2 2.9 %middle.1 = f32[16,9,8,128]{3,2,1,0:T(8,128)S(1)} custom-call(s32[1,128]{1,0:T(1,128)S(1)} %copy-done.2, s32[1,128]{1,0:T(1,128)S(1)} %copy-done.3, s32[1]{0:T(128)} %bitcast.3.worker, s32[1]{0:T(128)} %bitcast.2.firm, bf16[128,8,128]{2,1,0:T(8,128)(2,1)S(1)} %bitcast.8, f32[8,8,128]{2,1,0:T(8,128)S(1)} %get-tuple-element.155.firsts, f32[8,128]{1,0:T(8,128)S(1)} %bitcast.11, ...), custom_call_target="tpu_custom_call" | custom-call | flops 67108864 | bytes 1048576 | tf_op jit(solution)/shard_map/middle/pallas_call | solution.py:420
  69.1 14.6 %all_to_all.53.got = f32[16,9,8,128]{3,2,1,0:T(8,128)S(1)} all-to-all(f32[16,9,8,128]{3,2,1,0:T(8,128)S(1)} %middle.1), channel_id=1, replica_groups=mesh['firm_far'=8,'firm_middle'=1,'firm_near'=2,'worker'=8,'probe'=4] {'..., dimensions={0} | all-to-all | bytes 1179648 | tf_op jit(solution)/shard_map/all_to_all | solution.py:374
  83.8 16.2 %all_to_all.54.got = bf16[8,9,8,128]{3,2,1,0:T(8,128)(2,1)S(1)} all-to-all(bf16[8,9,8,128]{3,2,1,0:T(8,128)(2,1)S(1)} %fold.3), channel_id=1, replica_groups=mesh['firm_far'=8,'firm_middle'=1,'firm_near'=2,'worker'=8,'probe'=4] {'..., dimensions={0} | all-to-all | bytes 294912 | tf_op jit(solution)/shard_map/all_to_all | solution.py:374
  100.0 0.2 second.1
  100.1 13.7 %all_to_all.55 = bf16[16,8,8,128]{3,2,1,0:T(8,128)(2,1)S(1)} all-to-all(bf16[16,8,8,128]{3,2,1,0:T(8,128)(2,1)S(1)} %get-tuple-element.162), channel_id=1, replica_groups=mesh['firm_far'=8,'firm_middle'=1,'firm_near'=2,'worker'=8,'probe'=4] {'..., dimensions={0} | all-to-all | bytes 524288 | tf_op jit(solution)/shard_map/all_to_all | solution.py:374
  113.9 2.0 %rows.1 = f32[4,7,8,128]{3,2,1,0:T(8,128)S(1)} custom-call(s32[1,128]{1,0:T(1,128)S(1)} %copy-done.2, s32[1,128]{1,0:T(1,128)S(1)} %copy-done.3, bf16[128,8,128]{2,1,0:T(8,128)(2,1)S(1)} %bitcast.9, f32[8,128]{1,0:T(8,128)S(1)} %get-tuple-element.204.first, f32[8,128]{1,0:T(8,128)S(1)} %get-tuple-element.205.second, ...), custom_call_target="tpu_custom_call" | custom-call | flops 33554432 | bytes 1048576 | tf_op jit(solution)/shard_map/rows/pallas_call | solution.py:436
  115.9 8.6 %all_to_all.56.given = f32[4,7,8,128]{3,2,1,0:T(8,128)S(1)} all-to-all(f32[4,7,8,128]{3,2,1,0:T(8,128)S(1)} %rows.1), channel_id=1, replica_groups=mesh['firm_far'=8,'firm_middle'=1,'firm_near'=2,'worker'=8,'probe'=4] {'..., dimensions={0} | all-to-all | bytes 229376 | tf_op jit(solution)/shard_map/all_to_all | solution.py:374
  124.5 1.6 last.1
  126.1 16.1 %all_to_all.57.got = f32[16,9,8,128]{3,2,1,0:T(8,128)S(1)} all-to-all(f32[16,9,8,128]{3,2,1,0:T(8,128)S(1)} %last.1), channel_id=1, replica_groups=mesh['firm_far'=8,'firm_middle'=1,'firm_near'=2,'worker'=8,'probe'=4] {'..., dimensions={0} | all-to-all | bytes 1179648 | tf_op jit(solution)/shard_map/all_to_all | solution.py:374
  142.2 14.7 %all_to_all.58.got = f32[8,16,128]{2,1,0:T(8,128)S(1)} all-to-all(f32[8,16,128]{2,1,0:T(8,128)S(1)} %fold_last.1), channel_id=1, replica_groups=mesh['firm_far'=8,'firm_middle'=1,'firm_near'=2,'worker'=8,'probe'=4] {'..., dimensions={0} | all-to-all | bytes 131072 | tf_op jit(solution)/shard_map/all_to_all | solution.py:374
  156.9 16.5 %all_to_all.59.last = f32[32,4,8,128]{3,2,1,0:T(8,128)S(1)} all-to-all(f32[32,4,8,128]{3,2,1,0:T(8,128)S(1)} %third.1), channel_id=1, replica_groups=mesh['firm_far'=8,'firm_middle'=1,'firm_near'=2,'worker'=8,'probe'=4] {'..., dimensions={0} | all-to-all | bytes 1048576 | tf_op jit(solution)/shard_map/all_to_all | solution.py:374
  173.4 4.0 %final.1 = (f32[8,1024]{1,0:T(8,128)}, f32[8,1024]{1,0:T(8,128)}) custom-call(s32[1]{0:T(128)} %bitcast.4.probe, f32[4,7,8,128]{3,2,1,0:T(8,128)S(1)} %all_to_all.56.given, f32[32,4,8,128]{3,2,1,0:T(8,128)S(1)} %all_to_all.59.last), custom_call_target="tpu_custom_call" | custom-call | flops 8388608 | bytes 1048576 | tf_op jit(solution)/shard_map/final/pallas_call | solution.py:458
  (5 shorter events, 0.2 us)
Async XLA Ops:
  0.6 65.6 %copy-start.3 = (s32[1,128]{1,0:T(1,128)S(1)}, s32[1,128]{1,0:T(1,128)}, u32[]{:S(2)}) copy-start(s32[1,128]{1,0:T(1,128)} %tile_firms.5) | copy-start | bytes 1540
  0.6 65.5 %copy-start.2 = (s32[1,128]{1,0:T(1,128)S(1)}, s32[1,128]{1,0:T(1,128)}, u32[]{:S(2)}) copy-start(s32[1,128]{1,0:T(1,128)} %tile_rows.5) | copy-start | bytes 1540
  0.7 65.5 %copy-start = (s32[1,512]{1,0:T(1,128)S(1)}, s32[1,512]{1,0:T(1,128)}, u32[]{:S(2)}) copy-start(s32[1,512]{1,0:T(1,128)} %worker_ids.3) | copy-start | bytes 6148
  0.7 65.5 %copy-start.1 = (f32[1024]{0:T(1024)S(1)}, f32[1024]{0:T(1024)}, u32[]{:S(2)}) copy-start(f32[1024]{0:T(1024)} %param.11) | copy-start | bytes 12292

commit v12 on v11

--- a/solution.py
+++ b/solution.py
@@ -217,7 +217,7 @@
     )
     adjoint(tile_rows, tile_firms, rows, tiles, feature_sums, NEAR_FIRST)
     add_ridge(feature_sums, firm[0], worker[0], NEAR_FIRST, regular, second)
-    put_parts(out, feature_sums, [extra])
+    put_parts(out, feature_sums, three_parts(extra))
 
 
 def eliminate(table, pivots):
@@ -442,7 +442,7 @@
     given, (first, second, *at) = exchange(sent, "probe", (first, second, *at))
     firm, worker, probe = at
     parts = kernel(
-        last_body, shape(peers_first, held_first + 1),
+        last_body, shape(peers_first, held_first + 3, dtype=bf16),
         [SMEM, SMEM, SMEM, SMEM, SMEM, VMEM, VMEM, VMEM],
         [VMEM((ROWB_DEV, 2 * probe_dev, TILE), f32), sums_vmem], "last", cost,
     )(tile_rows, tile_firms, worker, firm, probe, given, reg_blocks, placed(tiles, VMEM))

time: 178 us -> 175 us (0.983)
  blocking collectives: 163 us -> 160 us
    all_to_all x10, blocking collectives: 163 us -> 160 us  [exchange(): got = lax.all_to_all(chunks, axis, 0, 0, tiled=True)]
where the time goes in v12:
time: 175 us
  blocking collectives  160 us (91%)
  Pallas kernels  13.5 us (8%)
    all_to_all x10, blocking collectives, exchange(): got = lax.all_to_all(chunks, axis, 0, 0, tiled=True)  160 us
    pallas_call x1, Pallas kernels, local(): kernel(final_body, (out, out), [SMEM, VMEM, VMEM], [VMEM((3 * total, WORK...  4 us

profile of v12, /device:TPU:1, one launch (start us, length us, event | category | flops | bytes accessed | tf_op | source)
XLA Modules:
  0.0 174.6 jit_solution(11810639764352349605)
XLA Ops:
  0.6 0.0 copy-start.3
  0.6 0.0 copy-start.2
  0.7 0.0 copy-start
  0.7 0.0 copy-start.1
  0.7 2.6 %start.1 = (f32[128,8,128]{2,1,0:T(8,128)S(1)}, bf16[128,128,128]{2,1,0:T(8,128)(2,1)S(1)}) custom-call(s32[1,128]{1,0:T(1,128)} %tile_rows.5, s32[1,128]{1,0:T(1,128)} %tile_firms.5, s32[5,4,8]{2,1,0:T(4,128)} %bitcast.13, s32[1,512]{1,0:T(1,128)} %worker_ids.3, bf16[128,128,128]{2,1,0:T(8,128)(2,1)} %tiles_hbm.1), custom_call_target="tpu_custom_call" | custom-call | flops 33554432 | bytes 1048576 | tf_op jit(solution)/shard_map/start/pallas_call | solution.py:403
  3.2 19.0 %all_to_all.50.got = f32[16,8,8,128]{3,2,1,0:T(8,128)S(1)} all-to-all(f32[16,8,8,128]{3,2,1,0:T(8,128)S(1)} %bitcast.10), channel_id=1, replica_groups=mesh['firm_far'=8,'firm_middle'=1,'firm_near'=2,'worker'=8,'probe'=4] {'..., dimensions={0} | all-to-all | bytes 1048576 | tf_op jit(solution)/shard_map/all_to_all | solution.py:374
  22.3 28.5 %all_to_all.51.got = f32[8,8,8,128]{3,2,1,0:T(8,128)S(1)} all-to-all(f32[8,8,8,128]{3,2,1,0:T(8,128)S(1)} %fold.2), channel_id=1, replica_groups=mesh['firm_far'=8,'firm_middle'=1,'firm_near'=2,'worker'=8,'probe'=4] {'..., dimensions={0} | all-to-all | bytes 524288 | tf_op jit(solution)/shard_map/all_to_all | solution.py:374
  50.9 15.3 %all_to_all.52 = bf16[16,8,8,128]{3,2,1,0:T(8,128)(2,1)S(1)} all-to-all(bf16[16,8,8,128]{3,2,1,0:T(8,128)(2,1)S(1)} %get-tuple-element.127), channel_id=1, replica_groups=mesh['firm_far'=8,'firm_middle'=1,'firm_near'=2,'worker'=8,'probe'=4] {'..., dimensions={0} | all-to-all | bytes 524288 | tf_op jit(solution)/shard_map/all_to_all | solution.py:374
  66.2 0.0 copy-done.3
  66.2 0.0 copy-done.2
  66.2 0.0 copy-done
  66.2 0.0 copy-done.1
  66.2 2.9 %middle.1 = f32[16,9,8,128]{3,2,1,0:T(8,128)S(1)} custom-call(s32[1,128]{1,0:T(1,128)S(1)} %copy-done.2, s32[1,128]{1,0:T(1,128)S(1)} %copy-done.3, s32[1]{0:T(128)} %bitcast.3.worker, s32[1]{0:T(128)} %bitcast.2.firm, bf16[128,8,128]{2,1,0:T(8,128)(2,1)S(1)} %bitcast.8, f32[8,8,128]{2,1,0:T(8,128)S(1)} %get-tuple-element.155.firsts, f32[8,128]{1,0:T(8,128)S(1)} %bitcast.11, ...), custom_call_target="tpu_custom_call" | custom-call | flops 67108864 | bytes 1048576 | tf_op jit(solution)/shard_map/middle/pallas_call | solution.py:420
  69.1 14.6 %all_to_all.53.got = f32[16,9,8,128]{3,2,1,0:T(8,128)S(1)} all-to-all(f32[16,9,8,128]{3,2,1,0:T(8,128)S(1)} %middle.1), channel_id=1, replica_groups=mesh['firm_far'=8,'firm_middle'=1,'firm_near'=2,'worker'=8,'probe'=4] {'..., dimensions={0} | all-to-all | bytes 1179648 | tf_op jit(solution)/shard_map/all_to_all | solution.py:374
  83.8 16.2 %all_to_all.54.got = bf16[8,9,8,128]{3,2,1,0:T(8,128)(2,1)S(1)} all-to-all(bf16[8,9,8,128]{3,2,1,0:T(8,128)(2,1)S(1)} %fold.3), channel_id=1, replica_groups=mesh['firm_far'=8,'firm_middle'=1,'firm_near'=2,'worker'=8,'probe'=4] {'..., dimensions={0} | all-to-all | bytes 294912 | tf_op jit(solution)/shard_map/all_to_all | solution.py:374
  100.0 0.2 second.1
  100.1 13.7 %all_to_all.55 = bf16[16,8,8,128]{3,2,1,0:T(8,128)(2,1)S(1)} all-to-all(bf16[16,8,8,128]{3,2,1,0:T(8,128)(2,1)S(1)} %get-tuple-element.162), channel_id=1, replica_groups=mesh['firm_far'=8,'firm_middle'=1,'firm_near'=2,'worker'=8,'probe'=4] {'..., dimensions={0} | all-to-all | bytes 524288 | tf_op jit(solution)/shard_map/all_to_all | solution.py:374
  113.9 2.0 %rows.1 = f32[4,7,8,128]{3,2,1,0:T(8,128)S(1)} custom-call(s32[1,128]{1,0:T(1,128)S(1)} %copy-done.2, s32[1,128]{1,0:T(1,128)S(1)} %copy-done.3, bf16[128,8,128]{2,1,0:T(8,128)(2,1)S(1)} %bitcast.9, f32[8,128]{1,0:T(8,128)S(1)} %get-tuple-element.204.first, f32[8,128]{1,0:T(8,128)S(1)} %get-tuple-element.205.second, ...), custom_call_target="tpu_custom_call" | custom-call | flops 33554432 | bytes 1048576 | tf_op jit(solution)/shard_map/rows/pallas_call | solution.py:436
  115.9 8.6 %all_to_all.56.given = f32[4,7,8,128]{3,2,1,0:T(8,128)S(1)} all-to-all(f32[4,7,8,128]{3,2,1,0:T(8,128)S(1)} %rows.1), channel_id=1, replica_groups=mesh['firm_far'=8,'firm_middle'=1,'firm_near'=2,'worker'=8,'probe'=4] {'..., dimensions={0} | all-to-all | bytes 229376 | tf_op jit(solution)/shard_map/all_to_all | solution.py:374
  124.5 1.6 last.1
  126.1 12.8 %all_to_all.57.got = bf16[16,11,8,128]{3,2,1,0:T(8,128)(2,1)S(1)} all-to-all(bf16[16,11,8,128]{3,2,1,0:T(8,128)(2,1)S(1)} %last.1), channel_id=1, replica_groups=mesh['firm_far'=8,'firm_middle'=1,'firm_near'=2,'worker'=8,'probe'=4] {'..., dimensions={0} | all-to-all | bytes 720896 | tf_op jit(solution)/shard_map/all_to_all | solution.py:374
  138.9 0.1 fold_last.1
  138.9 15.1 %all_to_all.58.got = f32[8,16,128]{2,1,0:T(8,128)S(1)} all-to-all(f32[8,16,128]{2,1,0:T(8,128)S(1)} %fold_last.1), channel_id=1, replica_groups=mesh['firm_far'=8,'firm_middle'=1,'firm_near'=2,'worker'=8,'probe'=4] {'..., dimensions={0} | all-to-all | bytes 131072 | tf_op jit(solution)/shard_map/all_to_all | solution.py:374
  154.1 16.5 %all_to_all.59.last = f32[32,4,8,128]{3,2,1,0:T(8,128)S(1)} all-to-all(f32[32,4,8,128]{3,2,1,0:T(8,128)S(1)} %third.1), channel_id=1, replica_groups=mesh['firm_far'=8,'firm_middle'=1,'firm_near'=2,'worker'=8,'probe'=4] {'..., dimensions={0} | all-to-all | bytes 1048576 | tf_op jit(solution)/shard_map/all_to_all | solution.py:374
  170.6 4.0 %final.1 = (f32[8,1024]{1,0:T(8,128)}, f32[8,1024]{1,0:T(8,128)}) custom-call(s32[1]{0:T(128)} %bitcast.4.probe, f32[4,7,8,128]{3,2,1,0:T(8,128)S(1)} %all_to_all.56.given, f32[32,4,8,128]{3,2,1,0:T(8,128)S(1)} %all_to_all.59.last), custom_call_target="tpu_custom_call" | custom-call | flops 8388608 | bytes 1048576 | tf_op jit(solution)/shard_map/final/pallas_call | solution.py:458
  (4 shorter events, 0.1 us)
Async XLA Ops:
  0.6 65.6 %copy-start.3 = (s32[1,128]{1,0:T(1,128)S(1)}, s32[1,128]{1,0:T(1,128)}, u32[]{:S(2)}) copy-start(s32[1,128]{1,0:T(1,128)} %tile_firms.5) | copy-start | bytes 1540
  0.6 65.5 %copy-start.2 = (s32[1,128]{1,0:T(1,128)S(1)}, s32[1,128]{1,0:T(1,128)}, u32[]{:S(2)}) copy-start(s32[1,128]{1,0:T(1,128)} %tile_rows.5) | copy-start | bytes 1540
  0.7 65.5 %copy-start = (s32[1,512]{1,0:T(1,128)S(1)}, s32[1,512]{1,0:T(1,128)}, u32[]{:S(2)}) copy-start(s32[1,512]{1,0:T(1,128)} %worker_ids.3) | copy-start | bytes 6148
  0.7 65.5 %copy-start.1 = (f32[1024]{0:T(1024)S(1)}, f32[1024]{0:T(1024)}, u32[]{:S(2)}) copy-start(f32[1024]{0:T(1024)} %param.11) | copy-start | bytes 12292

commit v13 on v10

--- a/solution.py
+++ b/solution.py
@@ -10,7 +10,7 @@
 ROWS_DEV = 512
 SHARD_WORKERS = 128
 BITS = 30
-CHUNKS = 4
+CHUNKS = 8
 PANEL = 16
 WORKERS = 8
 FIRMS = 16

time: 175 us -> 176 us (level)
  no operation moved by 1% of the time
where the time goes in v13:
time: 176 us; the launch traced here: 175 us
  blocking collectives  160 us (91%)
  Pallas kernels  14 us (8%)
    all_to_all x10, blocking collectives, exchange(): got = lax.all_to_all(chunks, axis, 0, 0, tiled=True)  160 us
    pallas_call x1, Pallas kernels, local(): kernel(final_body, (out, out), [SMEM, VMEM, VMEM], [VMEM((3 * total, WORK...  4 us

profile of v13, /device:TPU:1, one launch (start us, length us, event | category | flops | bytes accessed | tf_op | source)
XLA Modules:
  0.0 175.2 jit_solution(3586814562554297187)
XLA Ops:
  0.6 0.0 copy-start.3
  0.6 0.0 copy-start.2
  0.7 0.0 copy-start
  0.7 0.0 copy-start.1
  0.7 3.1 %start.1 = (f32[128,8,128]{2,1,0:T(8,128)S(1)}, bf16[128,128,128]{2,1,0:T(8,128)(2,1)S(1)}) custom-call(s32[1,128]{1,0:T(1,128)} %tile_rows.5, s32[1,128]{1,0:T(1,128)} %tile_firms.5, s32[5,4,8]{2,1,0:T(4,128)} %bitcast.13, s32[1,512]{1,0:T(1,128)} %worker_ids.3, bf16[128,128,128]{2,1,0:T(8,128)(2,1)} %tiles_hbm.1), custom_call_target="tpu_custom_call" | custom-call | flops 33554432 | bytes 1048576 | tf_op jit(solution)/shard_map/start/pallas_call | solution.py:403
  3.8 19.0 %all_to_all.50.got = f32[16,8,8,128]{3,2,1,0:T(8,128)S(1)} all-to-all(f32[16,8,8,128]{3,2,1,0:T(8,128)S(1)} %bitcast.10), channel_id=1, replica_groups=mesh['firm_far'=8,'firm_middle'=1,'firm_near'=2,'worker'=8,'probe'=4] {'..., dimensions={0} | all-to-all | bytes 1048576 | tf_op jit(solution)/shard_map/all_to_all | solution.py:374
  22.8 28.5 %all_to_all.51.got = f32[8,8,8,128]{3,2,1,0:T(8,128)S(1)} all-to-all(f32[8,8,8,128]{3,2,1,0:T(8,128)S(1)} %fold.2), channel_id=1, replica_groups=mesh['firm_far'=8,'firm_middle'=1,'firm_near'=2,'worker'=8,'probe'=4] {'..., dimensions={0} | all-to-all | bytes 524288 | tf_op jit(solution)/shard_map/all_to_all | solution.py:374
  51.4 15.3 %all_to_all.52 = bf16[16,8,8,128]{3,2,1,0:T(8,128)(2,1)S(1)} all-to-all(bf16[16,8,8,128]{3,2,1,0:T(8,128)(2,1)S(1)} %get-tuple-element.127), channel_id=1, replica_groups=mesh['firm_far'=8,'firm_middle'=1,'firm_near'=2,'worker'=8,'probe'=4] {'..., dimensions={0} | all-to-all | bytes 524288 | tf_op jit(solution)/shard_map/all_to_all | solution.py:374
  66.7 0.0 copy-done.3
  66.7 0.0 copy-done.2
  66.7 0.0 copy-done
  66.7 0.0 copy-done.1
  66.7 2.9 %middle.1 = f32[16,9,8,128]{3,2,1,0:T(8,128)S(1)} custom-call(s32[1,128]{1,0:T(1,128)S(1)} %copy-done.2, s32[1,128]{1,0:T(1,128)S(1)} %copy-done.3, s32[1]{0:T(128)} %bitcast.3.worker, s32[1]{0:T(128)} %bitcast.2.firm, bf16[128,8,128]{2,1,0:T(8,128)(2,1)S(1)} %bitcast.8, f32[8,8,128]{2,1,0:T(8,128)S(1)} %get-tuple-element.155.firsts, f32[8,128]{1,0:T(8,128)S(1)} %bitcast.11, ...), custom_call_target="tpu_custom_call" | custom-call | flops 67108864 | bytes 1048576 | tf_op jit(solution)/shard_map/middle/pallas_call | solution.py:420
  69.6 14.6 %all_to_all.53.got = f32[16,9,8,128]{3,2,1,0:T(8,128)S(1)} all-to-all(f32[16,9,8,128]{3,2,1,0:T(8,128)S(1)} %middle.1), channel_id=1, replica_groups=mesh['firm_far'=8,'firm_middle'=1,'firm_near'=2,'worker'=8,'probe'=4] {'..., dimensions={0} | all-to-all | bytes 1179648 | tf_op jit(solution)/shard_map/all_to_all | solution.py:374
  84.3 16.2 %all_to_all.54.got = bf16[8,9,8,128]{3,2,1,0:T(8,128)(2,1)S(1)} all-to-all(bf16[8,9,8,128]{3,2,1,0:T(8,128)(2,1)S(1)} %fold.3), channel_id=1, replica_groups=mesh['firm_far'=8,'firm_middle'=1,'firm_near'=2,'worker'=8,'probe'=4] {'..., dimensions={0} | all-to-all | bytes 294912 | tf_op jit(solution)/shard_map/all_to_all | solution.py:374
  100.5 0.2 second.1
  100.7 13.7 %all_to_all.55 = bf16[16,8,8,128]{3,2,1,0:T(8,128)(2,1)S(1)} all-to-all(bf16[16,8,8,128]{3,2,1,0:T(8,128)(2,1)S(1)} %get-tuple-element.162), channel_id=1, replica_groups=mesh['firm_far'=8,'firm_middle'=1,'firm_near'=2,'worker'=8,'probe'=4] {'..., dimensions={0} | all-to-all | bytes 524288 | tf_op jit(solution)/shard_map/all_to_all | solution.py:374
  114.4 2.0 %rows.1 = f32[4,7,8,128]{3,2,1,0:T(8,128)S(1)} custom-call(s32[1,128]{1,0:T(1,128)S(1)} %copy-done.2, s32[1,128]{1,0:T(1,128)S(1)} %copy-done.3, bf16[128,8,128]{2,1,0:T(8,128)(2,1)S(1)} %bitcast.9, f32[8,128]{1,0:T(8,128)S(1)} %get-tuple-element.204.first, f32[8,128]{1,0:T(8,128)S(1)} %get-tuple-element.205.second, ...), custom_call_target="tpu_custom_call" | custom-call | flops 33554432 | bytes 1048576 | tf_op jit(solution)/shard_map/rows/pallas_call | solution.py:436
  116.5 8.6 %all_to_all.56.given = f32[4,7,8,128]{3,2,1,0:T(8,128)S(1)} all-to-all(f32[4,7,8,128]{3,2,1,0:T(8,128)S(1)} %rows.1), channel_id=1, replica_groups=mesh['firm_far'=8,'firm_middle'=1,'firm_near'=2,'worker'=8,'probe'=4] {'..., dimensions={0} | all-to-all | bytes 229376 | tf_op jit(solution)/shard_map/all_to_all | solution.py:374
  125.0 1.6 last.1
  126.6 12.1 %all_to_all.57.got = bf16[8,19,8,128]{3,2,1,0:T(8,128)(2,1)S(1)} all-to-all(bf16[8,19,8,128]{3,2,1,0:T(8,128)(2,1)S(1)} %last.1), channel_id=1, replica_groups=mesh['firm_far'=8,'firm_middle'=1,'firm_near'=2,'worker'=8,'probe'=4] {'..., dimensions={0} | all-to-all | bytes 622592 | tf_op jit(solution)/shard_map/all_to_all | solution.py:374
  138.8 14.6 %all_to_all.58.got = f32[16,16,128]{2,1,0:T(8,128)S(1)} all-to-all(f32[16,16,128]{2,1,0:T(8,128)S(1)} %fold_last.1), channel_id=1, replica_groups=mesh['firm_far'=8,'firm_middle'=1,'firm_near'=2,'worker'=8,'probe'=4] {'..., dimensions={0} | all-to-all | bytes 262144 | tf_op jit(solution)/shard_map/all_to_all | solution.py:374
  153.4 0.1 third.1
  153.4 17.7 %all_to_all.59.last = f32[32,4,8,128]{3,2,1,0:T(8,128)S(1)} all-to-all(f32[32,4,8,128]{3,2,1,0:T(8,128)S(1)} %third.1), channel_id=1, replica_groups=mesh['firm_far'=8,'firm_middle'=1,'firm_near'=2,'worker'=8,'probe'=4] {'..., dimensions={0} | all-to-all | bytes 1048576 | tf_op jit(solution)/shard_map/all_to_all | solution.py:374
  171.2 4.0 %final.1 = (f32[8,1024]{1,0:T(8,128)}, f32[8,1024]{1,0:T(8,128)}) custom-call(s32[1]{0:T(128)} %bitcast.4.probe, f32[4,7,8,128]{3,2,1,0:T(8,128)S(1)} %all_to_all.56.given, f32[32,4,8,128]{3,2,1,0:T(8,128)S(1)} %all_to_all.59.last), custom_call_target="tpu_custom_call" | custom-call | flops 8388608 | bytes 1048576 | tf_op jit(solution)/shard_map/final/pallas_call | solution.py:458
  (4 shorter events, 0.2 us)
Async XLA Ops:
  0.6 66.1 %copy-start.3 = (s32[1,128]{1,0:T(1,128)S(1)}, s32[1,128]{1,0:T(1,128)}, u32[]{:S(2)}) copy-start(s32[1,128]{1,0:T(1,128)} %tile_firms.5) | copy-start | bytes 1540
  0.6 66.1 %copy-start.2 = (s32[1,128]{1,0:T(1,128)S(1)}, s32[1,128]{1,0:T(1,128)}, u32[]{:S(2)}) copy-start(s32[1,128]{1,0:T(1,128)} %tile_rows.5) | copy-start | bytes 1540
  0.7 66.1 %copy-start = (s32[1,512]{1,0:T(1,128)S(1)}, s32[1,512]{1,0:T(1,128)}, u32[]{:S(2)}) copy-start(s32[1,512]{1,0:T(1,128)} %worker_ids.3) | copy-start | bytes 6148
  0.7 66.1 %copy-start.1 = (f32[1024]{0:T(1024)S(1)}, f32[1024]{0:T(1024)}, u32[]{:S(2)}) copy-start(f32[1024]{0:T(1024)} %param.11) | copy-start | bytes 12292
